TPU v7x, 128 devices: a whole 4x4x4 slice. The times are simulated.
128 devices in a mesh: wide: 32 (over x_hi, y, z), narrow: 4 (over x_lo, core).
Axes of the slice: x: 4 (x_hi: 2, x_lo: 2; x = x_hi * 2 + x_lo), y: 4, z: 4, core: 2. Of those that a mesh axis runs over, the one named last changes fastest.
Arguments:
- displacement: float32 [3, 16, 2048, 1024], P(None, None, 'wide', 'narrow'), may hold values from -6 to 6
- velocity: float32 [3, 16, 2048, 1024], P(None, None, 'wide', 'narrow'), may hold values from -6 to 6
- region: int32 [16, 2048, 1024], P(None, 'wide', 'narrow'), may hold values from 0 to 3
- flags: int32 [256, 128], P('wide', 'narrow'), may hold values 0 or 1
- shear: float32 [4], replicated, may hold values from 0.5 to 2
- yields: float32 [4], replicated, may hold values from 2 to 16
- history: bfloat16 [32, 2, 3, 1024, 2048], P(None, None, None, ('wide', 'narrow')), may hold values from -6 to 6
- kernel: bfloat16 [33, 3, 1024, 2048], P(None, None, ('wide', 'narrow')), may hold values from -6 to 6
Outputs:
- displacement_out: float32 [3, 16, 2048, 1024], P(None, None, 'wide', 'narrow')
- velocity_out: float32 [3, 16, 2048, 1024], P(None, None, 'wide', 'narrow')
Inputs may be any that keep to these rules, and one draw needn't show every extreme that they name: `flags`: 1 marks a block of 8 x 8 cells along strike and dip, through the whole depth, as yielding.
All inputs are finite; a program needn't handle non-finite values.
Results may differ from a plain program's by a relative error of at most 0.0003.
Values sent between devices are 32-bit elements; how exact they have to be, the bound alone decides.
No kernel may reach another device: no remote copies, remote signals or barrier semaphores. Data moves between devices by JAX's collectives and lax.ppermute only.
A program may use at most 256 MiB of HBM per device.

v0:
```python
import math

import jax
import jax.numpy as jnp
from jax import lax
from jax.sharding import PartitionSpec as P

STEPS = 2


TIME_STEP = 0.1
DAMPING = 0.5
HIGHEST = lax.Precision.HIGHEST


def extended(cells, sides, width):
    for axis, dim in sides:
        count = lax.axis_size(axis)
        ends = count - 1
        head = lax.slice_in_dim(cells, 0, width, axis=dim)
        tail = lax.slice_in_dim(cells, cells.shape[dim] - width, cells.shape[dim], axis=dim)
        cells = jnp.concatenate(
            [
                lax.ppermute(tail, axis, [(i, (i + 1) % count) for i in range(ends)]),
                cells,
                lax.ppermute(head, axis, [((i + 1) % count, i) for i in range(ends)]),
            ],
            axis=dim,
        )
    return cells


def angle_table(places, length):
    columns = lax.iota(jnp.int32, length)
    product = places[:, None] * columns[None, :] % length
    angles = product.astype(jnp.float32) * (2.0 * math.pi / length)
    return jnp.concatenate([jnp.cos(angles), jnp.sin(angles)], axis=1)


def yielded_force(displacement, region, flags, shear, yields):
    padded = extended(displacement, (("wide", 2), ("narrow", 3)), 1)
    padded = jnp.pad(padded, ((0, 0), (1, 1), (0, 0), (0, 0)))
    center = padded[:, 1:-1, 1:-1, 1:-1]
    beside_all = padded[:, 2:, 1:-1, 1:-1] + padded[:, :-2, 1:-1, 1:-1]
    beside_all = beside_all + padded[:, 1:-1, 2:, 1:-1] + padded[:, 1:-1, :-2, 1:-1]
    beside_all = beside_all + padded[:, 1:-1, 1:-1, 2:] + padded[:, 1:-1, 1:-1, :-2]
    labels = lax.iota(jnp.int32, shear.shape[0])[:, None, None, None]
    matches = region[None] == labels
    modulus = jnp.sum(jnp.where(matches, shear[:, None, None, None], 0.0), axis=0)
    ceiling = jnp.sum(jnp.where(matches, yields[:, None, None, None], 0.0), axis=0)
    force = modulus[None] * (beside_all - 6.0 * center)
    squares = jnp.sum(force * force, axis=0)
    capped = lax.rsqrt(1.0 + squares / (ceiling * ceiling))
    strike_cells = displacement.shape[2]
    dip_cells = displacement.shape[3]
    strike_blocks = flags.shape[0]
    dip_blocks = flags.shape[1]
    widened = jnp.broadcast_to(
        flags[:, None, :, None],
        (strike_blocks, strike_cells // strike_blocks, dip_blocks, dip_cells // dip_blocks),
    )
    plastic = widened.reshape(strike_cells, dip_cells)
    scaling = jnp.where(plastic[None] == 1, capped, 1.0)
    return force * scaling[None]


def forward(slip, dip_table, strike_table, factor):
    gathered = lax.all_to_all(slip, "narrow", split_axis=1, concat_axis=2, tiled=True)
    dip_len = gathered.shape[2]
    spectra = jnp.einsum("cxy,yq->cxq", gathered, dip_table, precision=HIGHEST)
    stacked = jnp.stack([spectra[..., :dip_len], -spectra[..., dip_len:]])
    owned = lax.all_to_all(stacked, ("wide", "narrow"), split_axis=3, concat_axis=2, tiled=True)
    strike_len = owned.shape[2]
    mixed = jnp.einsum("rcpk,pq->rckq", owned, strike_table, precision=HIGHEST)
    real_part = mixed[0, ..., :strike_len] + mixed[1, ..., strike_len:]
    imag_part = mixed[1, ..., :strike_len] - mixed[0, ..., strike_len:]
    return jnp.stack([real_part, imag_part]) * factor


def inverse(spectrum, dip_table, strike_table, factor):
    real_part = spectrum[0]
    imag_part = spectrum[1]
    paired = jnp.stack(
        [
            jnp.concatenate([real_part, -imag_part], axis=-1),
            jnp.concatenate([imag_part, real_part], axis=-1),
        ]
    )
    strike_lines = jnp.einsum("rckq,pq->rckp", paired, strike_table, precision=HIGHEST) * factor
    columns = lax.all_to_all(
        strike_lines, ("wide", "narrow"), split_axis=3, concat_axis=2, tiled=True
    )
    folded = jnp.concatenate([columns[0], -columns[1]], axis=1)
    values = jnp.einsum("cqx,yq->cxy", folded, dip_table, precision=HIGHEST)
    return lax.all_to_all(values, "narrow", split_axis=2, concat_axis=1, tiled=True)


def body(displacement, velocity, region, flags, shear, yields, history, kernel):
    wide_count = lax.axis_size("wide")
    narrow_count = lax.axis_size("narrow")
    strike_len = history.shape[4]
    dip_len = history.shape[3] * wide_count * narrow_count
    positions = lax.iota(jnp.int32, strike_len)
    strike_table = angle_table(positions, strike_len)
    dip_table = angle_table(lax.iota(jnp.int32, dip_len), dip_len)
    factor = 1.0 / math.sqrt(strike_len * dip_len)
    stored = history.shape[0]
    earlier = []
    for number in range(STEPS):
        spectrum = forward(displacement[:, 0], dip_table, strike_table, factor)
        total = kernel[0].astype(jnp.float32)[None] * spectrum
        for offset, former in enumerate(earlier):
            total = total + kernel[offset + 1].astype(jnp.float32)[None] * former
        depth_kept = stored - len(earlier)
        weights = kernel[len(earlier) + 1 :].astype(jnp.float32)[:, None]
        total = total + jnp.sum(weights * history[:depth_kept].astype(jnp.float32), axis=0)
        earlier = [spectrum] + earlier
        traction = inverse(total, dip_table, strike_table, factor) - DAMPING * velocity[:, 0]
        force = yielded_force(displacement, region, flags, shear, yields)
        force = force.at[:, 0].add(traction)
        velocity = velocity + TIME_STEP * force
        displacement = displacement + TIME_STEP * velocity
    return (displacement, velocity)


def solution(mesh):
    in_specs = (
        P(None, None, "wide", "narrow"),
        P(None, None, "wide", "narrow"),
        P(None, "wide", "narrow"),
        P("wide", "narrow"),
        P(),
        P(),
        P(None, None, None, ("wide", "narrow"), None),
        P(None, None, ("wide", "narrow"), None),
    )
    out_specs = (P(None, None, "wide", "narrow"), P(None, None, "wide", "narrow"))
    return jax.shard_map(body, mesh=mesh, in_specs=in_specs, out_specs=out_specs, check_vma=False)
```

profile of v0, /device:TPU:1, one launch (start us, length us, event | category | flops | bytes accessed | tf_op | source)
XLA Modules:
  0.0 618.7 jit_solution(7066269835331108504)
XLA Ops:
  1.8 4.4 collective-permute-start
  9.3 5.0 all-to-all-start
  15.9 5.3 slice_convert_fusion.1
  22.1 17.5 %fusion.38 = (f32[1024,1024]{1,0:T(8,128)}, f32[1024,1024]{1,0:T(8,128)}) fusion(), kind=kLoop, calls=%fused_computation.91 | loop fusion | flops 14680064 | bytes 8388608 | tf_op jit(solution)/shard_map/sin | solution.py:37
  39.6 66.8 %fusion.10 = (f32[2048,2048]{1,0:T(8,128)}, f32[2048,2048]{1,0:T(8,128)}) fusion(), kind=kLoop, calls=%fused_computation.19 | loop fusion | flops 58720256 | bytes 33554432 | tf_op jit(solution)/shard_map/sin | solution.py:37
  106.4 5.6 multiply_reduce_fusion
  121.3 3.6 collective-permute-start.2
  137.9 7.7 %fusion.35 = f32[3,16,2048]{2,1,0:T(8,128)S(1)} fusion(f32[3,16,1024]{2,1,0:T(8,128)S(1)} %all_to_all.103, f32[1024,1024]{1,0:T(8,128)} %get-tuple-element.78, f32[1024,1024]{1,0:T(8,128)} %get-tuple-element.79), kind=kOutput, calls=%fused_computation.88 | convolution fusion | flops 1210056704 | bytes 8978432 | tf_op jit(solution)/shard_map/cxy,yq->cxq/dot_general | solution.py:70
  146.5 4.9 copy.289
  151.3 6.5 %reshape.123 = f32[128,1,768]{2,1,0:T(1,128)} reshape(f32[1024,3,2,16]{3,2,1,0:T(2,128)} %bitcast.127) | data formatting | bytes 786432
  157.9 12.4 %all-to-all-start.1 = ((f32[128,1,768]{2,1,0:T(1,128)}), f32[128,1,768]{2,1,0:T(1,128)}, u32[]{:S(2)}, u32[]{:S(2)}) async-start(f32[128,1,768]{2,1,0:T(1,128)} %reshape.123), calls=%async_computation.1 | async-start | bytes 786432 | tf_op jit(solution)/shard_map/all_to_all | solution.py:72
  170.3 7.5 %select_maximum_fusion.4 = f32[3,18,66,258]{3,2,0,1:T(8,128)} fusion(f32[3,16,66,1]{3,2,0,1:T(8,128)} %copy.281, f32[3,16,66,1]{3,2,0,1:T(8,128)} %copy.280, f32[3,16,1,256]{3,2,0,1:T(1,128)S(1)} %copy-done.20, f32[3,16,1,256]{3,2,0,1:T(1,128)S(1)} %copy-done.18, f32[3,16,64,256]{3,2,1,0:T(8,128)S(1)} %copy-done), kind=kLoop, calls=%fused_computation.28 | loop fusion | flops 11034144 | bytes 6947424 | tf_op jit(solution)/shard_map/concatenate | solution.py:22
  177.7 4.1 all-to-all-done.1
  182.4 3.2 reduce.4
  185.6 5.4 reshape.124
  191.7 3.3 all_to_all.107
  195.0 24.2 %fusion.9 = f32[2,3,8,4096]{3,2,1,0:T(8,128)S(1)} fusion(f32[2,3,2048,8]{2,3,1,0:T(8,128)} %all_to_all.107, f32[2048,2048]{1,0:T(8,128)} %get-tuple-element.80, f32[2048,2048]{1,0:T(8,128)} %get-tuple-element.81), kind=kOutput, calls=%fused_computation.13 | convolution fusion | flops 4840226816 | bytes 34734080 | tf_op jit(solution)/shard_map/rcpk,pq->rckq/dot_general | solution.py:74
  220.1 34.6 %fusion.36 = f32[2,3,8,2048]{3,2,1,0:T(8,128)S(1)} fusion(f32[2048,2048]{1,0:T(8,128)S(1)} %bitcast.122, f32[2048,2048]{1,0:T(8,128)} %get-tuple-element.81, f32[1,3,8,4096]{3,2,1,0:T(8,128)S(1)} %get-tuple-element.77, f32[1,3,8,4096]{3,2,1,0:T(8,128)S(1)} %get-tuple-element.76), kind=kOutput, calls=%fused_computation.89 | convolution fusion | flops 4840521728 | bytes 34734080 | tf_op jit(solution)/shard_map/rckq,pq->rckp/dot_general | solution.py:89
  254.8 6.6 %copy.292 = f32[2,3,8,2048]{2,0,1,3:T(2,128)} copy(f32[2,3,8,2048]{3,2,1,0:T(8,128)S(1)} %fusion.36) | data formatting | bytes 786432 | tf_op jit(solution)/shard_map/mul | solution.py:89
  261.4 11.4 %reshape.125 = f32[128,1,768]{2,1,0:T(1,128)} reshape(f32[2048,3,2,8]{3,2,1,0:T(2,128)} %bitcast.123) | data formatting | bytes 786432
  272.8 6.0 all-to-all-start.2
  278.8 14.2 %multiply_reduce_fusion.3 = (f32[16,64,256]{2,1,0:T(8,128)S(1)}, f32[3,16,64,256]{3,2,0,1:T(8,128)}) fusion(f32[3,16,64,256]{3,2,0,1:T(8,128)} %copy.304, f32[3,16,1,256]{3,2,0,1:T(1,128)} %copy-done.19, f32[3,16,1,256]{3,2,0,1:T(1,128)} %copy-done.17, f32[3,16,66,1]{3,2,0,1:T(8,128)S(1)} %copy-done.2, f32[3,16,66,1]{3,2,0,1:T(8,128)S(1)} %copy-done.1, ...), kind=kLoop, calls=%fused_computation.86 | loop fusion | flops 13893632 | bytes 14803712 | tf_op jit(solution)/shard_map/reduce_sum | solution.py:52
  294.3 2.5 reduce.5
  296.8 11.2 %reshape.126 = f32[2048,3,2,8]{3,2,1,0:T(2,128)} reshape(f32[128,768]{1,0:T(8,128)S(1)} %reduce.5) | data formatting | bytes 786432
  308.0 5.4 copy.294
  315.4 10.2 %fusion.21 = f32[3,16,1024]{2,1,0:T(8,128)S(1)} fusion(f32[1024,1024]{1,0:T(8,128)} %get-tuple-element.78, f32[1024,1024]{1,0:T(8,128)} %get-tuple-element.79, f32[3,1024,16]{1,2,0:T(8,128)S(1)} %copy.298, f32[3,1024,16]{1,2,0:T(8,128)S(1)} %copy.297), kind=kOutput, calls=%fused_computation.44 | convolution fusion | flops 1210155008 | bytes 8978432 | tf_op jit(solution)/shard_map/cqx,yq->cxy/dot_general | solution.py:94
  327.4 3.3 reshape.127
  330.7 4.5 all-to-all-start.3
  335.1 3.2 broadcast_multiply_fusion.1
  344.1 6.8 %multiply_add_fusion.2 = (f32[3,16,64,256]{3,2,0,1:T(8,128)S(1)}, f32[3,16,64,256]{3,2,0,1:T(8,128)}) fusion(f32[3,16,64,256]{3,2,1,0:T(8,128)} %param.12, f32[3,16,64,256]{3,2,0,1:T(8,128)} %fusion.60, f32[3,16,64,256]{3,2,1,0:T(8,128)} %param.13), kind=kLoop, calls=%fused_computation.83 | loop fusion | flops 3145728 | bytes 15728640 | tf_op jit(solution)/shard_map/add | solution.py:122
  350.9 2.6 collective-permute-start.4
  355.7 5.5 all-to-all-start.4
  364.0 2.7 copy.306
  366.8 2.7 copy.305
  369.5 3.5 collective-permute-start.6
  374.9 6.2 %multiply_reduce_fusion.1 = f32[2,3,8,2048]{3,2,1,0:T(8,128)S(1)} fusion(bf16[32,2,3,8,2048]{4,3,2,1,0:T(8,128)(2,1)} %param.18, f32[31,3,8,2048]{3,2,1,0:T(8,128)} %slice_convert_fusion.1), kind=kLoop, calls=%fused_computation.15 | loop fusion | flops 9043968 | bytes 12582912 | tf_op jit(solution)/shard_map/reduce_sum | solution.py:116
  381.1 2.6 copy.308
  383.7 2.6 copy.307
  389.8 8.6 %fusion.20 = f32[3,16,2048]{2,1,0:T(8,128)S(1)} fusion(f32[3,16,1024]{2,1,0:T(8,128)} %all_to_all.118, f32[1024,1024]{1,0:T(8,128)} %get-tuple-element.78, f32[1024,1024]{1,0:T(8,128)} %get-tuple-element.79), kind=kOutput, calls=%fused_computation.43 | convolution fusion | flops 1210056704 | bytes 8978432 | tf_op jit(solution)/shard_map/cxy,yq->cxq/dot_general | solution.py:70
  399.3 4.9 copy.313
  404.2 6.6 %reshape.129 = f32[128,1,768]{2,1,0:T(1,128)} reshape(f32[1024,3,2,16]{3,2,1,0:T(2,128)} %bitcast.130) | data formatting | bytes 786432
  410.7 12.9 %all-to-all-start.5 = ((f32[128,1,768]{2,1,0:T(1,128)}), f32[128,1,768]{2,1,0:T(1,128)}, u32[]{:S(2)}, u32[]{:S(2)}) async-start(f32[128,1,768]{2,1,0:T(1,128)} %reshape.129), calls=%async_computation.5 | async-start | bytes 786432 | tf_op jit(solution)/shard_map/all_to_all | solution.py:72
  423.6 7.5 %select_maximum_fusion = f32[3,18,66,258]{3,2,0,1:T(8,128)} fusion(f32[3,16,66,1]{3,2,0,1:T(8,128)} %copy.308, f32[3,16,66,1]{3,2,0,1:T(8,128)} %copy.307, f32[3,16,1,256]{3,2,0,1:T(1,128)} %copy-done.23, f32[3,16,64,256]{3,2,0,1:T(8,128)S(1)} %get-tuple-element.44, f32[3,16,1,256]{3,2,0,1:T(1,128)} %copy-done.21), kind=kLoop, calls=%fused_computation.24 | loop fusion | flops 11034144 | bytes 6947424 | tf_op jit(solution)/shard_map/concatenate | solution.py:22
  431.1 4.1 all-to-all-done.5
  435.2 3.2 reduce.7
  438.4 6.4 %reshape.130 = f32[1024,3,2,16]{3,2,1,0:T(2,128)} reshape(f32[128,768]{1,0:T(8,128)} %reduce.7) | data formatting | bytes 786432
  449.1 4.4 all_to_all.122
  453.6 24.4 %fusion.7 = f32[2,3,8,4096]{3,2,1,0:T(8,128)S(1)} fusion(f32[2,3,2048,8]{2,3,1,0:T(8,128)} %all_to_all.122, f32[2048,2048]{1,0:T(8,128)} %get-tuple-element.80, f32[2048,2048]{1,0:T(8,128)} %get-tuple-element.81), kind=kOutput, calls=%fused_computation.11 | convolution fusion | flops 4840226816 | bytes 34734080 | tf_op jit(solution)/shard_map/rcpk,pq->rckq/dot_general | solution.py:74
  478.3 34.9 %fusion.37 = f32[2,3,8,2048]{3,2,1,0:T(8,128)S(1)} fusion(f32[2048,2048]{1,0:T(8,128)} %get-tuple-element.80, f32[2048,2048]{1,0:T(8,128)} %get-tuple-element.81, f32[1,3,8,4096]{3,2,1,0:T(8,128)S(1)} %get-tuple-element.75, f32[1,3,8,4096]{3,2,1,0:T(8,128)S(1)} %get-tuple-element.74), kind=kOutput, calls=%fused_computation.90 | convolution fusion | flops 4840521728 | bytes 34734080 | tf_op jit(solution)/shard_map/rckq,pq->rckp/dot_general | solution.py:89
  513.2 6.6 %copy.316 = f32[2,3,8,2048]{2,0,1,3:T(2,128)} copy(f32[2,3,8,2048]{3,2,1,0:T(8,128)S(1)} %fusion.37) | data formatting | bytes 786432 | tf_op jit(solution)/shard_map/mul | solution.py:89
  519.8 11.0 %reshape.131 = f32[128,1,768]{2,1,0:T(1,128)} reshape(f32[2048,3,2,8]{3,2,1,0:T(2,128)} %bitcast.125) | data formatting | bytes 786432
  530.8 6.1 all-to-all-start.6
  536.9 10.1 %multiply_reduce_fusion.2 = (f32[16,64,256]{2,1,0:T(8,128)S(1)}, f32[3,16,64,256]{3,2,0,1:T(8,128)}) fusion(f32[3,16,64,256]{3,2,0,1:T(8,128)S(1)} %get-tuple-element.44, f32[3,16,1,256]{3,2,0,1:T(1,128)S(1)} %copy-done.24, f32[3,16,1,256]{3,2,0,1:T(1,128)S(1)} %copy-done.22, f32[3,16,66,1]{3,2,0,1:T(8,128)} %copy.307, f32[3,16,66,1]{3,2,0,1:T(8,128)} %copy.308, ...), kind=kLoop, calls=%fused_computation.82 | loop fusion | flops 13893632 | bytes 14803712 | tf_op jit(solution)/shard_map/reduce_sum | solution.py:52
  548.5 2.5 reduce.8
  551.0 11.3 %reshape.132 = f32[2048,3,2,8]{3,2,1,0:T(2,128)} reshape(f32[128,768]{1,0:T(8,128)S(1)} %reduce.8) | data formatting | bytes 786432
  562.3 5.6 copy.318
  568.7 2.6 copy.319
  576.7 11.9 %fusion.19 = f32[3,16,1024]{2,1,0:T(8,128)} fusion(f32[1024,1024]{1,0:T(8,128)} %get-tuple-element.78, f32[1024,1024]{1,0:T(8,128)} %get-tuple-element.79, f32[3,1024,16]{1,2,0:T(8,128)S(1)} %copy.322, f32[3,1024,16]{1,2,0:T(8,128)S(1)} %copy.321), kind=kOutput, calls=%fused_computation.42 | convolution fusion | flops 1210155008 | bytes 8978432 | tf_op jit(solution)/shard_map/cqx,yq->cxy/dot_general | solution.py:94
  588.6 2.6 copy.323
  591.2 3.1 reshape.133
  594.3 4.6 all-to-all-start.7
  598.9 4.3 broadcast_multiply_fusion
  604.3 2.7 reshape.134
  610.6 3.9 multiply_add_fusion
  (148 shorter events, 74.4 us)
Async XLA Ops:
  1.8 112.3 %collective-permute-start = (f32[3,16,1,256]{3,2,0,1:T(1,128)S(1)}, f32[3,16,1,256]{3,2,0,1:T(1,128)S(1)}, u32[]{:S(2)}, u32[]{:S(2)}) collective-permute-start(f32[3,16,1,256]{3,2,0,1:T(1,128)S(1)} %get-tuple-element.56), channel_id=1, source_target_pairs={{0,4},{4,8},{8,12},{12,16},{16,20},{20,24},{24,28},{28,32},{32,36}... | collective-permute-start | bytes 147464 | tf_op jit(solution)/shard_map/ppermute | solution.py:24
  6.2 107.9 %collective-permute-start.1 = (f32[3,16,1,256]{3,2,0,1:T(1,128)S(1)}, f32[3,16,1,256]{3,2,0,1:T(1,128)S(1)}, u32[]{:S(2)}, u32[]{:S(2)}) collective-permute-start(f32[3,16,1,256]{3,2,0,1:T(1,128)S(1)} %get-tuple-element.57), channel_id=1, source_target_pairs={{4,0},{8,4},{12,8},{16,12},{20,16},{24,20},{28,24},{32,28},{36,32}... | collective-permute-start | bytes 147464 | tf_op jit(solution)/shard_map/ppermute | solution.py:26
  9.3 125.8 %all-to-all-start = ((f32[3,64,256]{2,0,1:T(4,128)}), f32[3,64,256]{2,0,1:T(4,128)}, u32[]{:S(2)}, u32[]{:S(2)}) async-start(f32[3,64,256]{2,0,1:T(4,128)} %bitcast.118), calls=%async_computation | async-start | bytes 524288 | tf_op jit(solution)/shard_map/all_to_all | solution.py:68
  15.9 203.4 %copy-start.11 = (f32[3,8,2048]{2,1,0:T(8,128)}, f32[3,8,2048]{2,1,0:T(8,128)S(1)}, u32[]{:S(2)}) copy-start(f32[3,8,2048]{2,1,0:T(8,128)S(1)} %get-tuple-element.53) | copy-start | bytes 589828
  15.9 5.3 copy-start.3
  106.4 5.6 copy-start.14
  106.4 5.6 copy-start.26
  106.4 5.6 copy-start.27
  112.0 2.3 copy-start
  114.1 3.0 copy-start.17
  114.3 2.8 copy-start.19
  117.1 9.9 %copy-start.25 = (s32[8,32]{1,0:T(8,128)S(1)}, s32[8,32]{1,0:T(8,128)}, u32[]{:S(2)}) copy-start(s32[8,32]{1,0:T(8,128)} %param.15) | copy-start | bytes 3076
  121.3 12.0 %collective-permute-start.2 = (f32[3,16,66,1]{2,1,3,0:T(8,128)S(1)}, f32[3,16,66,1]{2,1,3,0:T(8,128)S(1)}, u32[]{:S(2)}, u32[]{:S(2)}) collective-permute-start(f32[3,16,66,1]{2,1,3,0:T(8,128)S(1)} %copy.278), channel_id=1, source_target_pairs={{0,1},{1,2},{2,3},{4,5},{5,6},{6,7},{8,9},{9,10},{10,11},{12,13},{... | collective-permute-start | bytes 38024 | tf_op jit(solution)/shard_map/ppermute | solution.py:24
  124.8 6.5 %collective-permute-start.3 = (f32[3,16,66,1]{2,1,3,0:T(8,128)S(1)}, f32[3,16,66,1]{2,1,3,0:T(8,128)S(1)}, u32[]{:S(2)}, u32[]{:S(2)}) collective-permute-start(f32[3,16,66,1]{2,1,3,0:T(8,128)S(1)} %copy.279), channel_id=1, source_target_pairs={{1,0},{2,1},{3,2},{5,4},{6,5},{7,6},{9,8},{10,9},{11,10},{13,12},{... | collective-permute-start | bytes 38024 | tf_op jit(solution)/shard_map/ppermute | solution.py:26
  146.5 23.8 %copy-start.18 = (f32[3,16,1,256]{3,2,0,1:T(1,128)S(1)}, f32[3,16,1,256]{3,2,0,1:T(1,128)}, u32[]{:S(2)}) copy-start(f32[3,16,1,256]{3,2,0,1:T(1,128)} %copy-done.17) | copy-start | bytes 147460
  146.5 23.8 %copy-start.20 = (f32[3,16,1,256]{3,2,0,1:T(1,128)S(1)}, f32[3,16,1,256]{3,2,0,1:T(1,128)}, u32[]{:S(2)}) copy-start(f32[3,16,1,256]{3,2,0,1:T(1,128)} %copy-done.19) | copy-start | bytes 147460
  157.9 24.0 %all-to-all-start.1 = ((f32[128,1,768]{2,1,0:T(1,128)}), f32[128,1,768]{2,1,0:T(1,128)}, u32[]{:S(2)}, u32[]{:S(2)}) async-start(f32[128,1,768]{2,1,0:T(1,128)} %reshape.123), calls=%async_computation.1 | async-start | bytes 786432 | tf_op jit(solution)/shard_map/all_to_all | solution.py:72
  195.0 25.1 %slice-start = ((s8[16777216]{0:T(1024)(128)(4,1)}), s8[4194304]{0:T(1024)(128)(4,1)S(1)}, s32[]{:S(2)}) async-start(s8[16777216]{0:T(1024)(128)(4,1)} %bitcast.121), calls=%async_computation.8 | async-start | bytes 8388608
  195.0 24.3 %copy-start.13 = (f32[2,3,8,2048]{3,2,1,0:T(8,128)S(1)}, f32[2,3,8,2048]{3,2,1,0:T(8,128)}, u32[]{:S(2)}) copy-start(f32[2,3,8,2048]{3,2,1,0:T(8,128)} %multiply_reduce_fusion) | copy-start | bytes 1179652
  195.0 25.1 %slice-start.1 = ((s8[16777216]{0:T(1024)(128)(4,1)}), s8[4194304]{0:T(1024)(128)(4,1)S(1)}, s32[]{:S(2)}) async-start(s8[16777216]{0:T(1024)(128)(4,1)} %bitcast.121), calls=%async_computation.9 | async-start | bytes 8388608
  195.0 25.1 %slice-start.2 = ((s8[16777216]{0:T(1024)(128)(4,1)}), s8[4194304]{0:T(1024)(128)(4,1)S(1)}, s32[]{:S(2)}) async-start(s8[16777216]{0:T(1024)(128)(4,1)} %bitcast.121), calls=%async_computation.10 | async-start | bytes 8388608
  195.0 25.1 %slice-start.3 = ((s8[16777216]{0:T(1024)(128)(4,1)}), s8[4194304]{0:T(1024)(128)(4,1)S(1)}, s32[]{:S(2)}) async-start(s8[16777216]{0:T(1024)(128)(4,1)} %bitcast.121), calls=%async_computation.11 | async-start | bytes 8388608
  219.3 0.7 copy-start.7
  219.3 0.7 copy-start.9
  261.4 17.4 %copy-start.1 = (f32[3,16,66,1]{3,2,0,1:T(8,128)S(1)}, f32[3,16,66,1]{3,2,0,1:T(8,128)}, u32[]{:S(2)}) copy-start(f32[3,16,66,1]{3,2,0,1:T(8,128)} %copy.281) | copy-start | bytes 38020
  261.4 17.4 %copy-start.2 = (f32[3,16,66,1]{3,2,0,1:T(8,128)S(1)}, f32[3,16,66,1]{3,2,0,1:T(8,128)}, u32[]{:S(2)}) copy-start(f32[3,16,66,1]{3,2,0,1:T(8,128)} %copy.280) | copy-start | bytes 38020
  272.8 21.5 %all-to-all-start.2 = ((f32[128,1,768]{2,1,0:T(1,128)}), f32[128,1,768]{2,1,0:T(1,128)}, u32[]{:S(2)}, u32[]{:S(2)}) async-start(f32[128,1,768]{2,1,0:T(1,128)} %reshape.125), calls=%async_computation.2 | async-start | bytes 786432 | tf_op jit(solution)/shard_map/all_to_all | solution.py:90
  278.8 14.2 %copy-start.5 = (f32[16,64,256]{2,1,0:T(8,128)S(1)}, f32[16,64,256]{2,1,0:T(8,128)}, u32[]{:S(2)}) copy-start(f32[16,64,256]{2,1,0:T(8,128)} %get-tuple-element.38) | copy-start | bytes 3145732
  325.7 9.5 %copy-start.4 = (f32[3,16,64,256]{3,2,0,1:T(8,128)S(1)}, f32[3,16,64,256]{3,2,0,1:T(8,128)}, u32[]{:S(2)}) copy-start(f32[3,16,64,256]{3,2,0,1:T(8,128)} %get-tuple-element.47) | copy-start | bytes 9437188
  330.7 8.6 %all-to-all-start.3 = ((f32[4,1,12288]{2,1,0:T(1,128)}), f32[4,1,12288]{2,1,0:T(1,128)S(1)}, u32[]{:S(2)}, u32[]{:S(2)}) async-start(f32[4,1,12288]{2,1,0:T(1,128)} %reshape.127), calls=%async_computation.3 | async-start | bytes 393216 | tf_op jit(solution)/shard_map/all_to_all | solution.py:95
  350.9 10.3 %collective-permute-start.4 = (f32[3,16,1,256]{3,2,0,1:T(1,128)S(1)}, f32[3,16,1,256]{3,2,0,1:T(1,128)S(1)}, u32[]{:S(2)}, u32[]{:S(2)}) collective-permute-start(f32[3,16,1,256]{3,2,0,1:T(1,128)S(1)} %get-tuple-element.54), channel_id=1, source_target_pairs={{0,4},{4,8},{8,12},{12,16},{16,20},{20,24},{24,28},{28,32},{32,36}... | collective-permute-start | bytes 147464 | tf_op jit(solution)/shard_map/ppermute | solution.py:24
  353.6 7.7 %collective-permute-start.5 = (f32[3,16,1,256]{3,2,0,1:T(1,128)S(1)}, f32[3,16,1,256]{3,2,0,1:T(1,128)S(1)}, u32[]{:S(2)}, u32[]{:S(2)}) collective-permute-start(f32[3,16,1,256]{3,2,0,1:T(1,128)S(1)} %get-tuple-element.55), channel_id=1, source_target_pairs={{4,0},{8,4},{12,8},{16,12},{20,16},{24,20},{28,24},{32,28},{36,32}... | collective-permute-start | bytes 147464 | tf_op jit(solution)/shard_map/ppermute | solution.py:26
  355.7 30.6 %all-to-all-start.4 = ((f32[3,64,256]{2,0,1:T(4,128)}), f32[3,64,256]{2,0,1:T(4,128)}, u32[]{:S(2)}, u32[]{:S(2)}) async-start(f32[3,64,256]{2,0,1:T(4,128)} %copy.311), calls=%async_computation.4 | async-start | bytes 524288 | tf_op jit(solution)/shard_map/all_to_all | solution.py:68
  361.2 2.8 copy-start.21
  361.2 2.8 copy-start.23
  369.5 14.3 %collective-permute-start.6 = (f32[3,16,66,1]{2,1,3,0:T(8,128)}, f32[3,16,66,1]{2,1,3,0:T(8,128)}, u32[]{:S(2)}, u32[]{:S(2)}) collective-permute-start(f32[3,16,66,1]{2,1,3,0:T(8,128)} %copy.305), channel_id=1, source_target_pairs={{0,1},{1,2},{2,3},{4,5},{5,6},{6,7},{8,9},{9,10},{10,11},{12,13},{... | collective-permute-start | bytes 38024 | tf_op jit(solution)/shard_map/ppermute | solution.py:24
  373.0 8.1 %collective-permute-start.7 = (f32[3,16,66,1]{2,1,3,0:T(8,128)}, f32[3,16,66,1]{2,1,3,0:T(8,128)}, u32[]{:S(2)}, u32[]{:S(2)}) collective-permute-start(f32[3,16,66,1]{2,1,3,0:T(8,128)} %copy.306), channel_id=1, source_target_pairs={{1,0},{2,1},{3,2},{5,4},{6,5},{7,6},{9,8},{10,9},{11,10},{13,12},{... | collective-permute-start | bytes 38024 | tf_op jit(solution)/shard_map/ppermute | solution.py:26
  410.7 24.5 %all-to-all-start.5 = ((f32[128,1,768]{2,1,0:T(1,128)}), f32[128,1,768]{2,1,0:T(1,128)}, u32[]{:S(2)}, u32[]{:S(2)}) async-start(f32[128,1,768]{2,1,0:T(1,128)} %reshape.129), calls=%async_computation.5 | async-start | bytes 786432 | tf_op jit(solution)/shard_map/all_to_all | solution.py:72
  453.6 24.4 %copy-start.8 = (f32[1,3,8,2048]{3,2,1,0:T(8,128)S(1)}, f32[1,3,8,2048]{3,2,1,0:T(8,128)}, u32[]{:S(2)}) copy-start(f32[1,3,8,2048]{3,2,1,0:T(8,128)} %copy-done.7) | copy-start | bytes 589828
  453.6 24.4 %copy-start.10 = (f32[1,3,8,2048]{3,2,1,0:T(8,128)S(1)}, f32[1,3,8,2048]{3,2,1,0:T(8,128)}, u32[]{:S(2)}) copy-start(f32[1,3,8,2048]{3,2,1,0:T(8,128)} %copy-done.9) | copy-start | bytes 589828
  453.6 24.4 %copy-start.12 = (f32[3,8,2048]{2,1,0:T(8,128)S(1)}, f32[3,8,2048]{2,1,0:T(8,128)}, u32[]{:S(2)}) copy-start(f32[3,8,2048]{2,1,0:T(8,128)} %copy-done.11) | copy-start | bytes 589828
  453.6 24.5 %copy-start.16 = (f32[3,8,2048]{2,1,0:T(8,128)S(1)}, f32[3,8,2048]{2,1,0:T(8,128)}, u32[]{:S(2)}) copy-start(f32[3,8,2048]{2,1,0:T(8,128)} %get-tuple-element.52) | copy-start | bytes 589828
  519.8 17.1 %copy-start.22 = (f32[3,16,1,256]{3,2,0,1:T(1,128)S(1)}, f32[3,16,1,256]{3,2,0,1:T(1,128)}, u32[]{:S(2)}) copy-start(f32[3,16,1,256]{3,2,0,1:T(1,128)} %copy-done.21) | copy-start | bytes 147460
  519.8 17.1 %copy-start.24 = (f32[3,16,1,256]{3,2,0,1:T(1,128)S(1)}, f32[3,16,1,256]{3,2,0,1:T(1,128)}, u32[]{:S(2)}) copy-start(f32[3,16,1,256]{3,2,0,1:T(1,128)} %copy-done.23) | copy-start | bytes 147460
  530.8 17.7 %all-to-all-start.6 = ((f32[128,1,768]{2,1,0:T(1,128)}), f32[128,1,768]{2,1,0:T(1,128)}, u32[]{:S(2)}, u32[]{:S(2)}) async-start(f32[128,1,768]{2,1,0:T(1,128)} %reshape.131), calls=%async_computation.6 | async-start | bytes 786432 | tf_op jit(solution)/shard_map/all_to_all | solution.py:90
  536.9 10.1 %copy-start.6 = (f32[16,64,256]{2,1,0:T(8,128)S(1)}, f32[16,64,256]{2,1,0:T(8,128)}, u32[]{:S(2)}) copy-start(f32[16,64,256]{2,1,0:T(8,128)} %get-tuple-element.38) | copy-start | bytes 3145732
  568.7 4.5 copy-start.15
  594.3 8.9 %all-to-all-start.7 = ((f32[4,1,12288]{2,1,0:T(1,128)}), f32[4,1,12288]{2,1,0:T(1,128)S(1)}, u32[]{:S(2)}, u32[]{:S(2)}) async-start(f32[4,1,12288]{2,1,0:T(1,128)} %reshape.133), calls=%async_computation.7 | async-start | bytes 393216 | tf_op jit(solution)/shard_map/all_to_all | solution.py:95
where the time goes:
time: 628 us; the launch traced here: 619 us
  local copies, waits for them, and re-layouts  187 us (30%)
  other arithmetic  187 us (30%)
  matrix products  157 us (25%)
  starting transfers between devices  77.5 us (12%)
  waiting for transfers between devices  9.46 us (2%)
    unnamed x80, local copies, waits for them, and re-layouts  87.8 us
    sin x2, other arithmetic, angle_table(): return jnp.concatenate([jnp.cos(angles), jnp.sin(angles)], axis=1)  84.3 us
    dot_general x2, matrix products, inverse(): jnp.einsum('rckq,pq->rckp', paired, strike_table, precision=HIGHEST)  69.5 us
    dot_general x2, matrix products, forward(): mixed = jnp.einsum('rcpk,pq->rckq', owned, strike_table, precision=HIGHEST)  48.6 us
    all_to_all x2, starting transfers between devices, forward(): lax.all_to_all(stacked, ('wide', 'narrow'), split_axis=3, concat_axis=2,...  25.2 us
    reduce_sum x2, other arithmetic, yielded_force(): squares = jnp.sum(force * force, axis=0)  24.3 us
    dot_general x2, matrix products, inverse(): values = jnp.einsum('cqx,yq->cxy', folded, dip_table, precision=HIGHEST)  22.2 us
    dot_general x2, matrix products, forward(): spectra = jnp.einsum('cxy,yq->cxq', gathered, dip_table, precision=HIGHEST)  16.4 us
  transfers between devices with their start and end apart: 16, of which 4 were waited for; matrix products, arithmetic and copies ran while one was open for 30% of the time, Pallas kernels for 0%

commit v1 on v0

v1 whole, which is shorter than its diff:
```python
import functools
import math

import jax
import jax.numpy as jnp
import ml_dtypes
import numpy as np
from jax import lax
from jax.experimental import pallas as pl
from jax.experimental.pallas import tpu as pltpu
from jax.sharding import PartitionSpec as P

DT = 0.1
DAMPING = 0.5
ALL = ("wide", "narrow")
F32 = jnp.float32
BF16 = jnp.bfloat16


def split_table(table):
    table = np.asarray(table, np.float64)
    high = table.astype(ml_dtypes.bfloat16)
    low = (table - high.astype(np.float64)).astype(ml_dtypes.bfloat16)
    return np.stack([high, low])


def make_tables():
    factor = 1.0 / math.sqrt(2048 * 1024)
    eye2 = np.eye(2)
    eye4 = np.eye(4)
    eye8 = np.eye(8)
    eye16 = np.eye(16)
    r8 = np.arange(8).reshape(2, 4)
    y1 = np.arange(8).reshape(4, 2)
    theta = 2 * np.pi * r8[:, :, None, None] * y1[None, None] / 8
    radix = np.stack([np.cos(theta), -np.sin(theta)])
    radix = np.einsum("isrnl,xz,fg->isxfrnglz", radix, eye16, eye2).reshape(512, 256)
    unradix = np.stack([np.cos(theta), -np.sin(theta)])
    unradix = np.einsum("isrnl,xz,fg->nglzisxfr", unradix, eye16, eye2).reshape(256, 512)
    y0 = np.arange(128)
    theta = 2 * np.pi * r8[:, :, None] * y0 / 1024
    turn = np.stack([np.cos(theta), -np.sin(theta)])[:, :, None, None]
    dip_turn = np.broadcast_to(turn, (2, 2, 16, 2, 4, 128)).reshape(2, 2, 128, 128) * factor
    alt = (-1.0) ** y0
    place = np.stack([np.arange(64), 63 - np.arange(64)])
    theta = 2 * np.pi * place[:, :, None] * y0 / 128
    cos, sin = np.cos(theta), np.sin(theta)
    dip_out = np.zeros((2, 136, 256))
    dip_out[:, :64] = np.concatenate([cos, sin], -1)
    dip_out[:, 64:128] = np.concatenate([-sin, cos], -1)
    dip_out[0, 128, :128] = alt
    dip_in = np.zeros((2, 128, 2, 2, 128))
    for s in range(2):
        rows = slice(s * 64, s * 64 + 64)
        dip_in[0, rows, s, 0] = cos[s]
        dip_in[0, rows, s, 1] = sin[s]
        dip_in[1, rows, s, 0] = -sin[s]
        dip_in[1, rows, s, 1] = cos[s]
    dip_in = dip_in.reshape(256, 512)
    theta = 2 * np.pi * np.outer(y0, y0) / 128
    cos, sin = np.cos(theta), np.sin(theta)
    strike_in = np.block([[cos, -sin], [sin, cos]])
    strike_out = np.block([[cos, -sin], [sin, cos]])
    a = np.arange(16)
    theta = 2 * np.pi * np.outer(a, y0) / 2048
    turn = np.stack([np.cos(theta), -np.sin(theta)])
    strike_turn = np.broadcast_to(turn[:, :, None], (2, 16, 8, 128)).reshape(2, 128, 128)
    theta = 2 * np.pi * np.outer(a, a) / 16
    cos, sin = np.kron(np.cos(theta), eye8), np.kron(np.sin(theta), eye8)
    strike_mix = np.block([[cos, sin], [-sin, cos]])
    strike_unmix = np.block([[cos, -sin], [sin, cos]]) * factor
    reverse = np.zeros((128, 128))
    reverse[(128 - y0) % 128, y0] = 1.0
    return {
        "radix": split_table(radix),
        "unradix": split_table(unradix),
        "dip_turn": dip_turn.astype(np.float32),
        "undip_turn": (dip_turn / factor * 2.0).astype(np.float32),
        "dip_out": split_table(dip_out),
        "dip_in": split_table(dip_in),
        "strike_in": split_table(strike_in),
        "strike_out": split_table(strike_out),
        "strike_turn": strike_turn.astype(np.float32),
        "strike_mix": split_table(strike_mix),
        "strike_unmix": split_table(strike_unmix),
        "reverse": reverse.astype(ml_dtypes.bfloat16),
    }


TABLES = make_tables()


def halves(x):
    high = x.astype(BF16)
    return high, (x - high.astype(F32)).astype(BF16)


def dot(a, b, contract=(1, 0)):
    return lax.dot_general(
        a, b, (((contract[0],), (contract[1],)), ((), ())), preferred_element_type=F32
    )


def left_dot(table, x, contract=(1, 0)):
    high, low = halves(x)
    return dot(table[0], high, contract) + (
        dot(table[1], high, contract) + dot(table[0], low, contract)
    )


def right_dot(x, table):
    high, low = halves(x)
    return dot(high, table[0]) + (dot(low, table[0]) + dot(high, table[1]))


def lanes(shape):
    return lax.broadcasted_iota(jnp.int32, shape, len(shape) - 1)


def rows_of(shape):
    return lax.broadcasted_iota(jnp.int32, shape, len(shape) - 2)


def neighbour_sum(center, above, below, top, bottom, left, right):
    rows = rows_of(center.shape)
    north = jnp.where(rows == 0, top, pltpu.roll(center, 1, 0))
    south = jnp.where(rows == 63, bottom, pltpu.roll(center, 63, 0))
    c0, c1 = center[:, :128], center[:, 128:]
    lane = lanes(c0.shape)
    w0, w1 = pltpu.roll(c0, 1, 1), pltpu.roll(c1, 1, 1)
    e0, e1 = pltpu.roll(c0, 127, 1), pltpu.roll(c1, 127, 1)
    west = jnp.concatenate([jnp.where(lane == 0, left, w0), jnp.where(lane == 0, w0, w1)], 1)
    east = jnp.concatenate([jnp.where(lane == 127, e1, e0), jnp.where(lane == 127, right, e1)], 1)
    return ((above + below) + (north + south)) + (west + east)


def plane_force(centers, sums, region, plastic, shear_ref, yields_ref):
    modulus = jnp.full(region.shape, shear_ref[0], F32)
    level = jnp.full(region.shape, yields_ref[0], F32)
    for label in range(1, 4):
        modulus = jnp.where(region == label, shear_ref[label], modulus)
        level = jnp.where(region == label, yields_ref[label], level)
    force = [modulus * (total - 6.0 * center) for total, center in zip(sums, centers)]
    squares = force[0] * force[0] + force[1] * force[1] + force[2] * force[2]
    capped = lax.rsqrt(1.0 + squares / (level * level))
    scaling = jnp.where(plastic > 0.5, capped, 1.0)
    return [f * scaling for f in force]


def slot(c, z):
    return c * 16 + z


def halo_columns(left_ref, right_ref, place):
    left = pltpu.roll(left_ref[...], lax.rem(128 - place, 128), 1)
    right = pltpu.roll(right_ref[...], 127 - place, 1)
    return left, right


def put_columns(left_ref, right_ref, center, place):
    c0, c1 = center[:, :128], center[:, 128:]
    lane = lanes(c0.shape)
    left_ref[...] = jnp.where(lane == place, pltpu.roll(c0, place, 1), left_ref[...])
    right_ref[...] = jnp.where(
        lane == place, pltpu.roll(c1, lax.rem(place + 1, 128), 1), right_ref[...]
    )


def edges_kernel(u_ref, flags_ref, first_ref, last_ref, left_ref, right_ref, plastic_ref):
    z = pl.program_id(0)

    @pl.when(z == 0)
    def _():
        left_ref[...] = jnp.zeros_like(left_ref)
        right_ref[...] = jnp.zeros_like(right_ref)
        wide = (rows_of((64, 8)) // 8 == lanes((64, 8))).astype(F32)
        high = (rows_of((32, 256)) == lanes((32, 256)) // 8).astype(F32)
        marks = (flags_ref[...] == 1).astype(F32)
        plastic_ref[...] = dot(dot(wide, marks), high)

    for c in range(3):
        plane = u_ref[c, 0]
        place = slot(c, z)
        first_ref[pl.ds(place, 1), :] = plane[0:1]
        last_ref[pl.ds(place, 1), :] = plane[63:64]
        put_columns(left_ref, right_ref, plane, place)


def slip_kernel(
    shear_ref, yields_ref, u_ref, v_ref, region_ref, plastic_ref,
    top_ref, bottom_ref, left_ref, right_ref, send_ref,
):
    centers, sums = [], []
    for c in range(3):
        center = u_ref[c, 0]
        left, right = halo_columns(left_ref, right_ref, slot(c, 0))
        place = slot(c, 0)
        sums.append(
            neighbour_sum(
                center, u_ref[c, 1], jnp.zeros_like(center),
                top_ref[place : place + 1, :], bottom_ref[place : place + 1, :], left, right,
            )
        )
        centers.append(center)
    force = plane_force(centers, sums, region_ref[0], plastic_ref[...], shear_ref, yields_ref)
    for c in range(3):
        v = v_ref[c, 0]
        v = v + DT * (force[c] - DAMPING * v)
        moved = centers[c] + DT * v
        for f, values in enumerate((centers[c], moved)):
            for n in range(4):
                for half in range(2):
                    start = f * 96 + c * 32 + half * 16
                    send_ref[n, start : start + 16, :] = values[
                        n * 16 : n * 16 + 16, half * 128 : half * 128 + 128
                    ]


def step_one_kernel(
    shear_ref, yields_ref, u_ref, v_ref, region_ref, plastic_ref,
    top_ref, bottom_ref, left_ref, right_ref,
    new_u_ref, new_v_ref, first_ref, last_ref, left_out_ref, right_out_ref,
):
    z = pl.program_id(0)

    @pl.when(z == 0)
    def _():
        left_out_ref[...] = jnp.zeros_like(left_out_ref)
        right_out_ref[...] = jnp.zeros_like(right_out_ref)

    lower = jnp.where(z > 0, 1.0, 0.0).astype(F32)
    upper = jnp.where(z < 15, 1.0, 0.0).astype(F32)
    centers, sums = [], []
    for c in range(3):
        place = slot(c, z)
        center = u_ref[c, z]
        left, right = halo_columns(left_ref, right_ref, place)
        sums.append(
            neighbour_sum(
                center,
                u_ref[c, jnp.minimum(z + 1, 15)] * upper,
                u_ref[c, jnp.maximum(z - 1, 0)] * lower,
                top_ref[pl.ds(place, 1), :], bottom_ref[pl.ds(place, 1), :], left, right,
            )
        )
        centers.append(center)
    force = plane_force(centers, sums, region_ref[0], plastic_ref[...], shear_ref, yields_ref)
    damping = jnp.where(z == 0, DAMPING, 0.0).astype(F32)
    for c in range(3):
        v = v_ref[c, 0]
        v = v + DT * (force[c] - damping * v)
        u = centers[c] + DT * v
        new_v_ref[c, 0] = v
        new_u_ref[c, 0] = u
        place = slot(c, z)
        first_ref[pl.ds(place, 1), :] = u[0:1]
        last_ref[pl.ds(place, 1), :] = u[63:64]
        put_columns(left_out_ref, right_out_ref, u, place)


def step_two_kernel(
    shear_ref, yields_ref, u_ref, v_ref, region_ref, plastic_ref,
    top_ref, bottom_ref, left_ref, right_ref, new_u_ref, new_v_ref,
):
    z = pl.program_id(0) + 2
    upper = jnp.where(z < 15, 1.0, 0.0).astype(F32)
    centers, sums = [], []
    for c in range(3):
        place = slot(c, z)
        center = u_ref[c, z]
        left, right = halo_columns(left_ref, right_ref, place)
        sums.append(
            neighbour_sum(
                center,
                u_ref[c, jnp.minimum(z + 1, 15)] * upper,
                u_ref[c, z - 1],
                top_ref[pl.ds(place, 1), :], bottom_ref[pl.ds(place, 1), :], left, right,
            )
        )
        centers.append(center)
    force = plane_force(centers, sums, region_ref[0], plastic_ref[...], shear_ref, yields_ref)
    for c in range(3):
        v = v_ref[c, 0] + DT * force[c]
        new_v_ref[c, 0] = v
        new_u_ref[c, 0] = centers[c] + DT * v


def traction_plane(recv_ref, f, c):
    parts = []
    for half in range(2):
        start = f * 96 + c * 32 + half * 16
        parts.append(
            jnp.concatenate([recv_ref[n, start : start + 16, :] for n in range(4)], 0)
        )
    return jnp.concatenate(parts, 1)


def traction_edges_kernel(recv_ref, first_ref, last_ref, left_ref, right_ref):
    left_ref[...] = jnp.zeros_like(left_ref)
    right_ref[...] = jnp.zeros_like(right_ref)
    first_ref[...] = jnp.zeros_like(first_ref)
    last_ref[...] = jnp.zeros_like(last_ref)
    for c in range(3):
        plane = traction_plane(recv_ref, 0, c)
        first_ref[c : c + 1, :] = plane[0:1]
        last_ref[c : c + 1, :] = plane[63:64]
        put_columns(left_ref, right_ref, plane, slot(c, 0))


def last_kernel(
    shear_ref, yields_ref, u_ref, v_ref, region_ref, plastic_ref,
    top_ref, bottom_ref, left_ref, right_ref,
    recv_ref, ttop_ref, tbottom_ref, tleft_ref, tright_ref,
    _old_u_ref, _old_v_ref, new_u_ref, new_v_ref,
):
    square = DT * DT
    traction = [traction_plane(recv_ref, 0, c) for c in range(3)]
    surface = [u_ref[c, 0] + square * traction[c] for c in range(3)]
    for z in range(2):
        centers, sums = [], []
        for c in range(3):
            place = slot(c, z)
            left, right = halo_columns(left_ref, right_ref, place)
            top = top_ref[place : place + 1, :]
            bottom = bottom_ref[place : place + 1, :]
            if z == 0:
                tleft, tright = halo_columns(tleft_ref, tright_ref, place)
                left = left + square * tleft
                right = right + square * tright
                top = top + square * ttop_ref[c : c + 1, :]
                bottom = bottom + square * tbottom_ref[c : c + 1, :]
                center = surface[c]
                below = jnp.zeros_like(center)
            else:
                center = u_ref[c, 1]
                below = surface[c]
            sums.append(neighbour_sum(center, u_ref[c, z + 1], below, top, bottom, left, right))
            centers.append(center)
        force = plane_force(
            centers, sums, region_ref[z], plastic_ref[...], shear_ref, yields_ref
        )
        for c in range(3):
            v = v_ref[c, z]
            if z == 0:
                v = v + DT * traction[c]
                v = v + DT * (force[c] + (traction_plane(recv_ref, 1, c) - DAMPING * v))
            else:
                v = v + DT * force[c]
            new_v_ref[c, z] = v
            new_u_ref[c, z] = centers[c] + DT * v


def history_kernel(where_ref, kernel_ref, history_ref, own_ref, main_ref, edge_ref):
    low = where_ref[0] == 1
    width = own_ref.shape[1]

    def step(m, total):
        out = []
        for c in range(3):
            one = kernel_ref[m + 1, c].astype(F32)
            two = kernel_ref[m + 2, c].astype(F32)
            for ri in range(2):
                past = history_ref[m, ri, c].astype(F32)
                p1, p2 = total[c * 2 + ri]
                out.append((p1 + one * past, p2 + two * past))
        return tuple(out)

    zero = jnp.zeros((8, width), F32)
    total = lax.fori_loop(0, 31, step, tuple((zero, zero) for _ in range(6)))
    values = [None] * 18
    for c in range(3):
        one = kernel_ref[32, c].astype(F32)
        for ri in range(2):
            p1, p2 = total[c * 2 + ri]
            values[ri * 3 + c] = p1 + one * history_ref[31, ri, c].astype(F32)
            values[6 + ri * 3 + c] = p2
        values[12 + c] = kernel_ref[0, c].astype(F32)
        values[15 + c] = kernel_ref[1, c].astype(F32)
    for i, value in enumerate(values):
        row = [value[r : r + 1] for r in range(8)]
        for r, (a, b) in enumerate(((0, 4), (1, 3), (2, 2), (3, 1))):
            own_ref[i * 4 + r : i * 4 + r + 1, :] = jnp.where(low, row[a], row[b])
        for r, (a, b) in enumerate(((4, 4), (5, 7), (6, 6), (7, 5))):
            main_ref[i * 4 + r : i * 4 + r + 1, :] = jnp.where(low, row[a], row[b])
        edge_ref[i : i + 1, :] = row[0]


def mirror_kernel(where_ref, reverse_ref, own_ref, main_ref, edge_ref, out_ref, tiles, turned):
    low = where_ref[0] == 1
    special = where_ref[1]
    for i in range(18):
        own = own_ref[i * 4 : i * 4 + 4, :]
        main = main_ref[i * 4 : i * 4 + 4, :]
        edge = edge_ref[i : i + 1, :]
        other = jnp.where(rows_of(main.shape) == 0, edge, main)
        tiles[i * 8 : i * 8 + 4, :] = jnp.where(low, own, main)
        tiles[i * 8 + 4 : i * 8 + 8, :] = jnp.where(low, other, own)
    for block in range(16):
        part = slice(block * 128, block * 128 + 128)
        high, rest = halves(tiles[:, part])
        turned[:, part] = dot(high, reverse_ref[...]) + dot(rest, reverse_ref[...])
    lane = lanes((8, 128))
    row = rows_of((8, 128))
    upper = row >= 4
    chosen = (lax.rem(row, 4) + (1 - special)) == 0

    def swap(x):
        return pltpu.roll(x, 4, 0)

    for block in range(16):
        part = slice(block * 128, block * 128 + 128)
        mirror = slice((15 - block) * 128, (15 - block) * 128 + 128)
        first = ((16 - block) % 16) * 128
        first = slice(first, first + 128)

        def load(i):
            rows = slice(i * 8, i * 8 + 8)
            back = jnp.where(lane == 0, turned[rows, first], turned[rows, mirror])
            return tiles[rows, part], back

        for c in range(3):
            for k in range(2):
                t, b = load(12 + k * 3 + c)
                own = 0.5 * (t + b)
                other = swap(own)
                mean = jnp.where(chosen, 0.5 * (own + other), 0.5 * (t + swap(b)))
                diff = jnp.where(chosen, 0.5 * (own - other), 0.0)
                out_ref[k, c, :, part] = jnp.where(upper, swap(mean), mean)
                out_ref[2 + k, c, :, part] = jnp.where(upper, swap(diff), diff)
            pair = []
            for k in range(2):
                tr, br = load(k * 6 + c)
                ti, bi = load(k * 6 + 3 + c)
                hr, hi = 0.5 * (tr + br), 0.5 * (ti - bi)
                sr, si = swap(hr), swap(hi)
                pair.append(
                    (
                        jnp.where(chosen, hr - si, 0.5 * (tr + swap(br))),
                        jnp.where(chosen, hi + sr, 0.5 * (ti - swap(bi))),
                        hr + si,
                        hi - sr,
                    )
                )
            out_ref[4, c, :, part] = jnp.where(upper, swap(pair[1][0]), pair[0][0])
            out_ref[5, c, :, part] = jnp.where(upper, swap(pair[1][1]), pair[0][1])
            out_ref[6, c, :, part] = pair[0][2]
            out_ref[7, c, :, part] = pair[0][3]


def dip_kernel(radix_ref, turn_ref, out_table_ref, recv_ref, send_ref):
    wide = []
    for c in range(3):
        pieces = []
        for n in range(4):
            for f in range(2):
                start = f * 96 + c * 32
                pieces.append(recv_ref[n, start : start + 32, :])
        wide.append(jnp.concatenate(pieces, 0))
    z = left_dot(radix_ref, jnp.concatenate(wide, 1))
    lane = lanes((1, 128))
    for s in range(2):
        tr, ti = turn_ref[0, s], turn_ref[1, s]
        for c in range(3):
            part = slice(c * 128, c * 128 + 128)
            zr = z[s * 128 : s * 128 + 128, part]
            zi = z[256 + s * 128 : 384 + s * 128, part]
            turned = jnp.concatenate([zr * tr - zi * ti, zr * ti + zi * tr], 1)
            high, low = halves(turned)
            table, rest = out_table_ref[0, s], out_table_ref[1, s]
            res = dot(table, high, (1, 1)) + (dot(rest, high, (1, 1)) + dot(table, low, (1, 1)))
            imag = res[64:128]
            if s == 0:
                extra = jnp.where(lax.rem(lane, 4) == 0, res[128:129], 0.0)
                imag = jnp.where(rows_of(imag.shape) == 0, imag + extra, imag)
            send_ref[pl.ds(s * 384 + c * 2, 64, stride=6), :] = res[0:64]
            send_ref[pl.ds(s * 384 + c * 2 + 1, 64, stride=6), :] = imag


def strike_kernel(
    in_ref, turn_ref, mix_ref, reverse_ref, unmix_ref, out_table_ref,
    coef_ref, recv_ref, send_ref, spec, back, total,
):
    tr, ti = turn_ref[0], turn_ref[1]
    real, imag = [], []
    for c in range(3):
        re = recv_ref[pl.ds(c * 2, 128, stride=6), :].T
        im = recv_ref[pl.ds(c * 2 + 1, 128, stride=6), :].T
        y = right_dot(jnp.concatenate([re, im], 1), in_ref)
        yr, yi = y[:, :128], y[:, 128:]
        real.append(yr * tr - yi * ti)
        imag.append(yr * ti + yi * tr)
    stacked = jnp.concatenate([jnp.concatenate(real, 1), jnp.concatenate(imag, 1)], 0)
    spec[...] = left_dot(mix_ref, stacked)
    for c in range(3):
        part = slice(c * 128, c * 128 + 128)
        high, low = halves(spec[:, part])
        back[:, part] = dot(high, reverse_ref[...]) + dot(low, reverse_ref[...])
    lane = lanes((8, 128))
    upper = rows_of((8, 128)) >= 4

    def swap(x):
        return pltpu.roll(x, 4, 0)

    for c in range(3):
        part = slice(c * 128, c * 128 + 128)
        for block in range(16):
            wave = slice(block * 128, block * 128 + 128)
            a0, a1 = coef_ref[0, c, :, wave], coef_ref[1, c, :, wave]
            m0, m1 = coef_ref[2, c, :, wave], coef_ref[3, c, :, wave]
            for ri in range(2):
                rows = slice(ri * 128 + block * 8, ri * 128 + block * 8 + 8)
                first = ri * 128 + ((16 - block) % 16) * 8
                other = ri * 128 + (15 - block) * 8
                s = spec[rows, part]
                r = jnp.where(
                    lane == 0, back[first : first + 8, part], back[other : other + 8, part]
                )
                if ri == 1:
                    r = -r
                t = a0 * s + m0 * r + coef_ref[4 + ri, c, :, wave]
                q = a0 * r + m0 * s + coef_ref[6 + ri, c, :, wave]
                more = (DT * DT) * (a0 * swap(t) + m0 * swap(q)) + a1 * swap(s) + m1 * swap(r)
                total[rows, part] = t + jnp.where(upper, more, 0.0)
    y = left_dot(unmix_ref, total[...])
    for c in range(3):
        part = slice(c * 128, c * 128 + 128)
        yr, yi = y[:128, part], y[128:, part]
        turned = jnp.concatenate([yr * tr + yi * ti, yi * tr - yr * ti], 1)
        high, low = halves(turned)
        res = dot(out_table_ref[0], high, (1, 1)) + (
            dot(out_table_ref[1], high, (1, 1)) + dot(out_table_ref[0], low, (1, 1))
        )
        send_ref[pl.ds(c * 2, 128, stride=6), :] = res[:128]
        send_ref[pl.ds(c * 2 + 1, 128, stride=6), :] = res[128:]


def undip_kernel(in_ref, turn_ref, unradix_ref, recv_ref, send_ref):
    row = rows_of((128, 128))
    lane = lanes((128, 128))
    alt = jnp.where(lax.rem(lane, 2) == 0, 0.5, -0.5).astype(F32)
    stacks = [[], [], [], []]
    for c in range(3):
        re = recv_ref[pl.ds(c * 2, 128, stride=6), :].T
        im = recv_ref[pl.ds(c * 2 + 1, 128, stride=6), :].T
        h = right_dot(jnp.concatenate([re, im], 1), in_ref)
        for s in range(2):
            hr = h[:, s * 256 : s * 256 + 128]
            hi = h[:, s * 256 + 128 : s * 256 + 256]
            if s == 0:
                fix = alt * im[:, 0:1] - 0.5 * re[:, 0:1]
                hr = hr + jnp.where(lax.rem(row, 4) == 0, fix, 0.0)
            tr, ti = turn_ref[0, s], turn_ref[1, s]
            stacks[s].append(hr * tr + hi * ti)
            stacks[2 + s].append(hi * tr - hr * ti)
    stacked = jnp.concatenate([jnp.concatenate(part, 1) for part in stacks], 0)
    out = left_dot(unradix_ref, stacked)
    for n in range(4):
        for f in range(2):
            for c in range(3):
                start = f * 96 + c * 32
                row0 = (n * 2 + f) * 32
                send_ref[n, start : start + 32, :] = out[row0 : row0 + 32, c * 128 : c * 128 + 128]


def full(shape):
    zeros = (0,) * len(shape)
    return pl.BlockSpec(shape, lambda *_: zeros)


SMEM = pl.BlockSpec(memory_space=pltpu.SMEM)


def shape_of(*shape):
    return jax.ShapeDtypeStruct(shape, F32)


def call(body, out_shape, args, smem=0, scratch=(), flops=0, name=None):
    outs = out_shape if isinstance(out_shape, (tuple, list)) else [out_shape]
    size = sum(math.prod(x.shape) * 4 for x in list(args) + list(outs))
    out_specs = [full(x.shape) for x in outs]
    return pl.pallas_call(
        body,
        grid=(1,),
        in_specs=[SMEM] * smem + [full(x.shape) for x in args[smem:]],
        out_specs=out_specs if isinstance(out_shape, (tuple, list)) else out_specs[0],
        out_shape=out_shape,
        scratch_shapes=scratch,
        cost_estimate=pl.CostEstimate(flops=flops, bytes_accessed=size, transcendentals=0),
        name=name,
    )(*args)


def halo(first, last, left, right):
    up = [(i, i + 1) for i in range(31)]
    down = [(i + 1, i) for i in range(31)]
    top = lax.ppermute(last, "wide", up)
    bottom = lax.ppermute(first, "wide", down)
    up = [(i, i + 1) for i in range(3)]
    down = [(i + 1, i) for i in range(3)]
    from_left = lax.ppermute(right, "narrow", up)
    from_right = lax.ppermute(left, "narrow", down)
    return top, bottom, from_left, from_right


def exchange(x, axis):
    return lax.all_to_all(x, axis, split_axis=0, concat_axis=0, tiled=True)


def all_exchange(x):
    return exchange(x.reshape(128, 1, 768), ALL).reshape(768, 128)


def body(u, v, region, flags, shear, yields, history, kernel):
    device = lax.axis_index(ALL)
    where = jnp.stack([device < 64, device == 0]).astype(jnp.int32)
    edge_shapes = [shape_of(48, 256)] * 2 + [shape_of(64, 128)] * 2
    plane_block = pl.BlockSpec((3, 1, 64, 256), lambda z: (0, z, 0, 0))
    first, last, left, right, plastic = pl.pallas_call(
        edges_kernel,
        grid=(16,),
        in_specs=[plane_block, full((8, 32))],
        out_specs=[full(s.shape) for s in edge_shapes] + [full((64, 256))],
        out_shape=edge_shapes + [shape_of(64, 256)],
        cost_estimate=pl.CostEstimate(flops=0, bytes_accessed=3300000, transcendentals=0),
        name="edges",
    )(u, flags)
    halo_one = halo(first, last, left, right)

    width = 256
    own, main, edge = pl.pallas_call(
        history_kernel,
        grid=(2048 // width,),
        in_specs=[
            SMEM,
            pl.BlockSpec((33, 3, 8, width), lambda i: (0, 0, 0, i)),
            pl.BlockSpec((32, 2, 3, 8, width), lambda i: (0, 0, 0, 0, i)),
        ],
        out_specs=[
            pl.BlockSpec((72, width), lambda i: (0, i)),
            pl.BlockSpec((72, width), lambda i: (0, i)),
            pl.BlockSpec((18, width), lambda i: (0, i)),
        ],
        out_shape=[shape_of(72, 2048), shape_of(72, 2048), shape_of(18, 2048)],
        cost_estimate=pl.CostEstimate(flops=0, bytes_accessed=11000000, transcendentals=0),
        name="history",
    )(where, kernel, history)
    main = lax.ppermute(main, ALL, [(i, 127 - i) for i in range(128)])
    edge = lax.ppermute(edge, ALL, [(64, 0)] + [(i, 128 - i) for i in range(65, 128)])

    near = lambda depth: pl.BlockSpec((3, depth, 64, 256), lambda *_: (0, 0, 0, 0))
    slab = lambda depth: pl.BlockSpec((depth, 64, 256), lambda *_: (0, 0, 0))
    halo_specs = [full((48, 256))] * 2 + [full((64, 128))] * 2
    send = pl.pallas_call(
        slip_kernel,
        grid=(1,),
        in_specs=[SMEM, SMEM, near(2), near(1), slab(1), full((64, 256))] + halo_specs,
        out_specs=full((4, 192, 128)),
        out_shape=shape_of(4, 192, 128),
        cost_estimate=pl.CostEstimate(flops=0, bytes_accessed=1500000, transcendentals=0),
        name="slip",
    )(shear, yields, u, v, region, plastic, *halo_one)
    lines = exchange(send, "narrow")

    t = TABLES
    send = call(
        dip_kernel, shape_of(768, 128), (t["radix"], t["dip_turn"], t["dip_out"], lines), name="dip"
    )
    waves = all_exchange(send)

    new_u, new_v, first, last, left, right = pl.pallas_call(
        step_one_kernel,
        grid=(16,),
        in_specs=[
            SMEM, SMEM, near(16), plane_block,
            pl.BlockSpec((1, 64, 256), lambda z: (z, 0, 0)), full((64, 256)),
        ]
        + halo_specs,
        out_specs=[plane_block] * 2 + [full(s.shape) for s in edge_shapes],
        out_shape=[shape_of(3, 16, 64, 256)] * 2 + edge_shapes,
        cost_estimate=pl.CostEstimate(flops=0, bytes_accessed=14000000, transcendentals=0),
        name="step_one",
    )(shear, yields, u, v, region, plastic, *halo_one)
    halo_two = halo(first, last, left, right)

    coefficients = call(
        mirror_kernel,
        shape_of(8, 3, 8, 2048),
        (where, t["reverse"], own, main, edge),
        smem=1,
        scratch=[pltpu.VMEM((144, 2048), F32)] * 2,
        name="mirror",
    )
    send = call(
        strike_kernel,
        shape_of(768, 128),
        (
            t["strike_in"], t["strike_turn"], t["strike_mix"], t["reverse"],
            t["strike_unmix"], t["strike_out"], coefficients, waves,
        ),
        scratch=[pltpu.VMEM((256, 384), F32)] * 3,
        name="strike",
    )
    columns = all_exchange(send)

    later = lambda z: (0, z + 2, 0, 0)
    out_u, out_v = pl.pallas_call(
        step_two_kernel,
        grid=(14,),
        in_specs=[
            SMEM, SMEM, near(16), pl.BlockSpec((3, 1, 64, 256), later),
            pl.BlockSpec((1, 64, 256), lambda z: (z + 2, 0, 0)), full((64, 256)),
        ]
        + halo_specs,
        out_specs=[pl.BlockSpec((3, 1, 64, 256), later)] * 2,
        out_shape=[shape_of(3, 16, 64, 256)] * 2,
        cost_estimate=pl.CostEstimate(flops=0, bytes_accessed=14000000, transcendentals=0),
        name="step_two",
    )(shear, yields, new_u, new_v, region, plastic, *halo_two)

    send = call(
        undip_kernel,
        shape_of(4, 192, 128),
        (t["dip_in"], t["undip_turn"], t["unradix"], columns),
        name="undip",
    )
    tractions = exchange(send, "narrow")
    edges = call(
        traction_edges_kernel,
        [shape_of(8, 256)] * 2 + [shape_of(64, 128)] * 2,
        (tractions,),
        name="traction_edges",
    )
    halo_three = halo(*edges)
    any_spec = pl.BlockSpec(memory_space=pl.ANY)
    return tuple(
        pl.pallas_call(
            last_kernel,
            grid=(1,),
            in_specs=[SMEM, SMEM, near(4), near(2), slab(2), full((64, 256))]
            + halo_specs
            + [full((4, 192, 128)), full((8, 256)), full((8, 256)), full((64, 128)), full((64, 128))]
            + [any_spec] * 2,
            out_specs=[near(2)] * 2,
            out_shape=[shape_of(3, 16, 64, 256)] * 2,
            input_output_aliases={15: 0, 16: 1},
            cost_estimate=pl.CostEstimate(flops=0, bytes_accessed=4000000, transcendentals=0),
            name="last",
        )(
            shear, yields, new_u, new_v, region, plastic, *halo_two,
            tractions, *halo_three, out_u, out_v,
        )
    )


def solution(mesh):
    tile = P(None, None, "wide", "narrow")
    in_specs = (
        tile,
        tile,
        P(None, "wide", "narrow"),
        P("wide", "narrow"),
        P(),
        P(),
        P(None, None, None, ALL, None),
        P(None, None, ALL, None),
    )
    return jax.shard_map(body, mesh=mesh, in_specs=in_specs, out_specs=(tile, tile), check_vma=False)
```

time: 628 us -> 179 us (0.29)
  the two profiles are of different devices: /device:TPU:1 before, /device:TPU:6 now
where the time goes in v1:
time: 179 us; the launch traced here: 177 us
  starting transfers between devices  75.9 us (42%)
  Pallas kernels  67.6 us (38%)
  blocking collectives  22 us (12%)
  waiting for transfers between devices  5.38 us (3%)
  local copies, waits for them, and re-layouts  4.94 us (3%)
    ppermute x3, starting transfers between devices, halo(): bottom = lax.ppermute(first, 'wide', down)  27 us
    all_to_all x1, blocking collectives, exchange(): return lax.all_to_all(x, axis, split_axis=0, concat_axis=0, tiled=True)  22 us
    pallas_call x5, Pallas kernels, call(): pl.pallas_call(body, grid=(1,), in_specs=[SMEM] * smem + [full(x.shape) f...  16.3 us
    pallas_call x1, Pallas kernels, body(): pl.pallas_call(step_one_kernel, grid=(16,), in_specs=[SMEM, SMEM, near(16...  14.6 us
    all_to_all x3, starting transfers between devices, exchange(): return lax.all_to_all(x, axis, split_axis=0, concat_axis=0, tiled=True)  14 us
    pallas_call x1, Pallas kernels, body(): pl.pallas_call(step_two_kernel, grid=(14,), in_specs=[SMEM, SMEM, near(16...  12.3 us
    ppermute x3, starting transfers between devices, halo(): from_right = lax.ppermute(left, 'narrow', down)  10.3 us
    pallas_call x1, Pallas kernels, body(): pl.pallas_call(edges_kernel, grid=(16,), in_specs=[plane_block, full((8,...  9.71 us
  transfers between devices with their start and end apart: 17, of which 2 were waited for; matrix products, arithmetic and copies ran while one was open for 0% of the time, Pallas kernels for 25%

profile of v1, /device:TPU:6, one launch (start us, length us, event | category | flops | bytes accessed | tf_op | source)
XLA Modules:
  0.0 177.5 jit_solution(4647109274979961771)
XLA Ops:
  0.6 9.7 %edges.1 = (f32[48,256]{1,0:T(8,128)}, f32[48,256]{1,0:T(8,128)}, f32[64,128]{1,0:T(8,128)}, f32[64,128]{1,0:T(8,128)}, f32[64,256]{1,0:T(8,128)}) custom-call(f32[3,16,64,256]{3,2,1,0:T(8,128)} %u_ref.5, s32[8,32]{1,0:T(8,128)} %flags_ref.1), custom_call_target="tpu_custom_call" | custom-call | bytes 3300000 | tf_op jit(solution)/shard_map/edges/pallas_call | solution.py:618
  10.3 3.8 %collective-permute-start = (f32[48,256]{1,0:T(8,128)}, f32[48,256]{1,0:T(8,128)S(1)}, u32[]{:S(2)}, u32[]{:S(2)}) collective-permute-start(f32[48,256]{1,0:T(8,128)} %get-tuple-element.23), channel_id=1, source_target_pairs={{0,4},{4,8},{8,12},{12,16},{16,20},{20,24},{24,28},{28,32},{32,36}... | collective-permute-start | bytes 147464 | tf_op jit(solution)/shard_map/ppermute | solution.py:596
  14.2 7.7 %collective-permute-start.1 = (f32[48,256]{1,0:T(8,128)}, f32[48,256]{1,0:T(8,128)S(1)}, u32[]{:S(2)}, u32[]{:S(2)}) collective-permute-start(f32[48,256]{1,0:T(8,128)} %get-tuple-element.24), channel_id=1, source_target_pairs={{4,0},{8,4},{12,8},{16,12},{20,16},{24,20},{28,24},{32,28},{36,32}... | collective-permute-start | bytes 147464 | tf_op jit(solution)/shard_map/ppermute | solution.py:597
  21.9 1.9 %collective-permute-start.2 = (f32[64,128]{1,0:T(8,128)}, f32[64,128]{1,0:T(8,128)S(1)}, u32[]{:S(2)}, u32[]{:S(2)}) collective-permute-start(f32[64,128]{1,0:T(8,128)} %get-tuple-element.25), channel_id=1, source_target_pairs={{0,1},{1,2},{2,3},{4,5},{5,6},{6,7},{8,9},{9,10},{10,11},{12,13},{... | collective-permute-start | bytes 98312 | tf_op jit(solution)/shard_map/ppermute | solution.py:600
  23.8 3.6 %collective-permute-start.3 = (f32[64,128]{1,0:T(8,128)}, f32[64,128]{1,0:T(8,128)S(1)}, u32[]{:S(2)}, u32[]{:S(2)}) collective-permute-start(f32[64,128]{1,0:T(8,128)} %get-tuple-element.26), channel_id=1, source_target_pairs={{1,0},{2,1},{3,2},{5,4},{6,5},{7,6},{9,8},{10,9},{11,10},{13,12},{... | collective-permute-start | bytes 98312 | tf_op jit(solution)/shard_map/ppermute | solution.py:601
  27.5 0.0 collective-permute-done.2.left_ref
  27.5 0.0 copy-start.9
  27.5 1.9 %collective-permute-done.3.right_ref = f32[64,128]{1,0:T(8,128)S(1)} collective-permute-done((f32[64,128]{1,0:T(8,128)}, f32[64,128]{1,0:T(8,128)S(1)}, u32[]{:S(2)}, u32[]{:S(2)}) %collective-permute-start.3) | collective-permute-done | bytes 32800 | tf_op jit(solution)/shard_map/ppermute | solution.py:601
  29.4 0.0 collective-permute-done.top_ref
  29.4 0.0 collective-permute-done.1.bottom_ref
  29.4 0.0 copy-start.5
  29.4 0.0 copy-done.9
  29.4 0.6 copy-done.10
  30.0 0.0 copy-done.4
  30.0 0.0 copy-done.5
  30.0 2.1 %slip.1 = f32[4,192,128]{2,1,0:T(8,128)} custom-call(f32[4]{0:T(128)} %shear_ref.7, f32[4]{0:T(128)} %yields_ref.7, f32[3,16,64,256]{3,2,1,0:T(8,128)} %u_ref.5, f32[3,16,64,256]{3,2,1,0:T(8,128)} %v_ref.3, s32[16,64,256]{2,1,0:T(8,128)} %region_ref.7, f32[64,256]{1,0:T(8,128)} %get-tuple-element.22.plastic_ref, f32[48,256]{1,0:T(8,128)} %copy-done.4, ...), custom_call_target="tpu_custom_call" | custom-call | bytes 1500000 | tf_op jit(solution)/shard_map/slip/pallas_call | solution.py:653
  32.2 3.4 %all-to-all-start = ((f32[4,192,128]{2,1,0:T(8,128)}), f32[4,192,128]{2,1,0:T(8,128)S(1)}, u32[]{:S(2)}, u32[]{:S(2)}) async-start(f32[4,192,128]{2,1,0:T(8,128)} %slip.1), calls=%async_computation | async-start | bytes 786432 | tf_op jit(solution)/shard_map/all_to_all | solution.py:606
  35.6 0.7 add_convert_fusion.where_ref
  36.3 9.6 %history.1 = (f32[72,2048]{1,0:T(8,128)}, f32[72,2048]{1,0:T(8,128)}, f32[18,2048]{1,0:T(8,128)}) custom-call(s32[2]{0:T(128)} %add_convert_fusion.where_ref, bf16[33,3,8,2048]{3,2,1,0:T(8,128)(2,1)} %kernel_ref.1, bf16[32,2,3,8,2048]{4,3,2,1,0:T(8,128)(2,1)} %history_ref.1), custom_call_target="tpu_custom_call" | custom-call | bytes 11000000 | tf_op jit(solution)/shard_map/history/pallas_call | solution.py:630
  45.9 2.6 %collective-permute-start.8 = (f32[72,2048]{1,0:T(8,128)}, f32[72,2048]{1,0:T(8,128)S(1)}, u32[]{:S(2)}, u32[]{:S(2)}) collective-permute-start(f32[72,2048]{1,0:T(8,128)} %get-tuple-element.34), channel_id=1, source_target_pairs={{0,127},{1,126},{2,125},{3,124},{4,123},{5,122},{6,121},{7,120},{8... | collective-permute-start | bytes 1769480 | tf_op jit(solution)/shard_map/ppermute | solution.py:647
  48.5 0.0 all-to-all-done.recv_ref
  48.5 0.7 copy-done.2
  49.2 3.2 %dip.1 = f32[768,128]{1,0:T(8,128)} custom-call(bf16[2,512,256]{2,1,0:T(8,128)(2,1)} %constant.37.clone.radix_ref, f32[2,2,128,128]{3,2,1,0:T(8,128)} %constant.38.clone.turn_ref, bf16[2,2,136,256]{3,2,1,0:T(8,128)(2,1)} %constant.39.clone.out_table_ref, f32[4,192,128]{2,1,0:T(8,128)} %copy-done.2), custom_call_target="tpu_custom_call" | custom-call | bytes 2654208 | tf_op jit(solution)/shard_map/dip/pallas_call | solution.py:581
  52.4 6.8 %all-to-all-start.1 = ((f32[128,1,768]{2,1,0:T(1,128)}), f32[128,1,768]{2,1,0:T(1,128)S(1)}, u32[]{:S(2)}, u32[]{:S(2)}) async-start(f32[128,1,768]{2,1,0:T(1,128)} %bitcast.7), calls=%async_computation.1 | async-start | bytes 786432 | tf_op jit(solution)/shard_map/all_to_all | solution.py:606
  59.2 8.5 %collective-permute-start.9 = (f32[18,2048]{1,0:T(8,128)}, f32[18,2048]{1,0:T(8,128)S(1)}, u32[]{:S(2)}, u32[]{:S(2)}) collective-permute-start(f32[18,2048]{1,0:T(8,128)} %get-tuple-element.35), channel_id=1, source_target_pairs={{64,0},{65,63},{66,62},{67,61},{68,60},{69,59},{70,58},{71,57},{72... | collective-permute-start | bytes 442376 | tf_op jit(solution)/shard_map/ppermute | solution.py:648
  67.7 3.5 %collective-permute-done.9.edge_ref = f32[18,2048]{1,0:T(8,128)S(1)} collective-permute-done((f32[18,2048]{1,0:T(8,128)}, f32[18,2048]{1,0:T(8,128)S(1)}, u32[]{:S(2)}, u32[]{:S(2)}) %collective-permute-start.9) | collective-permute-done | bytes 147488 | tf_op jit(solution)/shard_map/ppermute | solution.py:648
  71.2 0.0 collective-permute-done.8.main_ref
  71.2 0.7 copy-done.6
  71.8 0.2 copy-done.3
  72.1 3.6 %mirror.1.coef_ref = f32[8,3,8,2048]{3,2,1,0:T(8,128)} custom-call(s32[2]{0:T(128)} %add_convert_fusion.where_ref, bf16[128,128]{1,0:T(8,128)(2,1)} %constant.40.clone.reverse_ref, f32[72,2048]{1,0:T(8,128)} %get-tuple-element.33.own_ref, f32[72,2048]{1,0:T(8,128)} %copy-done.3, f32[18,2048]{1,0:T(8,128)} %copy-done.6), custom_call_target="tpu_custom_call" | custom-call | bytes 2965512 | tf_op jit(solution)/shard_map/mirror/pallas_call | solution.py:581
  75.6 0.0 all-to-all-done.1
  75.6 0.7 copy-done.1
  76.4 4.6 %strike.1 = f32[768,128]{1,0:T(8,128)} custom-call(bf16[2,256,256]{2,1,0:T(8,128)(2,1)} %constant.41.clone.in_ref.out_table_ref, f32[2,128,128]{2,1,0:T(8,128)} %constant.42.clone.turn_ref, bf16[2,256,256]{2,1,0:T(8,128)(2,1)} %constant.43.clone.mix_ref, bf16[128,128]{1,0:T(8,128)(2,1)} %constant.40.clone.reverse_ref, ...), custom_call_target="tpu_custom_call" | custom-call | bytes 4653056 | tf_op jit(solution)/shard_map/strike/pallas_call | solution.py:581
  81.0 22.0 %all_to_all.20 = f32[128,1,768]{2,1,0:T(1,128)} all-to-all(f32[128,1,768]{2,1,0:T(1,128)} %bitcast.8), channel_id=1, replica_groups=mesh['wide'=32,'narrow'=4] {'wide','narrow'}, dimensions={0} | all-to-all | bytes 786432 | tf_op jit(solution)/shard_map/all_to_all | solution.py:606
  103.0 3.2 %undip.1 = f32[4,192,128]{2,1,0:T(8,128)} custom-call(bf16[2,256,512]{2,1,0:T(8,128)(2,1)} %constant.45.clone.in_ref, f32[2,2,128,128]{3,2,1,0:T(8,128)} %constant.46.clone.turn_ref, bf16[2,256,512]{2,1,0:T(8,128)(2,1)} %constant.47.clone.unradix_ref, f32[768,128]{1,0:T(8,128)} %bitcast.9), custom_call_target="tpu_custom_call" | custom-call | bytes 3145728 | tf_op jit(solution)/shard_map/undip/pallas_call | solution.py:581
  106.2 3.8 %all-to-all-start.3 = ((f32[4,192,128]{2,1,0:T(8,128)}), f32[4,192,128]{2,1,0:T(8,128)S(1)}, u32[]{:S(2)}, u32[]{:S(2)}) async-start(f32[4,192,128]{2,1,0:T(8,128)} %undip.1), calls=%async_computation.3 | async-start | bytes 786432 | tf_op jit(solution)/shard_map/all_to_all | solution.py:606
  110.0 14.6 %step_one.1 = (f32[3,16,64,256]{3,2,1,0:T(8,128)}, f32[3,16,64,256]{3,2,1,0:T(8,128)}, f32[48,256]{1,0:T(8,128)}, f32[48,256]{1,0:T(8,128)}, f32[64,128]{1,0:T(8,128)}, /*index=5*/f32[64,128]{1,0:T(8,128)}) custom-call(f32[4]{0:T(128)} %shear_ref.7, f32[4]{0:T(128)} %yields_ref.7, f32[3,16,64,256]{3,2,1,0:T(8,128)} %u_ref.5, f32[3,16,64,256]{3,2,1,0:T(8,128)} %v_ref.3, ...), custom_call_target="tpu_custom_call" | custom-call | bytes 14000000 | tf_op jit(solution)/shard_map/step_one/pallas_call | solution.py:670
  124.6 2.0 %collective-permute-start.6 = (f32[64,128]{1,0:T(8,128)}, f32[64,128]{1,0:T(8,128)S(1)}, u32[]{:S(2)}, u32[]{:S(2)}) collective-permute-start(f32[64,128]{1,0:T(8,128)} %get-tuple-element.31), channel_id=1, source_target_pairs={{0,1},{1,2},{2,3},{4,5},{5,6},{6,7},{8,9},{9,10},{10,11},{12,13},{... | collective-permute-start | bytes 98312 | tf_op jit(solution)/shard_map/ppermute | solution.py:600
  126.7 1.9 %collective-permute-start.4 = (f32[48,256]{1,0:T(8,128)}, f32[48,256]{1,0:T(8,128)S(1)}, u32[]{:S(2)}, u32[]{:S(2)}) collective-permute-start(f32[48,256]{1,0:T(8,128)} %get-tuple-element.29), channel_id=1, source_target_pairs={{0,4},{4,8},{8,12},{12,16},{16,20},{20,24},{24,28},{28,32},{32,36}... | collective-permute-start | bytes 147464 | tf_op jit(solution)/shard_map/ppermute | solution.py:596
  128.6 9.6 %collective-permute-start.5 = (f32[48,256]{1,0:T(8,128)}, f32[48,256]{1,0:T(8,128)S(1)}, u32[]{:S(2)}, u32[]{:S(2)}) collective-permute-start(f32[48,256]{1,0:T(8,128)} %get-tuple-element.30), channel_id=1, source_target_pairs={{4,0},{8,4},{12,8},{16,12},{20,16},{24,20},{28,24},{32,28},{36,32}... | collective-permute-start | bytes 147464 | tf_op jit(solution)/shard_map/ppermute | solution.py:597
  138.2 3.0 %collective-permute-start.7 = (f32[64,128]{1,0:T(8,128)}, f32[64,128]{1,0:T(8,128)S(1)}, u32[]{:S(2)}, u32[]{:S(2)}) collective-permute-start(f32[64,128]{1,0:T(8,128)} %get-tuple-element.32), channel_id=1, source_target_pairs={{1,0},{2,1},{3,2},{5,4},{6,5},{7,6},{9,8},{10,9},{11,10},{13,12},{... | collective-permute-start | bytes 98312 | tf_op jit(solution)/shard_map/ppermute | solution.py:601
  141.2 0.0 all-to-all-done.3.recv_ref
  141.2 0.8 copy-done
  142.0 1.7 traction_edges.1
  143.7 1.9 %collective-permute-start.12 = (f32[64,128]{1,0:T(8,128)}, f32[64,128]{1,0:T(8,128)S(1)}, u32[]{:S(2)}, u32[]{:S(2)}) collective-permute-start(f32[64,128]{1,0:T(8,128)} %get-tuple-element.38), channel_id=1, source_target_pairs={{0,1},{1,2},{2,3},{4,5},{5,6},{6,7},{8,9},{9,10},{10,11},{12,13},{... | collective-permute-start | bytes 98312 | tf_op jit(solution)/shard_map/ppermute | solution.py:600
  145.6 0.0 collective-permute-done.6.left_ref
  145.6 3.6 %collective-permute-start.13 = (f32[64,128]{1,0:T(8,128)}, f32[64,128]{1,0:T(8,128)S(1)}, u32[]{:S(2)}, u32[]{:S(2)}) collective-permute-start(f32[64,128]{1,0:T(8,128)} %get-tuple-element.39), channel_id=1, source_target_pairs={{1,0},{2,1},{3,2},{5,4},{6,5},{7,6},{9,8},{10,9},{11,10},{13,12},{... | collective-permute-start | bytes 98312 | tf_op jit(solution)/shard_map/ppermute | solution.py:601
  149.3 0.0 collective-permute-done.7.right_ref
  149.3 1.9 %collective-permute-start.10 = (f32[8,256]{1,0:T(8,128)}, f32[8,256]{1,0:T(8,128)S(1)}, u32[]{:S(2)}, u32[]{:S(2)}) collective-permute-start(f32[8,256]{1,0:T(8,128)} %get-tuple-element.36), channel_id=1, source_target_pairs={{0,4},{4,8},{8,12},{12,16},{16,20},{20,24},{24,28},{28,32},{32,36}... | collective-permute-start | bytes 24584 | tf_op jit(solution)/shard_map/ppermute | solution.py:596
  151.2 0.0 collective-permute-done.4.top_ref
  151.3 9.6 %collective-permute-start.11 = (f32[8,256]{1,0:T(8,128)}, f32[8,256]{1,0:T(8,128)S(1)}, u32[]{:S(2)}, u32[]{:S(2)}) collective-permute-start(f32[8,256]{1,0:T(8,128)} %get-tuple-element.37), channel_id=1, source_target_pairs={{4,0},{8,4},{12,8},{16,12},{20,16},{24,20},{28,24},{32,28},{36,32}... | collective-permute-start | bytes 24584 | tf_op jit(solution)/shard_map/ppermute | solution.py:597
  160.9 0.0 collective-permute-done.5.bottom_ref
  160.9 0.0 copy-start.8
  161.0 0.6 copy-done.8
  161.5 12.3 %step_two.1 = (f32[3,16,64,256]{3,2,1,0:T(8,128)}, f32[3,16,64,256]{3,2,1,0:T(8,128)}) custom-call(f32[4]{0:T(128)} %shear_ref.7, f32[4]{0:T(128)} %yields_ref.7, f32[3,16,64,256]{3,2,1,0:T(8,128)} %get-tuple-element.27.u_ref, f32[3,16,64,256]{3,2,1,0:T(8,128)} %get-tuple-element.28.v_ref, s32[16,64,256]{2,1,0:T(8,128)} %region_ref.7, ...), custom_call_target="tpu_custom_call" | custom-call | bytes 14000000 | tf_op jit(solution)/shard_map/step_two/pallas_call | solution.py:706
  173.9 0.0 collective-permute-done.10.ttop_ref
  173.9 0.0 collective-permute-done.11.tbottom_ref
  173.9 0.0 collective-permute-done.12.tleft_ref
  173.9 0.0 collective-permute-done.13.tright_ref
  173.9 0.5 copy-done.15
  174.5 0.0 copy-done.16
  174.5 0.0 copy-done.13
  174.5 0.0 copy-done.14
  174.5 2.9 %last.1 = (f32[3,16,64,256]{3,2,1,0:T(8,128)}, f32[3,16,64,256]{3,2,1,0:T(8,128)}) custom-call(f32[4]{0:T(128)} %shear_ref.7, f32[4]{0:T(128)} %yields_ref.7, f32[3,16,64,256]{3,2,1,0:T(8,128)} %get-tuple-element.27.u_ref, f32[3,16,64,256]{3,2,1,0:T(8,128)} %get-tuple-element.28.v_ref, ...), custom_call_target="tpu_custom_call", output_to_operand_aliasing={{0}: (15, {}), {1}: (16, {})} | custom-call | bytes 4000000 | tf_op jit(solution)/shard_map/last/pallas_call | solution.py:736
  (17 shorter events, 0.0 us)
Async XLA Ops:
  10.3 19.0 %collective-permute-start = (f32[48,256]{1,0:T(8,128)}, f32[48,256]{1,0:T(8,128)S(1)}, u32[]{:S(2)}, u32[]{:S(2)}) collective-permute-start(f32[48,256]{1,0:T(8,128)} %get-tuple-element.23), channel_id=1, source_target_pairs={{0,4},{4,8},{8,12},{12,16},{16,20},{20,24},{24,28},{28,32},{32,36}... | collective-permute-start | bytes 147464 | tf_op jit(solution)/shard_map/ppermute | solution.py:596
  14.2 15.2 %collective-permute-start.1 = (f32[48,256]{1,0:T(8,128)}, f32[48,256]{1,0:T(8,128)S(1)}, u32[]{:S(2)}, u32[]{:S(2)}) collective-permute-start(f32[48,256]{1,0:T(8,128)} %get-tuple-element.24), channel_id=1, source_target_pairs={{4,0},{8,4},{12,8},{16,12},{20,16},{24,20},{28,24},{32,28},{36,32}... | collective-permute-start | bytes 147464 | tf_op jit(solution)/shard_map/ppermute | solution.py:597
  21.9 5.6 %collective-permute-start.2 = (f32[64,128]{1,0:T(8,128)}, f32[64,128]{1,0:T(8,128)S(1)}, u32[]{:S(2)}, u32[]{:S(2)}) collective-permute-start(f32[64,128]{1,0:T(8,128)} %get-tuple-element.25), channel_id=1, source_target_pairs={{0,1},{1,2},{2,3},{4,5},{5,6},{6,7},{8,9},{9,10},{10,11},{12,13},{... | collective-permute-start | bytes 98312 | tf_op jit(solution)/shard_map/ppermute | solution.py:600
  23.8 5.5 %collective-permute-start.3 = (f32[64,128]{1,0:T(8,128)}, f32[64,128]{1,0:T(8,128)S(1)}, u32[]{:S(2)}, u32[]{:S(2)}) collective-permute-start(f32[64,128]{1,0:T(8,128)} %get-tuple-element.26), channel_id=1, source_target_pairs={{1,0},{2,1},{3,2},{5,4},{6,5},{7,6},{9,8},{10,9},{11,10},{13,12},{... | collective-permute-start | bytes 98312 | tf_op jit(solution)/shard_map/ppermute | solution.py:601
  27.5 1.9 %copy-start.9 = (f32[64,128]{1,0:T(8,128)}, f32[64,128]{1,0:T(8,128)S(1)}, u32[]{:S(2)}) copy-start(f32[64,128]{1,0:T(8,128)S(1)} %collective-permute-done.2.left_ref) | copy-start | bytes 98308
  29.4 0.6 copy-start.10
  29.4 0.6 copy-start.4
  29.4 0.6 copy-start.5
  32.2 16.3 %all-to-all-start = ((f32[4,192,128]{2,1,0:T(8,128)}), f32[4,192,128]{2,1,0:T(8,128)S(1)}, u32[]{:S(2)}, u32[]{:S(2)}) async-start(f32[4,192,128]{2,1,0:T(8,128)} %slip.1), calls=%async_computation | async-start | bytes 786432 | tf_op jit(solution)/shard_map/all_to_all | solution.py:606
  45.9 25.3 %collective-permute-start.8 = (f32[72,2048]{1,0:T(8,128)}, f32[72,2048]{1,0:T(8,128)S(1)}, u32[]{:S(2)}, u32[]{:S(2)}) collective-permute-start(f32[72,2048]{1,0:T(8,128)} %get-tuple-element.34), channel_id=1, source_target_pairs={{0,127},{1,126},{2,125},{3,124},{4,123},{5,122},{6,121},{7,120},{8... | collective-permute-start | bytes 1769480 | tf_op jit(solution)/shard_map/ppermute | solution.py:647
  48.5 0.7 copy-start.2
  52.4 23.2 %all-to-all-start.1 = ((f32[128,1,768]{2,1,0:T(1,128)}), f32[128,1,768]{2,1,0:T(1,128)S(1)}, u32[]{:S(2)}, u32[]{:S(2)}) async-start(f32[128,1,768]{2,1,0:T(1,128)} %bitcast.7), calls=%async_computation.1 | async-start | bytes 786432 | tf_op jit(solution)/shard_map/all_to_all | solution.py:606
  59.2 12.0 %collective-permute-start.9 = (f32[18,2048]{1,0:T(8,128)}, f32[18,2048]{1,0:T(8,128)S(1)}, u32[]{:S(2)}, u32[]{:S(2)}) collective-permute-start(f32[18,2048]{1,0:T(8,128)} %get-tuple-element.35), channel_id=1, source_target_pairs={{64,0},{65,63},{66,62},{67,61},{68,60},{69,59},{70,58},{71,57},{72... | collective-permute-start | bytes 442376 | tf_op jit(solution)/shard_map/ppermute | solution.py:648
  71.2 0.7 copy-start.6
  71.2 0.9 copy-start.3
  75.6 0.7 copy-start.1
  106.2 35.0 %all-to-all-start.3 = ((f32[4,192,128]{2,1,0:T(8,128)}), f32[4,192,128]{2,1,0:T(8,128)S(1)}, u32[]{:S(2)}, u32[]{:S(2)}) async-start(f32[4,192,128]{2,1,0:T(8,128)} %undip.1), calls=%async_computation.3 | async-start | bytes 786432 | tf_op jit(solution)/shard_map/all_to_all | solution.py:606
  124.6 21.0 %collective-permute-start.6 = (f32[64,128]{1,0:T(8,128)}, f32[64,128]{1,0:T(8,128)S(1)}, u32[]{:S(2)}, u32[]{:S(2)}) collective-permute-start(f32[64,128]{1,0:T(8,128)} %get-tuple-element.31), channel_id=1, source_target_pairs={{0,1},{1,2},{2,3},{4,5},{5,6},{6,7},{8,9},{9,10},{10,11},{12,13},{... | collective-permute-start | bytes 98312 | tf_op jit(solution)/shard_map/ppermute | solution.py:600
  126.7 24.6 %collective-permute-start.4 = (f32[48,256]{1,0:T(8,128)}, f32[48,256]{1,0:T(8,128)S(1)}, u32[]{:S(2)}, u32[]{:S(2)}) collective-permute-start(f32[48,256]{1,0:T(8,128)} %get-tuple-element.29), channel_id=1, source_target_pairs={{0,4},{4,8},{8,12},{12,16},{16,20},{20,24},{24,28},{28,32},{32,36}... | collective-permute-start | bytes 147464 | tf_op jit(solution)/shard_map/ppermute | solution.py:596
  128.6 32.3 %collective-permute-start.5 = (f32[48,256]{1,0:T(8,128)}, f32[48,256]{1,0:T(8,128)S(1)}, u32[]{:S(2)}, u32[]{:S(2)}) collective-permute-start(f32[48,256]{1,0:T(8,128)} %get-tuple-element.30), channel_id=1, source_target_pairs={{4,0},{8,4},{12,8},{16,12},{20,16},{24,20},{28,24},{32,28},{36,32}... | collective-permute-start | bytes 147464 | tf_op jit(solution)/shard_map/ppermute | solution.py:597
  138.2 11.1 %collective-permute-start.7 = (f32[64,128]{1,0:T(8,128)}, f32[64,128]{1,0:T(8,128)S(1)}, u32[]{:S(2)}, u32[]{:S(2)}) collective-permute-start(f32[64,128]{1,0:T(8,128)} %get-tuple-element.32), channel_id=1, source_target_pairs={{1,0},{2,1},{3,2},{5,4},{6,5},{7,6},{9,8},{10,9},{11,10},{13,12},{... | collective-permute-start | bytes 98312 | tf_op jit(solution)/shard_map/ppermute | solution.py:601
  141.2 0.8 copy-start
  143.7 30.2 %collective-permute-start.12 = (f32[64,128]{1,0:T(8,128)}, f32[64,128]{1,0:T(8,128)S(1)}, u32[]{:S(2)}, u32[]{:S(2)}) collective-permute-start(f32[64,128]{1,0:T(8,128)} %get-tuple-element.38), channel_id=1, source_target_pairs={{0,1},{1,2},{2,3},{4,5},{5,6},{6,7},{8,9},{9,10},{10,11},{12,13},{... | collective-permute-start | bytes 98312 | tf_op jit(solution)/shard_map/ppermute | solution.py:600
  145.6 15.3 %copy-start.11 = (f32[64,128]{1,0:T(8,128)}, f32[64,128]{1,0:T(8,128)S(1)}, u32[]{:S(2)}) copy-start(f32[64,128]{1,0:T(8,128)S(1)} %collective-permute-done.6.left_ref) | copy-start | bytes 98308
  145.6 28.3 %collective-permute-start.13 = (f32[64,128]{1,0:T(8,128)}, f32[64,128]{1,0:T(8,128)S(1)}, u32[]{:S(2)}, u32[]{:S(2)}) collective-permute-start(f32[64,128]{1,0:T(8,128)} %get-tuple-element.39), channel_id=1, source_target_pairs={{1,0},{2,1},{3,2},{5,4},{6,5},{7,6},{9,8},{10,9},{11,10},{13,12},{... | collective-permute-start | bytes 98312 | tf_op jit(solution)/shard_map/ppermute | solution.py:601
  149.3 11.6 %copy-start.12 = (f32[64,128]{1,0:T(8,128)}, f32[64,128]{1,0:T(8,128)S(1)}, u32[]{:S(2)}) copy-start(f32[64,128]{1,0:T(8,128)S(1)} %collective-permute-done.7.right_ref) | copy-start | bytes 98308
  149.3 24.6 %collective-permute-start.10 = (f32[8,256]{1,0:T(8,128)}, f32[8,256]{1,0:T(8,128)S(1)}, u32[]{:S(2)}, u32[]{:S(2)}) collective-permute-start(f32[8,256]{1,0:T(8,128)} %get-tuple-element.36), channel_id=1, source_target_pairs={{0,4},{4,8},{8,12},{12,16},{16,20},{20,24},{24,28},{28,32},{32,36}... | collective-permute-start | bytes 24584 | tf_op jit(solution)/shard_map/ppermute | solution.py:596
  151.2 9.7 %copy-start.7 = (f32[48,256]{1,0:T(8,128)}, f32[48,256]{1,0:T(8,128)S(1)}, u32[]{:S(2)}) copy-start(f32[48,256]{1,0:T(8,128)S(1)} %collective-permute-done.4.top_ref) | copy-start | bytes 147460
  151.3 22.6 %collective-permute-start.11 = (f32[8,256]{1,0:T(8,128)}, f32[8,256]{1,0:T(8,128)S(1)}, u32[]{:S(2)}, u32[]{:S(2)}) collective-permute-start(f32[8,256]{1,0:T(8,128)} %get-tuple-element.37), channel_id=1, source_target_pairs={{4,0},{8,4},{12,8},{16,12},{20,16},{24,20},{28,24},{32,28},{36,32}... | collective-permute-start | bytes 24584 | tf_op jit(solution)/shard_map/ppermute | solution.py:597
  160.9 0.6 copy-start.8
  173.9 0.6 copy-start.15
  173.9 0.6 copy-start.16
  173.9 0.6 copy-start.13
  173.9 0.6 copy-start.14

commit v2 on v1

v2 whole, which is shorter than its diff:
```python
import functools
import math

import jax
import jax.numpy as jnp
import ml_dtypes
import numpy as np
from jax import lax
from jax.experimental import pallas as pl
from jax.experimental.pallas import tpu as pltpu
from jax.sharding import PartitionSpec as P

DT = 0.1
DAMPING = 0.5
ALL = ("wide", "narrow")
PLANES = 2
F32 = jnp.float32
BF16 = jnp.bfloat16


def split_table(table):
    table = np.asarray(table, np.float64)
    high = table.astype(ml_dtypes.bfloat16)
    low = (table - high.astype(np.float64)).astype(ml_dtypes.bfloat16)
    return np.stack([high, low])


def make_tables():
    factor = 1.0 / math.sqrt(2048 * 1024)
    eye2 = np.eye(2)
    eye4 = np.eye(4)
    eye8 = np.eye(8)
    eye16 = np.eye(16)
    r8 = np.arange(8).reshape(2, 4)
    y1 = np.arange(8).reshape(4, 2)
    theta = 2 * np.pi * r8[:, :, None, None] * y1[None, None] / 8
    radix = np.stack([np.cos(theta), -np.sin(theta)])
    radix = np.einsum("isrnl,xz,fg->isxfrnglz", radix, eye16, eye2).reshape(512, 256)
    unradix = np.stack([np.cos(theta), -np.sin(theta)])
    unradix = np.einsum("isrnl,xz,fg->nglzisxfr", unradix, eye16, eye2).reshape(256, 512)
    y0 = np.arange(128)
    theta = 2 * np.pi * r8[:, :, None] * y0 / 1024
    turn = np.stack([np.cos(theta), -np.sin(theta)])[:, :, None, None]
    dip_turn = np.broadcast_to(turn, (2, 2, 16, 2, 4, 128)).reshape(2, 2, 128, 128) * factor
    alt = (-1.0) ** y0
    place = np.stack([np.arange(64), 63 - np.arange(64)])
    theta = 2 * np.pi * place[:, :, None] * y0 / 128
    cos, sin = np.cos(theta), np.sin(theta)
    dip_out = np.zeros((2, 136, 256))
    dip_out[:, :64] = np.concatenate([cos, sin], -1)
    dip_out[:, 64:128] = np.concatenate([-sin, cos], -1)
    dip_out[0, 128, :128] = alt
    dip_in = np.zeros((2, 128, 2, 2, 128))
    for s in range(2):
        rows = slice(s * 64, s * 64 + 64)
        dip_in[0, rows, s, 0] = cos[s]
        dip_in[0, rows, s, 1] = sin[s]
        dip_in[1, rows, s, 0] = -sin[s]
        dip_in[1, rows, s, 1] = cos[s]
    dip_in = dip_in.reshape(256, 512)
    theta = 2 * np.pi * np.outer(y0, y0) / 128
    cos, sin = np.cos(theta), np.sin(theta)
    strike_in = np.block([[cos, -sin], [sin, cos]])
    strike_out = np.block([[cos, -sin], [sin, cos]])
    a = np.arange(16)
    theta = 2 * np.pi * np.outer(a, y0) / 2048
    turn = np.stack([np.cos(theta), -np.sin(theta)])
    strike_turn = np.broadcast_to(turn[:, :, None], (2, 16, 8, 128)).reshape(2, 128, 128)
    theta = 2 * np.pi * np.outer(a, a) / 16
    cos, sin = np.kron(np.cos(theta), eye8), np.kron(np.sin(theta), eye8)
    strike_mix = np.block([[cos, sin], [-sin, cos]])
    strike_unmix = np.block([[cos, -sin], [sin, cos]]) * factor
    reverse = np.zeros((128, 128))
    reverse[(128 - y0) % 128, y0] = 1.0
    return {
        "radix": split_table(radix),
        "unradix": split_table(unradix),
        "dip_turn": dip_turn.astype(np.float32),
        "undip_turn": (dip_turn / factor * 2.0).astype(np.float32),
        "dip_out": split_table(dip_out),
        "dip_in": split_table(dip_in),
        "strike_in": split_table(strike_in),
        "strike_out": split_table(strike_out),
        "strike_turn": strike_turn.astype(np.float32),
        "strike_mix": split_table(strike_mix),
        "strike_unmix": split_table(strike_unmix),
        "reverse": reverse.astype(ml_dtypes.bfloat16),
    }


TABLES = make_tables()


def halves(x):
    high = x.astype(BF16)
    return high, (x - high.astype(F32)).astype(BF16)


def dot(a, b, contract=(1, 0)):
    return lax.dot_general(
        a, b, (((contract[0],), (contract[1],)), ((), ())), preferred_element_type=F32
    )


def left_dot(table, x, contract=(1, 0)):
    high, low = halves(x)
    return dot(table[0], high, contract) + (
        dot(table[1], high, contract) + dot(table[0], low, contract)
    )


def right_dot(x, table):
    high, low = halves(x)
    return dot(high, table[0]) + (dot(low, table[0]) + dot(high, table[1]))


def lanes(shape):
    return lax.broadcasted_iota(jnp.int32, shape, len(shape) - 1)


def rows_of(shape):
    return lax.broadcasted_iota(jnp.int32, shape, len(shape) - 2)


def neighbour_sum(center, above, below, before, after, left, right):
    rows = rows_of(center.shape)
    north = jnp.where(rows == 0, before, pltpu.roll(center, 1, 0))
    south = jnp.where(rows == 7, after, pltpu.roll(center, 7, 0))
    c0, c1 = center[:, :128], center[:, 128:]
    lane = lanes(c0.shape)
    w0, w1 = pltpu.roll(c0, 1, 1), pltpu.roll(c1, 1, 1)
    e0, e1 = pltpu.roll(c0, 127, 1), pltpu.roll(c1, 127, 1)
    west = jnp.concatenate([jnp.where(lane == 0, left, w0), jnp.where(lane == 0, w0, w1)], 1)
    east = jnp.concatenate([jnp.where(lane == 127, e1, e0), jnp.where(lane == 127, right, e1)], 1)
    total = (north + south) + (west + east)
    for other in (above, below):
        if other is not None:
            total = total + other
    return total


def strip_force(centers, sums, region, plastic, shear_ref, yields_ref):
    one = jnp.ones((8, 128), F32)
    wide = lambda x: jnp.concatenate([x, x], 1)
    modulus = wide(one * shear_ref[0])
    level = one * yields_ref[0]
    level = wide(1.0 / (level * level))
    for label in range(1, 4):
        modulus = jnp.where(region == label, shear_ref[label], modulus)
        other = one * yields_ref[label]
        level = jnp.where(region == label, wide(1.0 / (other * other)), level)
    force = [modulus * (total - 6.0 * center) for total, center in zip(sums, centers)]
    squares = force[0] * force[0] + force[1] * force[1] + force[2] * force[2]
    capped = lax.rsqrt(1.0 + squares * level)
    scaling = jnp.where(plastic > 0.5, capped, 1.0)
    return [f * scaling for f in force]


def strip_of(i):
    return slice(i * 8, i * 8 + 8)


def stencil_strip(i, load, beside, load_above, load_below, halo_refs, z):
    top_ref, bottom_ref, left_ref, right_ref = halo_refs
    centers, sums = [], []
    for c in range(3):
        place = slot(c, z)
        center = load(c, strip_of(i))
        if i == 0:
            before = top_ref[pl.ds(place, 1), :]
        else:
            before = load(c, slice(i * 8 - 1, i * 8))
        if i == 7:
            after = bottom_ref[pl.ds(place, 1), :]
        else:
            after = load(c, slice(i * 8 + 8, i * 8 + 9))
        left = pltpu.roll(left_ref[strip_of(i), :], lax.rem(128 - place, 128), 1)
        right = pltpu.roll(right_ref[strip_of(i), :], 127 - place, 1)
        if beside is not None:
            before, after, left, right = beside(c, i, before, after, left, right)
        above = load_above(c, strip_of(i)) if load_above else None
        below = load_below(c, strip_of(i)) if load_below else None
        sums.append(neighbour_sum(center, above, below, before, after, left, right))
        centers.append(center)
    return centers, sums


def slot(c, z):
    return c * 16 + z


def put_columns(left_ref, right_ref, strip, i, place):
    c0, c1 = strip[:, :128], strip[:, 128:]
    lane = lanes(c0.shape)
    rows = strip_of(i)
    left_ref[rows, :] = jnp.where(lane == place, pltpu.roll(c0, place, 1), left_ref[rows, :])
    right_ref[rows, :] = jnp.where(
        lane == place, pltpu.roll(c1, lax.rem(place + 1, 128), 1), right_ref[rows, :]
    )


def edges_kernel(u_ref, flags_ref, first_ref, last_ref, left_ref, right_ref, plastic_ref):
    step = pl.program_id(0)

    @pl.when(step == 0)
    def _():
        left_ref[...] = jnp.zeros_like(left_ref)
        right_ref[...] = jnp.zeros_like(right_ref)
        wide = (rows_of((64, 8)) // 8 == lanes((64, 8))).astype(F32)
        high = (rows_of((32, 256)) == lanes((32, 256)) // 8).astype(F32)
        marks = (flags_ref[...] == 1).astype(F32)
        plastic_ref[...] = dot(dot(wide, marks), high)

    for k in range(u_ref.shape[1]):
        z = step * u_ref.shape[1] + k
        for c in range(3):
            place = slot(c, z)
            first_ref[pl.ds(place, 1), :] = u_ref[c, k, 0:1, :]
            last_ref[pl.ds(place, 1), :] = u_ref[c, k, 63:64, :]
            for i in range(8):
                put_columns(left_ref, right_ref, u_ref[c, k, strip_of(i), :], i, place)


def slip_kernel(
    shear_ref, yields_ref, u_ref, v_ref, region_ref, plastic_ref,
    top_ref, bottom_ref, left_ref, right_ref, _after_ref, send_ref,
):
    halo_refs = (top_ref, bottom_ref, left_ref, right_ref)
    for i in range(8):
        rows = strip_of(i)
        centers, sums = stencil_strip(
            i,
            lambda c, r: u_ref[c, 0, r, :],
            None,
            lambda c, r: u_ref[c, 1, r, :],
            None,
            halo_refs,
            0,
        )
        force = strip_force(
            centers, sums, region_ref[0, rows, :], plastic_ref[rows, :], shear_ref, yields_ref
        )
        n, part = i // 2, (i % 2) * 8
        for c in range(3):
            v = v_ref[c, 0, rows, :]
            v = v + DT * (force[c] - DAMPING * v)
            moved = centers[c] + DT * v
            for f, values in enumerate((centers[c], moved)):
                for half in range(2):
                    start = f * 96 + c * 32 + half * 16 + part
                    send_ref[n, start : start + 8, :] = values[:, half * 128 : half * 128 + 128]


def step_one_kernel(
    shear_ref, yields_ref, u_ref, v_ref, region_ref, plastic_ref,
    top_ref, bottom_ref, left_ref, right_ref, _after_ref,
    new_u_ref, new_v_ref, first_ref, last_ref, left_out_ref, right_out_ref,
):
    step = pl.program_id(0)

    @pl.when(step == 0)
    def _():
        left_out_ref[...] = jnp.zeros_like(left_out_ref)
        right_out_ref[...] = jnp.zeros_like(right_out_ref)

    halo_refs = (top_ref, bottom_ref, left_ref, right_ref)
    for k in range(PLANES):
        z = step * PLANES + k
        damping = jnp.where(z == 0, DAMPING, 0.0).astype(F32)
        lower = jnp.where(z > 0, 1.0, 0.0).astype(F32)
        upper = jnp.where(z < 15, 1.0, 0.0).astype(F32)
        if k < PLANES - 1:
            load_above = lambda c, r: u_ref[c, z + 1, r, :]
        else:
            load_above = lambda c, r: u_ref[c, jnp.minimum(z + 1, 15), r, :] * upper
        if k > 0:
            load_below = lambda c, r: u_ref[c, z - 1, r, :]
        else:
            load_below = lambda c, r: u_ref[c, jnp.maximum(z - 1, 0), r, :] * lower
        for i in range(8):
            rows = strip_of(i)
            centers, sums = stencil_strip(
                i, lambda c, r: u_ref[c, z, r, :], None, load_above, load_below, halo_refs, z
            )
            force = strip_force(
                centers, sums, region_ref[k, rows, :], plastic_ref[rows, :], shear_ref, yields_ref
            )
            for c in range(3):
                v = v_ref[c, k, rows, :]
                v = v + DT * (force[c] - damping * v)
                u = centers[c] + DT * v
                new_v_ref[c, k, rows, :] = v
                new_u_ref[c, k, rows, :] = u
                place = slot(c, z)
                if i == 0:
                    first_ref[pl.ds(place, 1), :] = u[0:1]
                if i == 7:
                    last_ref[pl.ds(place, 1), :] = u[7:8]
                put_columns(left_out_ref, right_out_ref, u, i, place)


def step_two_kernel(start, *refs):
    (shear_ref, yields_ref, u_ref, v_ref, region_ref, plastic_ref) = refs[:6]
    halo_refs = refs[6:10]
    new_u_ref, new_v_ref = refs[-2:]
    for k in range(PLANES):
        z = pl.program_id(0) * PLANES + (start + k)
        upper = jnp.where(z < 15, 1.0, 0.0).astype(F32)
        if k < PLANES - 1:
            load_above = lambda c, r: u_ref[c, z + 1, r, :]
        else:
            load_above = lambda c, r: u_ref[c, jnp.minimum(z + 1, 15), r, :] * upper
        for i in range(8):
            rows = strip_of(i)
            centers, sums = stencil_strip(
                i,
                lambda c, r: u_ref[c, z, r, :],
                None,
                load_above,
                lambda c, r: u_ref[c, z - 1, r, :],
                halo_refs,
                z,
            )
            force = strip_force(
                centers, sums, region_ref[k, rows, :], plastic_ref[rows, :], shear_ref, yields_ref
            )
            for c in range(3):
                v = v_ref[c, k, rows, :] + DT * force[c]
                new_v_ref[c, k, rows, :] = v
                new_u_ref[c, k, rows, :] = centers[c] + DT * v


def last_kernel(
    shear_ref, yields_ref, u_ref, v_ref, region_ref, plastic_ref,
    top_ref, bottom_ref, left_ref, right_ref,
    recv_ref, _old_u_ref, _old_v_ref, new_u_ref, new_v_ref, surface,
):
    square = DT * DT
    halo_refs = (top_ref, bottom_ref, left_ref, right_ref)

    def traction(f, c, i):
        start = f * 96 + c * 32 + (i % 2) * 8
        return jnp.concatenate(
            [recv_ref[i // 2, start + half * 16 : start + half * 16 + 8, :] for half in range(2)], 1
        )

    def outside(n, c, side):
        row = 208 + c * 2 + side
        return jnp.concatenate(
            [recv_ref[n, row + half * 8 : row + half * 8 + 1, :] for half in range(2)], 1
        )

    def beside(c, i, before, after, left, right):
        if i == 0:
            before = before + square * outside(0, c, 0)
        if i == 7:
            after = after + square * outside(3, c, 1)
        start = 192 + (i % 2) * 8
        columns = recv_ref[i // 2, start : start + 8, :]
        left = left + square * pltpu.roll(columns, (128 - c) % 128, 1)
        right = right + square * pltpu.roll(columns, 127 - (3 + c), 1)
        return before, after, left, right

    for i in range(8):
        for c in range(3):
            surface[c, strip_of(i), :] = u_ref[c, 0, strip_of(i), :] + square * traction(0, c, i)
    for z in range(2):
        for i in range(8):
            rows = strip_of(i)
            above = lambda c, r: u_ref[c, z + 1, r, :]
            if z == 0:
                load, below = lambda c, r: surface[c, r, :], None
            else:
                load, below = lambda c, r: u_ref[c, 1, r, :], lambda c, r: surface[c, r, :]
            centers, sums = stencil_strip(
                i, load, beside if z == 0 else None, above, below, halo_refs, z
            )
            force = strip_force(
                centers, sums, region_ref[z, rows, :], plastic_ref[rows, :], shear_ref, yields_ref
            )
            for c in range(3):
                v = v_ref[c, z, rows, :]
                if z == 0:
                    v = v + DT * traction(0, c, i)
                    v = v + DT * (force[c] + (traction(1, c, i) - DAMPING * v))
                else:
                    v = v + DT * force[c]
                new_v_ref[c, z, rows, :] = v
                new_u_ref[c, z, rows, :] = centers[c] + DT * v


def history_kernel(where_ref, kernel_ref, history_ref, *refs):
    own_ref, main_ref, edge_ref = refs[-3:]
    low = where_ref[0] == 1
    width = own_ref.shape[1]

    def step(m, carry):
        total, ones = carry
        out, twos = [], []
        for c in range(3):
            two = kernel_ref[m + 2, c].astype(F32)
            twos.append(two)
            for ri in range(2):
                past = history_ref[m, ri, c].astype(F32)
                p1, p2 = total[c * 2 + ri]
                out.append((p1 + ones[c] * past, p2 + two * past))
        return tuple(out), tuple(twos)

    zero = jnp.zeros((8, width), F32)
    total, _ = lax.fori_loop(
        0, 31, step,
        (tuple((zero, zero) for _ in range(6)), tuple(kernel_ref[1, c].astype(F32) for c in range(3))),
    )
    values = [None] * 18
    for c in range(3):
        one = kernel_ref[32, c].astype(F32)
        for ri in range(2):
            p1, p2 = total[c * 2 + ri]
            values[ri * 3 + c] = p1 + one * history_ref[31, ri, c].astype(F32)
            values[6 + ri * 3 + c] = p2
        values[12 + c] = kernel_ref[0, c].astype(F32)
        values[15 + c] = kernel_ref[1, c].astype(F32)
    for i, value in enumerate(values):
        row = [value[r : r + 1] for r in range(8)]
        for r, (a, b) in enumerate(((0, 4), (1, 3), (2, 2), (3, 1))):
            own_ref[i * 4 + r : i * 4 + r + 1, :] = jnp.where(low, row[a], row[b])
        for r, (a, b) in enumerate(((4, 4), (5, 7), (6, 6), (7, 5))):
            main_ref[i * 4 + r : i * 4 + r + 1, :] = jnp.where(low, row[a], row[b])
        edge_ref[i : i + 1, :] = row[0]


def mirror_kernel(where_ref, reverse_ref, own_ref, main_ref, edge_ref, out_ref, tiles, turned):
    low = where_ref[0] == 1
    special = where_ref[1]
    for i in range(18):
        own = own_ref[i * 4 : i * 4 + 4, :]
        main = main_ref[i * 4 : i * 4 + 4, :]
        edge = edge_ref[i : i + 1, :]
        other = jnp.where(rows_of(main.shape) == 0, edge, main)
        tiles[i * 8 : i * 8 + 4, :] = jnp.where(low, own, main)
        tiles[i * 8 + 4 : i * 8 + 8, :] = jnp.where(low, other, own)
    for block in range(16):
        part = slice(block * 128, block * 128 + 128)
        high, rest = halves(tiles[:, part])
        turned[:, part] = dot(high, reverse_ref[...]) + dot(rest, reverse_ref[...])
    lane = lanes((8, 128))
    row = rows_of((8, 128))
    upper = row >= 4
    chosen = (lax.rem(row, 4) + (1 - special)) == 0

    def swap(x):
        return pltpu.roll(x, 4, 0)

    for block in range(16):
        part = slice(block * 128, block * 128 + 128)
        mirror = slice((15 - block) * 128, (15 - block) * 128 + 128)
        first = ((16 - block) % 16) * 128
        first = slice(first, first + 128)

        def load(i):
            rows = slice(i * 8, i * 8 + 8)
            back = jnp.where(lane == 0, turned[rows, first], turned[rows, mirror])
            return tiles[rows, part], back

        for c in range(3):
            for k in range(2):
                t, b = load(12 + k * 3 + c)
                own = 0.5 * (t + b)
                other = swap(own)
                mean = jnp.where(chosen, 0.5 * (own + other), 0.5 * (t + swap(b)))
                diff = jnp.where(chosen, 0.5 * (own - other), 0.0)
                out_ref[k, c, :, part] = jnp.where(upper, swap(mean), mean)
                out_ref[2 + k, c, :, part] = jnp.where(upper, swap(diff), diff)
            pair = []
            for k in range(2):
                tr, br = load(k * 6 + c)
                ti, bi = load(k * 6 + 3 + c)
                hr, hi = 0.5 * (tr + br), 0.5 * (ti - bi)
                sr, si = swap(hr), swap(hi)
                pair.append(
                    (
                        jnp.where(chosen, hr - si, 0.5 * (tr + swap(br))),
                        jnp.where(chosen, hi + sr, 0.5 * (ti - swap(bi))),
                        hr + si,
                        hi - sr,
                    )
                )
            out_ref[4, c, :, part] = jnp.where(upper, swap(pair[1][0]), pair[0][0])
            out_ref[5, c, :, part] = jnp.where(upper, swap(pair[1][1]), pair[0][1])
            out_ref[6, c, :, part] = pair[0][2]
            out_ref[7, c, :, part] = pair[0][3]


def dip_kernel(radix_ref, turn_ref, out_table_ref, recv_ref, _after_ref, send_ref):
    wide = []
    for c in range(3):
        pieces = []
        for n in range(4):
            for f in range(2):
                start = f * 96 + c * 32
                pieces.append(recv_ref[n, start : start + 32, :])
        wide.append(jnp.concatenate(pieces, 0))
    z = left_dot(radix_ref, jnp.concatenate(wide, 1))
    lane = lanes((1, 128))
    for s in range(2):
        tr, ti = turn_ref[0, s], turn_ref[1, s]
        for c in range(3):
            part = slice(c * 128, c * 128 + 128)
            zr = z[s * 128 : s * 128 + 128, part]
            zi = z[256 + s * 128 : 384 + s * 128, part]
            turned = jnp.concatenate([zr * tr - zi * ti, zr * ti + zi * tr], 1)
            high, low = halves(turned)
            table, rest = out_table_ref[0, s], out_table_ref[1, s]
            res = dot(table, high, (1, 1)) + (dot(rest, high, (1, 1)) + dot(table, low, (1, 1)))
            imag = res[64:128]
            if s == 0:
                extra = jnp.where(lax.rem(lane, 4) == 0, res[128:129], 0.0)
                imag = jnp.where(rows_of(imag.shape) == 0, imag + extra, imag)
            send_ref[pl.ds(s * 384 + c * 2, 64, stride=6), :] = res[0:64]
            send_ref[pl.ds(s * 384 + c * 2 + 1, 64, stride=6), :] = imag


def strike_kernel(
    in_ref, turn_ref, mix_ref, reverse_ref, unmix_ref, out_table_ref,
    coef_ref, recv_ref, _after_ref, send_ref, spec, back, total,
):
    tr, ti = turn_ref[0], turn_ref[1]
    real, imag = [], []
    for c in range(3):
        re = recv_ref[pl.ds(c * 2, 128, stride=6), :].T
        im = recv_ref[pl.ds(c * 2 + 1, 128, stride=6), :].T
        y = right_dot(jnp.concatenate([re, im], 1), in_ref)
        yr, yi = y[:, :128], y[:, 128:]
        real.append(yr * tr - yi * ti)
        imag.append(yr * ti + yi * tr)
    stacked = jnp.concatenate([jnp.concatenate(real, 1), jnp.concatenate(imag, 1)], 0)
    spec[...] = left_dot(mix_ref, stacked)
    for c in range(3):
        part = slice(c * 128, c * 128 + 128)
        high, low = halves(spec[:, part])
        back[:, part] = dot(high, reverse_ref[...]) + dot(low, reverse_ref[...])
    lane = lanes((8, 128))
    upper = rows_of((8, 128)) >= 4

    def swap(x):
        return pltpu.roll(x, 4, 0)

    for c in range(3):
        part = slice(c * 128, c * 128 + 128)
        for block in range(16):
            wave = slice(block * 128, block * 128 + 128)
            a0, a1 = coef_ref[0, c, :, wave], coef_ref[1, c, :, wave]
            m0, m1 = coef_ref[2, c, :, wave], coef_ref[3, c, :, wave]
            for ri in range(2):
                rows = slice(ri * 128 + block * 8, ri * 128 + block * 8 + 8)
                first = ri * 128 + ((16 - block) % 16) * 8
                other = ri * 128 + (15 - block) * 8
                s = spec[rows, part]
                r = jnp.where(
                    lane == 0, back[first : first + 8, part], back[other : other + 8, part]
                )
                if ri == 1:
                    r = -r
                t = a0 * s + m0 * r + coef_ref[4 + ri, c, :, wave]
                q = a0 * r + m0 * s + coef_ref[6 + ri, c, :, wave]
                more = (DT * DT) * (a0 * swap(t) + m0 * swap(q)) + a1 * swap(s) + m1 * swap(r)
                total[rows, part] = t + jnp.where(upper, more, 0.0)
    y = left_dot(unmix_ref, total[...])
    owner = rows_of((128, 128))
    wide_lane = lanes((128, 128))
    extra = [jnp.zeros((128, 128), F32)] * 2
    for c in range(3):
        part = slice(c * 128, c * 128 + 128)
        yr, yi = y[:128, part], y[128:, part]
        turned = jnp.concatenate([yr * tr + yi * ti, yi * tr - yr * ti], 1)
        high, low = halves(turned)
        res = dot(out_table_ref[0], high, (1, 1)) + (
            dot(out_table_ref[1], high, (1, 1)) + dot(out_table_ref[0], low, (1, 1))
        )
        for ri in range(2):
            lines = res[ri * 128 : ri * 128 + 128]
            send_ref[pl.ds(c * 2 + ri, 128, stride=8), :] = lines
            for side in range(2):
                group = c * 2 + side
                if side == 0:
                    moved = jnp.where(owner == 0, 0.0, pltpu.roll(lines, 1, 0))
                    moved = pltpu.roll(moved, (group * 8 + 8) % 128, 1)
                else:
                    moved = jnp.where(owner == 127, 0.0, pltpu.roll(lines, 127, 0))
                    moved = pltpu.roll(moved, group * 8, 1) if group else moved
                extra[ri] = jnp.where(wide_lane // 8 == group, moved, extra[ri])
    for ri in range(2):
        send_ref[pl.ds(6 + ri, 128, stride=8), :] = extra[ri]


def undip_kernel(in_ref, turn_ref, unradix_ref, recv_ref, _after_ref, send_ref):
    row = rows_of((128, 128))
    lane = lanes((128, 128))
    alt = jnp.where(lax.rem(lane, 2) == 0, 0.5, -0.5).astype(F32)
    stacks = [[], [], [], []]
    for c in range(4):
        re = recv_ref[pl.ds(c * 2, 128, stride=8), :].T
        im = recv_ref[pl.ds(c * 2 + 1, 128, stride=8), :].T
        h = right_dot(jnp.concatenate([re, im], 1), in_ref)
        for s in range(2):
            hr = h[:, s * 256 : s * 256 + 128]
            hi = h[:, s * 256 + 128 : s * 256 + 256]
            if s == 0:
                fix = alt * im[:, 0:1] - 0.5 * re[:, 0:1]
                hr = hr + jnp.where(lax.rem(row, 4) == 0, fix, 0.0)
            tr, ti = turn_ref[0, s], turn_ref[1, s]
            stacks[s].append(hr * tr + hi * ti)
            stacks[2 + s].append(hi * tr - hr * ti)
    stacked = jnp.concatenate([jnp.concatenate(part, 1) for part in stacks], 0)
    out = left_dot(unradix_ref, stacked)
    for n in range(4):
        for f in range(2):
            for c in range(3):
                start = f * 96 + c * 32
                row0 = (n * 2 + f) * 32
                send_ref[n, start : start + 32, :] = out[row0 : row0 + 32, c * 128 : c * 128 + 128]
    small = lanes((16, 128))

    def plane(n, half, c):
        row0 = n * 64 + half * 16
        return out[row0 : row0 + 16, c * 128 : c * 128 + 128]

    for n in range(4):
        columns = jnp.zeros((16, 128), F32)
        for c in range(3):
            if n > 0:
                moved = pltpu.roll(plane(n - 1, 1, c), c + 1, 1)
                columns = jnp.where(small == c, moved, columns)
            if n < 3:
                moved = pltpu.roll(plane(n + 1, 0, c), 3 + c, 1)
                columns = jnp.where(small == 3 + c, moved, columns)
        send_ref[n, 192:208, :] = columns
        for half in range(2):
            send_ref[n, 208 + half * 8 : 216 + half * 8, :] = plane(n, half, 3)[:8]


def full(shape):
    zeros = (0,) * len(shape)
    return pl.BlockSpec(shape, lambda *_: zeros)


SMEM = pl.BlockSpec(memory_space=pltpu.SMEM)


def shape_of(*shape):
    return jax.ShapeDtypeStruct(shape, F32)


def call(body, out_shape, args, smem=0, scratch=(), after=(), name=None):
    outs = out_shape if isinstance(out_shape, (tuple, list)) else [out_shape]
    size = sum(math.prod(x.shape) * 4 for x in list(args) + list(outs))
    out_specs = [full(x.shape) for x in outs]
    return pl.pallas_call(
        body,
        grid=(1,),
        in_specs=[SMEM] * smem
        + [full(x.shape) for x in args[smem:]]
        + [pl.BlockSpec(memory_space=pl.ANY)] * len(after),
        out_specs=out_specs if isinstance(out_shape, (tuple, list)) else out_specs[0],
        out_shape=out_shape,
        scratch_shapes=scratch,
        cost_estimate=pl.CostEstimate(flops=0, bytes_accessed=size, transcendentals=0),
        name=name,
    )(*args, *after)


def halo(first, last, left, right):
    up = [(i, i + 1) for i in range(31)]
    down = [(i + 1, i) for i in range(31)]
    top = lax.ppermute(last, "wide", up)
    bottom = lax.ppermute(first, "wide", down)
    up = [(i, i + 1) for i in range(3)]
    down = [(i + 1, i) for i in range(3)]
    from_left = lax.ppermute(right, "narrow", up)
    from_right = lax.ppermute(left, "narrow", down)
    return top, bottom, from_left, from_right


def exchange(x, axis):
    return lax.all_to_all(x, axis, split_axis=0, concat_axis=0, tiled=True)


def body(u, v, region, flags, shear, yields, history, kernel):
    device = lax.axis_index(ALL)
    where = jnp.stack([device < 64, device == 0]).astype(jnp.int32)
    edge_shapes = [shape_of(48, 256)] * 2 + [shape_of(64, 128)] * 2
    near = lambda depth: pl.BlockSpec((3, depth, 64, 256), lambda *_: (0, 0, 0, 0))
    slab = lambda depth: pl.BlockSpec((depth, 64, 256), lambda *_: (0, 0, 0))
    planes = lambda depth, start=0: pl.BlockSpec(
        (3, depth, 64, 256), lambda z: (0, z + start // depth, 0, 0)
    )
    slabs = lambda depth, start=0: pl.BlockSpec(
        (depth, 64, 256), lambda z: (z + start // depth, 0, 0)
    )
    halo_specs = [full((48, 256))] * 2 + [full((64, 128))] * 2
    any_spec = pl.BlockSpec(memory_space=pl.ANY)
    t = TABLES

    first, last, left, right, plastic = pl.pallas_call(
        edges_kernel,
        grid=(4,),
        in_specs=[planes(4), full((8, 32))],
        out_specs=[full(s.shape) for s in edge_shapes] + [full((64, 256))],
        out_shape=edge_shapes + [shape_of(64, 256)],
        cost_estimate=pl.CostEstimate(flops=0, bytes_accessed=3300000, transcendentals=0),
        name="edges",
    )(u, flags)
    halo_one = halo(first, last, left, right)

    width = 256
    steps = 1024 // width

    def sums(part, after):
        shift = part * steps
        given = [] if part == 0 else list(after)
        return pl.pallas_call(
            history_kernel,
            grid=(steps,),
            in_specs=[
                SMEM,
                pl.BlockSpec((33, 3, 8, width), lambda i: (0, 0, 0, i + shift)),
                pl.BlockSpec((32, 2, 3, 8, width), lambda i: (0, 0, 0, 0, i + shift)),
            ]
            + [any_spec] * len(given),
            out_specs=[
                pl.BlockSpec((72, width), lambda i: (0, i + shift)),
                pl.BlockSpec((72, width), lambda i: (0, i + shift)),
                pl.BlockSpec((18, width), lambda i: (0, i + shift)),
            ],
            out_shape=[shape_of(72, 2048), shape_of(72, 2048), shape_of(18, 2048)],
            input_output_aliases={3: 0, 4: 1, 5: 2} if given else {},
            cost_estimate=pl.CostEstimate(flops=0, bytes_accessed=5500000, transcendentals=0),
            name="history",
        )(where, kernel, history, *given)

    partial = sums(0, None)
    send = pl.pallas_call(
        slip_kernel,
        grid=(1,),
        in_specs=[SMEM, SMEM, near(2), near(1), slab(1), full((64, 256))] + halo_specs + [any_spec],
        out_specs=full((4, 192, 128)),
        out_shape=shape_of(4, 192, 128),
        cost_estimate=pl.CostEstimate(flops=0, bytes_accessed=1500000, transcendentals=0),
        name="slip",
    )(shear, yields, u, v, region, plastic, *halo_one, partial[2])
    lines = exchange(send, "narrow")
    own, main, edge = sums(1, partial)
    main = lax.ppermute(main, ALL, [(i, 127 - i) for i in range(128)])
    edge = lax.ppermute(edge, ALL, [(64, 0)] + [(i, 128 - i) for i in range(65, 128)])

    send = call(
        dip_kernel, shape_of(768, 128), (t["radix"], t["dip_turn"], t["dip_out"], lines),
        after=[own], name="dip",
    )
    waves = exchange(send.reshape(128, 1, 768), ALL).reshape(768, 128)

    new_u, new_v, first, last, left, right = pl.pallas_call(
        step_one_kernel,
        grid=(16 // PLANES,),
        in_specs=[SMEM, SMEM, near(16), planes(PLANES), slabs(PLANES), full((64, 256))]
        + halo_specs
        + [any_spec],
        out_specs=[planes(PLANES)] * 2 + [full(s.shape) for s in edge_shapes],
        out_shape=[shape_of(3, 16, 64, 256)] * 2 + edge_shapes,
        cost_estimate=pl.CostEstimate(flops=0, bytes_accessed=14000000, transcendentals=0),
        name="step_one",
    )(shear, yields, u, v, region, plastic, *halo_one, send)
    halo_two = halo(first, last, left, right)

    coefficients = call(
        mirror_kernel,
        shape_of(8, 3, 8, 2048),
        (where, t["reverse"], own, main, edge),
        smem=1,
        scratch=[pltpu.VMEM((144, 2048), F32)] * 2,
        name="mirror",
    )
    send = call(
        strike_kernel,
        shape_of(1024, 128),
        (
            t["strike_in"], t["strike_turn"], t["strike_mix"], t["reverse"],
            t["strike_unmix"], t["strike_out"], coefficients, waves,
        ),
        scratch=[pltpu.VMEM((256, 384), F32)] * 3,
        after=[new_u],
        name="strike",
    )
    columns = exchange(send.reshape(128, 8, 128), ALL).reshape(1024, 128)

    def later(start, stop, given, after):
        return pl.pallas_call(
            functools.partial(step_two_kernel, start),
            grid=((stop - start) // PLANES,),
            in_specs=[
                SMEM, SMEM, near(16), planes(PLANES, start), slabs(PLANES, start), full((64, 256)),
            ]
            + halo_specs
            + [any_spec] * (len(given) + 1),
            out_specs=[planes(PLANES, start)] * 2,
            out_shape=[shape_of(3, 16, 64, 256)] * 2,
            input_output_aliases={10: 0, 11: 1} if given else {},
            cost_estimate=pl.CostEstimate(
                flops=0, bytes_accessed=(stop - start) * 800000, transcendentals=0
            ),
            name="step_two",
        )(shear, yields, new_u, new_v, region, plastic, *halo_two, *given, after)

    out = later(2, 10, [], send)
    send = call(
        undip_kernel,
        shape_of(4, 224, 128),
        (t["dip_in"], t["undip_turn"], t["unradix"], columns),
        after=[out[0]],
        name="undip",
    )
    tractions = exchange(send, "narrow")
    out = later(10, 16, out, send)
    return tuple(
        pl.pallas_call(
            last_kernel,
            grid=(1,),
            in_specs=[SMEM, SMEM, near(4), near(2), slab(2), full((64, 256))]
            + halo_specs
            + [full((4, 224, 128))]
            + [any_spec] * 2,
            out_specs=[near(2)] * 2,
            out_shape=[shape_of(3, 16, 64, 256)] * 2,
            scratch_shapes=[pltpu.VMEM((3, 64, 256), F32)],
            input_output_aliases={11: 0, 12: 1},
            cost_estimate=pl.CostEstimate(flops=0, bytes_accessed=4000000, transcendentals=0),
            name="last",
        )(shear, yields, new_u, new_v, region, plastic, *halo_two, tractions, *out)
    )


def solution(mesh):
    tile = P(None, None, "wide", "narrow")
    in_specs = (
        tile,
        tile,
        P(None, "wide", "narrow"),
        P("wide", "narrow"),
        P(),
        P(),
        P(None, None, None, ALL, None),
        P(None, None, ALL, None),
    )
    return jax.shard_map(body, mesh=mesh, in_specs=in_specs, out_specs=(tile, tile), check_vma=False)
```

time: 179 us -> 135 us (0.75)
  the two profiles are of different devices: /device:TPU:6 before, /device:TPU:4 now
where the time goes in v2:
time: 135 us; the launch traced here: 134 us
  Pallas kernels  60.6 us (45%)
  starting transfers between devices  60.3 us (45%)
  waiting for transfers between devices  5.92 us (4%)
  local copies, waits for them, and re-layouts  5.84 us (4%)
    all_to_all x4, starting transfers between devices, exchange(): return lax.all_to_all(x, axis, split_axis=0, concat_axis=0, tiled=True)  24.8 us
    ppermute x2, starting transfers between devices, halo(): bottom = lax.ppermute(first, 'wide', down)  15.8 us
    pallas_call x4, Pallas kernels, call(): pl.pallas_call(body, grid=(1,), in_specs=[SMEM] * smem + [full(x.shape) f...  15 us
    pallas_call x1, Pallas kernels, body(): pl.pallas_call(step_one_kernel, grid=(16 // PLANES,), in_specs=[SMEM, SME...  14.6 us
    pallas_call x2, Pallas kernels, later(): pl.pallas_call(functools.partial(step_two_kernel, start), grid=((stop - s...  11.1 us
    pallas_call x2, Pallas kernels, sums(): pl.pallas_call(history_kernel, grid=(steps,), in_specs=[SMEM, pl.BlockSpe...  10.9 us
    ppermute x2, starting transfers between devices, halo(): top = lax.ppermute(last, 'wide', up)  7.35 us
    unnamed x38, local copies, waits for them, and re-layouts  5.84 us
  transfers between devices with their start and end apart: 14, of which 2 were waited for; matrix products, arithmetic and copies ran while one was open for 0% of the time, Pallas kernels for 32%

profile of v2, /device:TPU:4, one launch (start us, length us, event | category | flops | bytes accessed | tf_op | source)
XLA Modules:
  0.0 134.1 jit_solution(1070068184887879403)
XLA Ops:
  0.6 4.1 %edges.1 = (f32[48,256]{1,0:T(8,128)}, f32[48,256]{1,0:T(8,128)}, f32[64,128]{1,0:T(8,128)}, f32[64,128]{1,0:T(8,128)}, f32[64,256]{1,0:T(8,128)}) custom-call(f32[3,16,64,256]{3,2,1,0:T(8,128)} %u_ref.5, s32[8,32]{1,0:T(8,128)} %flags_ref.1), custom_call_target="tpu_custom_call" | custom-call | bytes 3300000 | tf_op jit(solution)/shard_map/edges/pallas_call | solution.py:704
  4.7 1.7 %collective-permute-start.2 = (f32[64,128]{1,0:T(8,128)}, f32[64,128]{1,0:T(8,128)S(1)}, u32[]{:S(2)}, u32[]{:S(2)}) collective-permute-start(f32[64,128]{1,0:T(8,128)} %get-tuple-element.26), channel_id=1, source_target_pairs={{0,1},{1,2},{2,3},{4,5},{5,6},{6,7},{8,9},{9,10},{10,11},{12,13},{... | collective-permute-start | bytes 98312 | tf_op jit(solution)/shard_map/ppermute | solution.py:679
  6.5 1.3 collective-permute-start.3
  7.8 3.8 %collective-permute-start = (f32[48,256]{1,0:T(8,128)}, f32[48,256]{1,0:T(8,128)S(1)}, u32[]{:S(2)}, u32[]{:S(2)}) collective-permute-start(f32[48,256]{1,0:T(8,128)} %get-tuple-element.24), channel_id=1, source_target_pairs={{0,4},{4,8},{8,12},{12,16},{16,20},{20,24},{24,28},{28,32},{32,36}... | collective-permute-start | bytes 147464 | tf_op jit(solution)/shard_map/ppermute | solution.py:675
  11.6 7.7 %collective-permute-start.1 = (f32[48,256]{1,0:T(8,128)}, f32[48,256]{1,0:T(8,128)S(1)}, u32[]{:S(2)}, u32[]{:S(2)}) collective-permute-start(f32[48,256]{1,0:T(8,128)} %get-tuple-element.25), channel_id=1, source_target_pairs={{4,0},{8,4},{12,8},{16,12},{20,16},{24,20},{28,24},{32,28},{36,32}... | collective-permute-start | bytes 147464 | tf_op jit(solution)/shard_map/ppermute | solution.py:676
  19.4 0.6 add_convert_fusion.where_ref
  20.0 5.4 %history.2 = (f32[72,2048]{1,0:T(8,128)}, f32[72,2048]{1,0:T(8,128)}, f32[18,2048]{1,0:T(8,128)}) custom-call(s32[2]{0:T(128)} %add_convert_fusion.where_ref, bf16[33,3,8,2048]{3,2,1,0:T(8,128)(2,1)} %kernel_ref.3, bf16[32,2,3,8,2048]{4,3,2,1,0:T(8,128)(2,1)} %history_ref.3), custom_call_target="tpu_custom_call" | custom-call | bytes 5500000 | tf_op jit(solution)/shard_map/history/pallas_call | solution.py:721
  25.4 0.0 collective-permute-done.2.left_ref
  25.4 0.0 copy-start.13
  25.4 0.0 collective-permute-done.3.right_ref
  25.4 0.0 copy-start.14
  25.4 0.0 collective-permute-done.top_ref
  25.4 0.0 copy-start.10
  25.5 0.0 collective-permute-done.1.bottom_ref
  25.5 0.0 copy-start.11
  25.5 0.5 copy-done.13
  26.0 0.0 copy-done.14
  26.0 0.0 copy-done.10
  26.1 0.0 copy-done.11
  26.1 2.1 %slip.1 = f32[4,192,128]{2,1,0:T(8,128)} custom-call(f32[4]{0:T(128)} %shear_ref.5, f32[4]{0:T(128)} %yields_ref.5, f32[3,16,64,256]{3,2,1,0:T(8,128)} %u_ref.5, f32[3,16,64,256]{3,2,1,0:T(8,128)} %v_ref.3, s32[16,64,256]{2,1,0:T(8,128)} %region_ref.5, f32[64,256]{1,0:T(8,128)} %get-tuple-element.23.plastic_ref.refs_5_, f32[48,256]{1,0:T(8,128)} %copy-done.10, ...), custom_call_target="tpu_custom_call" | custom-call | bytes 1500000 | tf_op jit(solution)/shard_map/slip/pallas_call | solution.py:742
  28.2 5.0 %all-to-all-start = ((f32[4,192,128]{2,1,0:T(8,128)}), f32[4,192,128]{2,1,0:T(8,128)S(1)}, u32[]{:S(2)}, u32[]{:S(2)}) async-start(f32[4,192,128]{2,1,0:T(8,128)} %slip.1), calls=%async_computation | async-start | bytes 786432 | tf_op jit(solution)/shard_map/all_to_all | solution.py:685
  33.2 5.4 %history.3 = (f32[72,2048]{1,0:T(8,128)}, f32[72,2048]{1,0:T(8,128)}, f32[18,2048]{1,0:T(8,128)}) custom-call(s32[2]{0:T(128)} %add_convert_fusion.where_ref, bf16[33,3,8,2048]{3,2,1,0:T(8,128)(2,1)} %kernel_ref.3, bf16[32,2,3,8,2048]{4,3,2,1,0:T(8,128)(2,1)} %history_ref.3, ...), custom_call_target="tpu_custom_call", output_to_operand_aliasing={{0}: (3, {}), {1}: (4, {}), {2}: (5, {})} | custom-call | bytes 5500000 | tf_op jit(solution)/shard_map/history/pallas_call | solution.py:721
  38.6 3.6 %collective-permute-start.8 = (f32[72,2048]{1,0:T(8,128)}, f32[72,2048]{1,0:T(8,128)S(1)}, u32[]{:S(2)}, u32[]{:S(2)}) collective-permute-start(f32[72,2048]{1,0:T(8,128)} %get-tuple-element.38), channel_id=1, source_target_pairs={{0,127},{1,126},{2,125},{3,124},{4,123},{5,122},{6,121},{7,120},{8... | collective-permute-start | bytes 1769480 | tf_op jit(solution)/shard_map/ppermute | solution.py:753
  42.3 0.0 all-to-all-done.recv_ref
  42.3 0.7 copy-done.2
  43.0 3.2 %dip.1._after_ref = f32[768,128]{1,0:T(8,128)} custom-call(bf16[2,512,256]{2,1,0:T(8,128)(2,1)} %constant.37.clone.radix_ref, f32[2,2,128,128]{3,2,1,0:T(8,128)} %constant.38.clone.turn_ref, bf16[2,2,136,256]{3,2,1,0:T(8,128)(2,1)} %constant.39.clone.out_table_ref, f32[4,192,128]{2,1,0:T(8,128)} %copy-done.2, f32[72,2048]{1,0:T(8,128)} %get-tuple-element.31._after_ref.own_ref), custom_call_target="tpu_custom_call" | custom-call | bytes 2654208 | tf_op jit(solution)/shard_map/dip/pallas_call | solution.py:658
  46.2 6.1 %all-to-all-start.1 = ((f32[128,1,768]{2,1,0:T(1,128)}), f32[128,1,768]{2,1,0:T(1,128)S(1)}, u32[]{:S(2)}, u32[]{:S(2)}) async-start(f32[128,1,768]{2,1,0:T(1,128)} %bitcast.7), calls=%async_computation.1 | async-start | bytes 786432 | tf_op jit(solution)/shard_map/all_to_all | solution.py:685
  52.3 0.0 copy-done.4
  52.3 3.0 %collective-permute-start.9 = (f32[18,2048]{1,0:T(8,128)S(1)}, f32[18,2048]{1,0:T(8,128)S(1)}, u32[]{:S(2)}, u32[]{:S(2)}) collective-permute-start(f32[18,2048]{1,0:T(8,128)S(1)} %copy-done.4), channel_id=1, source_target_pairs={{64,0},{65,63},{66,62},{67,61},{68,60},{69,59},{70,58},{71,57},{72... | collective-permute-start | bytes 442376 | tf_op jit(solution)/shard_map/ppermute | solution.py:754
  55.3 14.6 %step_one.1 = (f32[3,16,64,256]{3,2,1,0:T(8,128)}, f32[3,16,64,256]{3,2,1,0:T(8,128)}, f32[48,256]{1,0:T(8,128)}, f32[48,256]{1,0:T(8,128)}, f32[64,128]{1,0:T(8,128)}, /*index=5*/f32[64,128]{1,0:T(8,128)}) custom-call(f32[4]{0:T(128)} %shear_ref.5, f32[4]{0:T(128)} %yields_ref.5, f32[3,16,64,256]{3,2,1,0:T(8,128)} %u_ref.5, f32[3,16,64,256]{3,2,1,0:T(8,128)} %v_ref.3, ...), custom_call_target="tpu_custom_call" | custom-call | bytes 14000000 | tf_op jit(solution)/shard_map/step_one/pallas_call | solution.py:762
  69.9 0.0 collective-permute-done.9.edge_ref
  69.9 0.0 copy-start.12
  69.9 0.0 collective-permute-done.8.main_ref
  69.9 0.7 copy-done.12
  70.6 0.8 copy-done.5
  71.4 3.6 %mirror.1.coef_ref = f32[8,3,8,2048]{3,2,1,0:T(8,128)} custom-call(s32[2]{0:T(128)} %add_convert_fusion.where_ref, bf16[128,128]{1,0:T(8,128)(2,1)} %constant.40.clone.reverse_ref, f32[72,2048]{1,0:T(8,128)} %get-tuple-element.31._after_ref.own_ref, f32[72,2048]{1,0:T(8,128)} %copy-done.5, f32[18,2048]{1,0:T(8,128)} %copy-done.12), custom_call_target="tpu_custom_call" | custom-call | bytes 2965512 | tf_op jit(solution)/shard_map/mirror/pallas_call | solution.py:658
  75.0 0.0 all-to-all-done.1
  75.0 0.7 copy-done.3
  75.7 4.8 %strike.1.refs_10_ = f32[1024,128]{1,0:T(8,128)} custom-call(bf16[2,256,256]{2,1,0:T(8,128)(2,1)} %constant.41.clone.in_ref.out_table_ref, f32[2,128,128]{2,1,0:T(8,128)} %constant.42.clone.turn_ref, bf16[2,256,256]{2,1,0:T(8,128)(2,1)} %constant.43.clone.mix_ref, bf16[128,128]{1,0:T(8,128)(2,1)} %constant.40.clone.reverse_ref, ...), custom_call_target="tpu_custom_call" | custom-call | bytes 4784128 | tf_op jit(solution)/shard_map/strike/pallas_call | solution.py:658
  80.5 9.8 %all-to-all-start.2 = ((f32[128,8,128]{2,1,0:T(8,128)}), f32[128,8,128]{2,1,0:T(8,128)S(1)}, u32[]{:S(2)}, u32[]{:S(2)}) async-start(f32[128,8,128]{2,1,0:T(8,128)} %bitcast.6), calls=%async_computation.2 | async-start | bytes 1048576 | tf_op jit(solution)/shard_map/all_to_all | solution.py:685
  90.2 0.0 copy-done.16
  90.2 3.5 %collective-permute-start.4 = (f32[48,256]{1,0:T(8,128)S(1)}, f32[48,256]{1,0:T(8,128)S(1)}, u32[]{:S(2)}, u32[]{:S(2)}) collective-permute-start(f32[48,256]{1,0:T(8,128)S(1)} %copy-done.16), channel_id=1, source_target_pairs={{0,4},{4,8},{8,12},{12,16},{16,20},{20,24},{24,28},{28,32},{32,36}... | collective-permute-start | bytes 147464 | tf_op jit(solution)/shard_map/ppermute | solution.py:675
  93.8 0.0 copy-done.15
  93.8 8.0 %collective-permute-start.5 = (f32[48,256]{1,0:T(8,128)S(1)}, f32[48,256]{1,0:T(8,128)S(1)}, u32[]{:S(2)}, u32[]{:S(2)}) collective-permute-start(f32[48,256]{1,0:T(8,128)S(1)} %copy-done.15), channel_id=1, source_target_pairs={{4,0},{8,4},{12,8},{16,12},{20,16},{24,20},{28,24},{32,28},{36,32}... | collective-permute-start | bytes 147464 | tf_op jit(solution)/shard_map/ppermute | solution.py:676
  101.8 0.0 copy-done.18
  101.8 1.5 %collective-permute-start.6 = (f32[64,128]{1,0:T(8,128)S(1)}, f32[64,128]{1,0:T(8,128)S(1)}, u32[]{:S(2)}, u32[]{:S(2)}) collective-permute-start(f32[64,128]{1,0:T(8,128)S(1)} %copy-done.18), channel_id=1, source_target_pairs={{0,1},{1,2},{2,3},{4,5},{5,6},{6,7},{8,9},{9,10},{10,11},{12,13},{... | collective-permute-start | bytes 98312 | tf_op jit(solution)/shard_map/ppermute | solution.py:679
  103.3 1.3 collective-permute-start.7
  104.6 0.0 collective-permute-done.6.refs_8_.left_ref
  104.6 3.0 %collective-permute-done.7.refs_9_.right_ref = f32[64,128]{1,0:T(8,128)S(1)} collective-permute-done((f32[64,128]{1,0:T(8,128)S(1)}, f32[64,128]{1,0:T(8,128)S(1)}, u32[]{:S(2)}, u32[]{:S(2)}) %collective-permute-start.7) | collective-permute-done | bytes 32800 | tf_op jit(solution)/shard_map/ppermute | solution.py:680
  107.7 0.0 collective-permute-done.4.refs_6_.top_ref
  107.7 0.0 collective-permute-done.5.refs_7_.bottom_ref
  107.7 0.6 copy-done.9
  108.3 0.0 copy-done.6
  108.3 0.0 copy-done.7
  108.3 5.8 %step_two.2 = (f32[3,16,64,256]{3,2,1,0:T(8,128)}, f32[3,16,64,256]{3,2,1,0:T(8,128)}) custom-call(f32[4]{0:T(128)} %shear_ref.5, f32[4]{0:T(128)} %yields_ref.5, f32[3,16,64,256]{3,2,1,0:T(8,128)} %get-tuple-element.32._after_ref.refs_2_.u_ref, f32[3,16,64,256]{3,2,1,0:T(8,128)} %get-tuple-element.33.refs_3_.v_ref, s32[16,64,256]{2,1,0:T(8,128)} %region_ref.5, ...), custom_call_target="tpu_custom_call" | custom-call | bytes 6400000 | tf_op jit(solution)/shard_map/step_two/pallas_call | solution.py:797
  114.2 0.0 all-to-all-done.2
  114.2 0.0 copy-start
  114.2 0.8 copy-done
  115.0 3.5 %undip.1.refs_12_ = f32[4,224,128]{2,1,0:T(8,128)} custom-call(bf16[2,256,512]{2,1,0:T(8,128)(2,1)} %constant.45.clone.in_ref, f32[2,2,128,128]{3,2,1,0:T(8,128)} %constant.46.clone.turn_ref, bf16[2,256,512]{2,1,0:T(8,128)(2,1)} %constant.47.clone.unradix_ref, f32[1024,128]{1,0:T(8,128)} %bitcast.8, f32[3,16,64,256]{3,2,1,0:T(8,128)} %get-tuple-element.40._after_ref.refs_10_), custom_call_target="tpu_custom_call" | custom-call | bytes 3342336 | tf_op jit(solution)/shard_map/undip/pallas_call | solution.py:658
  118.5 3.9 %all-to-all-start.3 = ((f32[4,224,128]{2,1,0:T(8,128)}), f32[4,224,128]{2,1,0:T(8,128)S(1)}, u32[]{:S(2)}, u32[]{:S(2)}) async-start(f32[4,224,128]{2,1,0:T(8,128)} %undip.1.refs_12_), calls=%async_computation.3 | async-start | bytes 917504 | tf_op jit(solution)/shard_map/all_to_all | solution.py:685
  122.4 5.2 %step_two.3 = (f32[3,16,64,256]{3,2,1,0:T(8,128)}, f32[3,16,64,256]{3,2,1,0:T(8,128)}) custom-call(f32[4]{0:T(128)} %shear_ref.5, f32[4]{0:T(128)} %yields_ref.5, f32[3,16,64,256]{3,2,1,0:T(8,128)} %get-tuple-element.32._after_ref.refs_2_.u_ref, f32[3,16,64,256]{3,2,1,0:T(8,128)} %get-tuple-element.33.refs_3_.v_ref, ...), custom_call_target="tpu_custom_call", output_to_operand_aliasing={{0}: (10, {}), {1}: (11, {})} | custom-call | bytes 4800000 | tf_op jit(solution)/shard_map/step_two/pallas_call | solution.py:797
  127.6 2.9 %all-to-all-done.3.recv_ref = f32[4,224,128]{2,1,0:T(8,128)S(1)} async-done(((f32[4,224,128]{2,1,0:T(8,128)}), f32[4,224,128]{2,1,0:T(8,128)S(1)}, u32[]{:S(2)}, u32[]{:S(2)}) %all-to-all-start.3) | async-done | bytes 458784 | tf_op jit(solution)/shard_map/all_to_all | solution.py:685
  130.5 0.8 copy-done.1
  131.3 2.8 %last.1 = (f32[3,16,64,256]{3,2,1,0:T(8,128)}, f32[3,16,64,256]{3,2,1,0:T(8,128)}) custom-call(f32[4]{0:T(128)} %shear_ref.5, f32[4]{0:T(128)} %yields_ref.5, f32[3,16,64,256]{3,2,1,0:T(8,128)} %get-tuple-element.32._after_ref.refs_2_.u_ref, f32[3,16,64,256]{3,2,1,0:T(8,128)} %get-tuple-element.33.refs_3_.v_ref, ...), custom_call_target="tpu_custom_call", output_to_operand_aliasing={{0}: (11, {}), {1}: (12, {})} | custom-call | bytes 4000000 | tf_op jit(solution)/shard_map/last/pallas_call | solution.py:825
  (15 shorter events, 0.0 us)
Async XLA Ops:
  4.7 20.7 %collective-permute-start.2 = (f32[64,128]{1,0:T(8,128)}, f32[64,128]{1,0:T(8,128)S(1)}, u32[]{:S(2)}, u32[]{:S(2)}) collective-permute-start(f32[64,128]{1,0:T(8,128)} %get-tuple-element.26), channel_id=1, source_target_pairs={{0,1},{1,2},{2,3},{4,5},{5,6},{6,7},{8,9},{9,10},{10,11},{12,13},{... | collective-permute-start | bytes 98312 | tf_op jit(solution)/shard_map/ppermute | solution.py:679
  6.5 19.0 %collective-permute-start.3 = (f32[64,128]{1,0:T(8,128)}, f32[64,128]{1,0:T(8,128)S(1)}, u32[]{:S(2)}, u32[]{:S(2)}) collective-permute-start(f32[64,128]{1,0:T(8,128)} %get-tuple-element.27), channel_id=1, source_target_pairs={{1,0},{2,1},{3,2},{5,4},{6,5},{7,6},{9,8},{10,9},{11,10},{13,12},{... | collective-permute-start | bytes 98312 | tf_op jit(solution)/shard_map/ppermute | solution.py:680
  7.8 17.7 %collective-permute-start = (f32[48,256]{1,0:T(8,128)}, f32[48,256]{1,0:T(8,128)S(1)}, u32[]{:S(2)}, u32[]{:S(2)}) collective-permute-start(f32[48,256]{1,0:T(8,128)} %get-tuple-element.24), channel_id=1, source_target_pairs={{0,4},{4,8},{8,12},{12,16},{16,20},{20,24},{24,28},{28,32},{32,36}... | collective-permute-start | bytes 147464 | tf_op jit(solution)/shard_map/ppermute | solution.py:675
  11.6 13.9 %collective-permute-start.1 = (f32[48,256]{1,0:T(8,128)}, f32[48,256]{1,0:T(8,128)S(1)}, u32[]{:S(2)}, u32[]{:S(2)}) collective-permute-start(f32[48,256]{1,0:T(8,128)} %get-tuple-element.25), channel_id=1, source_target_pairs={{4,0},{8,4},{12,8},{16,12},{20,16},{24,20},{28,24},{32,28},{36,32}... | collective-permute-start | bytes 147464 | tf_op jit(solution)/shard_map/ppermute | solution.py:676
  25.4 0.6 copy-start.13
  25.4 0.6 copy-start.14
  25.4 0.6 copy-start.10
  25.5 0.6 copy-start.11
  28.2 14.1 %all-to-all-start = ((f32[4,192,128]{2,1,0:T(8,128)}), f32[4,192,128]{2,1,0:T(8,128)S(1)}, u32[]{:S(2)}, u32[]{:S(2)}) async-start(f32[4,192,128]{2,1,0:T(8,128)} %slip.1), calls=%async_computation | async-start | bytes 786432 | tf_op jit(solution)/shard_map/all_to_all | solution.py:685
  38.6 13.6 %copy-start.4 = (f32[18,2048]{1,0:T(8,128)S(1)}, f32[18,2048]{1,0:T(8,128)}, u32[]{:S(2)}) copy-start(f32[18,2048]{1,0:T(8,128)} %get-tuple-element.39) | copy-start | bytes 442372
  38.6 31.2 %collective-permute-start.8 = (f32[72,2048]{1,0:T(8,128)}, f32[72,2048]{1,0:T(8,128)S(1)}, u32[]{:S(2)}, u32[]{:S(2)}) collective-permute-start(f32[72,2048]{1,0:T(8,128)} %get-tuple-element.38), channel_id=1, source_target_pairs={{0,127},{1,126},{2,125},{3,124},{4,123},{5,122},{6,121},{7,120},{8... | collective-permute-start | bytes 1769480 | tf_op jit(solution)/shard_map/ppermute | solution.py:753
  42.3 0.7 copy-start.2
  46.2 28.8 %all-to-all-start.1 = ((f32[128,1,768]{2,1,0:T(1,128)}), f32[128,1,768]{2,1,0:T(1,128)S(1)}, u32[]{:S(2)}, u32[]{:S(2)}) async-start(f32[128,1,768]{2,1,0:T(1,128)} %bitcast.7), calls=%async_computation.1 | async-start | bytes 786432 | tf_op jit(solution)/shard_map/all_to_all | solution.py:685
  52.3 17.6 %collective-permute-start.9 = (f32[18,2048]{1,0:T(8,128)S(1)}, f32[18,2048]{1,0:T(8,128)S(1)}, u32[]{:S(2)}, u32[]{:S(2)}) collective-permute-start(f32[18,2048]{1,0:T(8,128)S(1)} %copy-done.4), channel_id=1, source_target_pairs={{64,0},{65,63},{66,62},{67,61},{68,60},{69,59},{70,58},{71,57},{72... | collective-permute-start | bytes 442376 | tf_op jit(solution)/shard_map/ppermute | solution.py:754
  69.9 0.7 copy-start.12
  70.6 0.8 copy-start.5
  75.0 0.7 copy-start.3
  75.7 14.5 %copy-start.16 = (f32[48,256]{1,0:T(8,128)S(1)}, f32[48,256]{1,0:T(8,128)}, u32[]{:S(2)}) copy-start(f32[48,256]{1,0:T(8,128)} %get-tuple-element.34) | copy-start | bytes 147460
  75.7 18.1 %copy-start.15 = (f32[48,256]{1,0:T(8,128)S(1)}, f32[48,256]{1,0:T(8,128)}, u32[]{:S(2)}) copy-start(f32[48,256]{1,0:T(8,128)} %get-tuple-element.35) | copy-start | bytes 147460
  75.7 26.1 %copy-start.18 = (f32[64,128]{1,0:T(8,128)S(1)}, f32[64,128]{1,0:T(8,128)}, u32[]{:S(2)}) copy-start(f32[64,128]{1,0:T(8,128)} %get-tuple-element.36) | copy-start | bytes 98308
  75.7 27.6 %copy-start.17 = (f32[64,128]{1,0:T(8,128)S(1)}, f32[64,128]{1,0:T(8,128)}, u32[]{:S(2)}) copy-start(f32[64,128]{1,0:T(8,128)} %get-tuple-element.37) | copy-start | bytes 98308
  80.5 33.7 %all-to-all-start.2 = ((f32[128,8,128]{2,1,0:T(8,128)}), f32[128,8,128]{2,1,0:T(8,128)S(1)}, u32[]{:S(2)}, u32[]{:S(2)}) async-start(f32[128,8,128]{2,1,0:T(8,128)} %bitcast.6), calls=%async_computation.2 | async-start | bytes 1048576 | tf_op jit(solution)/shard_map/all_to_all | solution.py:685
  90.2 17.4 %collective-permute-start.4 = (f32[48,256]{1,0:T(8,128)S(1)}, f32[48,256]{1,0:T(8,128)S(1)}, u32[]{:S(2)}, u32[]{:S(2)}) collective-permute-start(f32[48,256]{1,0:T(8,128)S(1)} %copy-done.16), channel_id=1, source_target_pairs={{0,4},{4,8},{8,12},{12,16},{16,20},{20,24},{24,28},{28,32},{32,36}... | collective-permute-start | bytes 147464 | tf_op jit(solution)/shard_map/ppermute | solution.py:675
  93.8 13.9 %collective-permute-start.5 = (f32[48,256]{1,0:T(8,128)S(1)}, f32[48,256]{1,0:T(8,128)S(1)}, u32[]{:S(2)}, u32[]{:S(2)}) collective-permute-start(f32[48,256]{1,0:T(8,128)S(1)} %copy-done.15), channel_id=1, source_target_pairs={{4,0},{8,4},{12,8},{16,12},{20,16},{24,20},{28,24},{32,28},{36,32}... | collective-permute-start | bytes 147464 | tf_op jit(solution)/shard_map/ppermute | solution.py:676
  101.8 2.8 %collective-permute-start.6 = (f32[64,128]{1,0:T(8,128)S(1)}, f32[64,128]{1,0:T(8,128)S(1)}, u32[]{:S(2)}, u32[]{:S(2)}) collective-permute-start(f32[64,128]{1,0:T(8,128)S(1)} %copy-done.18), channel_id=1, source_target_pairs={{0,1},{1,2},{2,3},{4,5},{5,6},{6,7},{8,9},{9,10},{10,11},{12,13},{... | collective-permute-start | bytes 98312 | tf_op jit(solution)/shard_map/ppermute | solution.py:679
  103.3 4.3 %collective-permute-start.7 = (f32[64,128]{1,0:T(8,128)S(1)}, f32[64,128]{1,0:T(8,128)S(1)}, u32[]{:S(2)}, u32[]{:S(2)}) collective-permute-start(f32[64,128]{1,0:T(8,128)S(1)} %copy-done.17), channel_id=1, source_target_pairs={{1,0},{2,1},{3,2},{5,4},{6,5},{7,6},{9,8},{10,9},{11,10},{13,12},{... | collective-permute-start | bytes 98312 | tf_op jit(solution)/shard_map/ppermute | solution.py:680
  104.6 3.1 %copy-start.8 = (f32[64,128]{1,0:T(8,128)}, f32[64,128]{1,0:T(8,128)S(1)}, u32[]{:S(2)}) copy-start(f32[64,128]{1,0:T(8,128)S(1)} %collective-permute-done.6.refs_8_.left_ref) | copy-start | bytes 98308
  107.7 0.6 copy-start.9
  107.7 0.6 copy-start.6
  107.7 0.7 copy-start.7
  114.2 0.8 copy-start
  118.5 12.0 %all-to-all-start.3 = ((f32[4,224,128]{2,1,0:T(8,128)}), f32[4,224,128]{2,1,0:T(8,128)S(1)}, u32[]{:S(2)}, u32[]{:S(2)}) async-start(f32[4,224,128]{2,1,0:T(8,128)} %undip.1.refs_12_), calls=%async_computation.3 | async-start | bytes 917504 | tf_op jit(solution)/shard_map/all_to_all | solution.py:685
  130.5 0.8 copy-start.1

commit v3 on v2

--- a/solution.py
+++ b/solution.py
@@ -640,24 +640,31 @@
 
 
 def full(shape):
-    zeros = (0,) * len(shape)
-    return pl.BlockSpec(shape, lambda *_: zeros)
+    del shape
+    return pl.BlockSpec(memory_space=pltpu.VMEM)
 
 
 SMEM = pl.BlockSpec(memory_space=pltpu.SMEM)
+
+
+def in_hbm(x):
+    return pltpu.with_memory_space_constraint(x, pltpu.HBM)
+
+
+def hbm_shape(*shape):
+    return pltpu.HBM(shape, F32)
 
 
 def shape_of(*shape):
     return jax.ShapeDtypeStruct(shape, F32)
 
 
-def call(body, out_shape, args, smem=0, scratch=(), after=(), name=None):
+def call(body, out_shape, args, smem=0, scratch=(), after=(), name=None, limit=16 << 20):
     outs = out_shape if isinstance(out_shape, (tuple, list)) else [out_shape]
     size = sum(math.prod(x.shape) * 4 for x in list(args) + list(outs))
     out_specs = [full(x.shape) for x in outs]
     return pl.pallas_call(
         body,
-        grid=(1,),
         in_specs=[SMEM] * smem
         + [full(x.shape) for x in args[smem:]]
         + [pl.BlockSpec(memory_space=pl.ANY)] * len(after),
@@ -665,6 +672,7 @@
         out_shape=out_shape,
         scratch_shapes=scratch,
         cost_estimate=pl.CostEstimate(flops=0, bytes_accessed=size, transcendentals=0),
+        compiler_params=pltpu.CompilerParams(vmem_limit_bytes=limit),
         name=name,
     )(*args, *after)
 
@@ -700,6 +708,7 @@
     halo_specs = [full((48, 256))] * 2 + [full((64, 128))] * 2
     any_spec = pl.BlockSpec(memory_space=pl.ANY)
     t = TABLES
+    u, v, region, history, kernel = (in_hbm(x) for x in (u, v, region, history, kernel))
 
     first, last, left, right, plastic = pl.pallas_call(
         edges_kernel,
@@ -708,7 +717,8 @@
         out_specs=[full(s.shape) for s in edge_shapes] + [full((64, 256))],
         out_shape=edge_shapes + [shape_of(64, 256)],
         cost_estimate=pl.CostEstimate(flops=0, bytes_accessed=3300000, transcendentals=0),
-        name="edges",
+        compiler_params=pltpu.CompilerParams(vmem_limit_bytes=16 << 20),
+            name="edges",
     )(u, flags)
     halo_one = halo(first, last, left, right)
 
@@ -732,9 +742,10 @@
                 pl.BlockSpec((72, width), lambda i: (0, i + shift)),
                 pl.BlockSpec((18, width), lambda i: (0, i + shift)),
             ],
-            out_shape=[shape_of(72, 2048), shape_of(72, 2048), shape_of(18, 2048)],
+            out_shape=[hbm_shape(72, 2048), hbm_shape(72, 2048), hbm_shape(18, 2048)],
             input_output_aliases={3: 0, 4: 1, 5: 2} if given else {},
             cost_estimate=pl.CostEstimate(flops=0, bytes_accessed=5500000, transcendentals=0),
+            compiler_params=pltpu.CompilerParams(vmem_limit_bytes=16 << 20),
             name="history",
         )(where, kernel, history, *given)
 
@@ -746,7 +757,8 @@
         out_specs=full((4, 192, 128)),
         out_shape=shape_of(4, 192, 128),
         cost_estimate=pl.CostEstimate(flops=0, bytes_accessed=1500000, transcendentals=0),
-        name="slip",
+        compiler_params=pltpu.CompilerParams(vmem_limit_bytes=16 << 20),
+            name="slip",
     )(shear, yields, u, v, region, plastic, *halo_one, partial[2])
     lines = exchange(send, "narrow")
     own, main, edge = sums(1, partial)
@@ -766,10 +778,12 @@
         + halo_specs
         + [any_spec],
         out_specs=[planes(PLANES)] * 2 + [full(s.shape) for s in edge_shapes],
-        out_shape=[shape_of(3, 16, 64, 256)] * 2 + edge_shapes,
+        out_shape=[hbm_shape(3, 16, 64, 256)] * 2 + edge_shapes,
         cost_estimate=pl.CostEstimate(flops=0, bytes_accessed=14000000, transcendentals=0),
-        name="step_one",
+        compiler_params=pltpu.CompilerParams(vmem_limit_bytes=24 << 20),
+            name="step_one",
     )(shear, yields, u, v, region, plastic, *halo_one, send)
+    new_u, new_v = in_hbm(new_u), in_hbm(new_v)
     halo_two = halo(first, last, left, right)
 
     coefficients = call(
@@ -803,11 +817,12 @@
             + halo_specs
             + [any_spec] * (len(given) + 1),
             out_specs=[planes(PLANES, start)] * 2,
-            out_shape=[shape_of(3, 16, 64, 256)] * 2,
+            out_shape=[hbm_shape(3, 16, 64, 256)] * 2,
             input_output_aliases={10: 0, 11: 1} if given else {},
             cost_estimate=pl.CostEstimate(
                 flops=0, bytes_accessed=(stop - start) * 800000, transcendentals=0
             ),
+            compiler_params=pltpu.CompilerParams(vmem_limit_bytes=24 << 20),
             name="step_two",
         )(shear, yields, new_u, new_v, region, plastic, *halo_two, *given, after)
 
@@ -830,10 +845,11 @@
             + [full((4, 224, 128))]
             + [any_spec] * 2,
             out_specs=[near(2)] * 2,
-            out_shape=[shape_of(3, 16, 64, 256)] * 2,
+            out_shape=[hbm_shape(3, 16, 64, 256)] * 2,
             scratch_shapes=[pltpu.VMEM((3, 64, 256), F32)],
             input_output_aliases={11: 0, 12: 1},
             cost_estimate=pl.CostEstimate(flops=0, bytes_accessed=4000000, transcendentals=0),
+            compiler_params=pltpu.CompilerParams(vmem_limit_bytes=16 << 20),
             name="last",
         )(shear, yields, new_u, new_v, region, plastic, *halo_two, tractions, *out)
     )

time: 135 us -> 128 us (0.948)
  Pallas kernels: 60.6 us -> 52.9 us
    pallas_call x4, Pallas kernels: 15 us -> 8.45 us  [call(): pl.pallas_call(body, in_specs=[SMEM] * smem + [full(x.shape) for x in arg...]
    unnamed x38 -> x46, local copies, waits for them, and re-layouts: 5.84 us -> 6.74 us
  transfers between devices with their start and end apart: 14 -> 14, of which waited for: 2 -> 2; matrix products, arithmetic and copies ran while one was open for 0% -> 0% of each run, Pallas kernels for 32% -> 31%
where the time goes in v3:
time: 128 us; the launch traced here: 127 us
  starting transfers between devices  60.3 us (47%)
  Pallas kernels  52.9 us (41%)
  local copies, waits for them, and re-layouts  6.74 us (5%)
  waiting for transfers between devices  5.98 us (5%)
    all_to_all x4, starting transfers between devices, exchange(): return lax.all_to_all(x, axis, split_axis=0, concat_axis=0, tiled=True)  24.4 us
    ppermute x2, starting transfers between devices, halo(): bottom = lax.ppermute(first, 'wide', down)  15.8 us
    pallas_call x1, Pallas kernels, body(): pl.pallas_call(step_one_kernel, grid=(16 // PLANES,), in_specs=[SMEM, SME...  14.3 us
    pallas_call x2, Pallas kernels, later(): pl.pallas_call(functools.partial(step_two_kernel, start), grid=((stop - s...  11.1 us
    pallas_call x2, Pallas kernels, sums(): pl.pallas_call(history_kernel, grid=(steps,), in_specs=[SMEM, pl.BlockSpe...  11 us
    pallas_call x4, Pallas kernels, call(): pl.pallas_call(body, in_specs=[SMEM] * smem + [full(x.shape) for x in arg...  8.45 us
    ppermute x2, starting transfers between devices, halo(): top = lax.ppermute(last, 'wide', up)  7.35 us
    unnamed x46, local copies, waits for them, and re-layouts  6.74 us
  transfers between devices with their start and end apart: 14, of which 2 were waited for; matrix products, arithmetic and copies ran while one was open for 0% of the time, Pallas kernels for 31%

profile of v3, /device:TPU:4, one launch (start us, length us, event | category | flops | bytes accessed | tf_op | source)
XLA Modules:
  0.0 127.1 jit_solution(7966693851550339652)
XLA Ops:
  0.6 0.0 copy-start.18
  0.6 0.7 copy-done.18
  1.3 3.5 %edges.1 = (f32[48,256]{1,0:T(8,128)S(1)}, f32[48,256]{1,0:T(8,128)S(1)}, f32[64,128]{1,0:T(8,128)S(1)}, f32[64,128]{1,0:T(8,128)S(1)}, f32[64,256]{1,0:T(8,128)S(1)}) custom-call(f32[3,16,64,256]{3,2,1,0:T(8,128)} %u_ref.5, s32[8,32]{1,0:T(8,128)S(1)} %copy-done.18), custom_call_target="tpu_custom_call" | custom-call | bytes 3300000 | tf_op jit(solution)/shard_map/edges/pallas_call | solution.py:713
  4.8 1.7 %collective-permute-start.2 = (f32[64,128]{1,0:T(8,128)S(1)}, f32[64,128]{1,0:T(8,128)S(1)}, u32[]{:S(2)}, u32[]{:S(2)}) collective-permute-start(f32[64,128]{1,0:T(8,128)S(1)} %get-tuple-element.26), channel_id=1, source_target_pairs={{0,1},{1,2},{2,3},{4,5},{5,6},{6,7},{8,9},{9,10},{10,11},{12,13},{... | collective-permute-start | bytes 98312 | tf_op jit(solution)/shard_map/ppermute | solution.py:687
  6.5 1.3 %collective-permute-start.3 = (f32[64,128]{1,0:T(8,128)S(1)}, f32[64,128]{1,0:T(8,128)S(1)}, u32[]{:S(2)}, u32[]{:S(2)}) collective-permute-start(f32[64,128]{1,0:T(8,128)S(1)} %get-tuple-element.27), channel_id=1, source_target_pairs={{1,0},{2,1},{3,2},{5,4},{6,5},{7,6},{9,8},{10,9},{11,10},{13,12},{... | collective-permute-start | bytes 98312 | tf_op jit(solution)/shard_map/ppermute | solution.py:688
  7.8 3.8 %collective-permute-start = (f32[48,256]{1,0:T(8,128)S(1)}, f32[48,256]{1,0:T(8,128)S(1)}, u32[]{:S(2)}, u32[]{:S(2)}) collective-permute-start(f32[48,256]{1,0:T(8,128)S(1)} %get-tuple-element.24), channel_id=1, source_target_pairs={{0,4},{4,8},{8,12},{12,16},{16,20},{20,24},{24,28},{28,32},{32,36}... | collective-permute-start | bytes 147464 | tf_op jit(solution)/shard_map/ppermute | solution.py:683
  11.7 7.7 %collective-permute-start.1 = (f32[48,256]{1,0:T(8,128)S(1)}, f32[48,256]{1,0:T(8,128)S(1)}, u32[]{:S(2)}, u32[]{:S(2)}) collective-permute-start(f32[48,256]{1,0:T(8,128)S(1)} %get-tuple-element.25), channel_id=1, source_target_pairs={{4,0},{8,4},{12,8},{16,12},{20,16},{24,20},{28,24},{32,28},{36,32}... | collective-permute-start | bytes 147464 | tf_op jit(solution)/shard_map/ppermute | solution.py:684
  19.4 0.1 add_convert_fusion.where_ref
  19.5 5.5 %history.2 = (f32[72,2048]{1,0:T(8,128)}, f32[72,2048]{1,0:T(8,128)}, f32[18,2048]{1,0:T(8,128)}) custom-call(s32[2]{0:T(128)S(1)} %add_convert_fusion.where_ref, bf16[33,3,8,2048]{3,2,1,0:T(8,128)(2,1)} %kernel_ref.3, bf16[32,2,3,8,2048]{4,3,2,1,0:T(8,128)(2,1)} %history_ref.3), custom_call_target="tpu_custom_call" | custom-call | bytes 5500000 | tf_op jit(solution)/shard_map/history/pallas_call | solution.py:731
  25.0 0.0 collective-permute-done.2.left_ref
  25.0 0.0 collective-permute-done.3.right_ref
  25.0 0.0 collective-permute-done.top_ref
  25.0 0.0 collective-permute-done.1.bottom_ref
  25.0 0.0 copy-done.16
  25.0 0.0 copy-done.17
  25.0 0.0 copy-start.4
  25.0 0.9 copy-done.4
  26.0 2.1 %slip.1 = f32[4,192,128]{2,1,0:T(8,128)} custom-call(f32[4]{0:T(128)S(1)} %copy-done.16, f32[4]{0:T(128)S(1)} %copy-done.17, f32[3,16,64,256]{3,2,1,0:T(8,128)} %u_ref.5, f32[3,16,64,256]{3,2,1,0:T(8,128)} %v_ref.3, s32[16,64,256]{2,1,0:T(8,128)} %region_ref.5, f32[64,256]{1,0:T(8,128)S(1)} %get-tuple-element.23.plastic_ref.refs_5_, ...), custom_call_target="tpu_custom_call" | custom-call | bytes 1500000 | tf_op jit(solution)/shard_map/slip/pallas_call | solution.py:753
  28.0 5.0 %all-to-all-start = ((f32[4,192,128]{2,1,0:T(8,128)}), f32[4,192,128]{2,1,0:T(8,128)S(1)}, u32[]{:S(2)}, u32[]{:S(2)}) async-start(f32[4,192,128]{2,1,0:T(8,128)} %slip.1), calls=%async_computation | async-start | bytes 786432 | tf_op jit(solution)/shard_map/all_to_all | solution.py:693
  33.0 5.5 %history.3 = (f32[72,2048]{1,0:T(8,128)}, f32[72,2048]{1,0:T(8,128)}, f32[18,2048]{1,0:T(8,128)}) custom-call(s32[2]{0:T(128)S(1)} %add_convert_fusion.where_ref, bf16[33,3,8,2048]{3,2,1,0:T(8,128)(2,1)} %kernel_ref.3, bf16[32,2,3,8,2048]{4,3,2,1,0:T(8,128)(2,1)} %history_ref.3, ...), custom_call_target="tpu_custom_call", output_to_operand_aliasing={{0}: (3, {}), {1}: (4, {}), {2}: (5, {})} | custom-call | bytes 5500000 | tf_op jit(solution)/shard_map/history/pallas_call | solution.py:731
  38.6 3.9 %collective-permute-start.8 = (f32[72,2048]{1,0:T(8,128)}, f32[72,2048]{1,0:T(8,128)S(1)}, u32[]{:S(2)}, u32[]{:S(2)}) collective-permute-start(f32[72,2048]{1,0:T(8,128)} %get-tuple-element.38), channel_id=1, source_target_pairs={{0,127},{1,126},{2,125},{3,124},{4,123},{5,122},{6,121},{7,120},{8... | collective-permute-start | bytes 1769480 | tf_op jit(solution)/shard_map/ppermute | solution.py:765
  42.4 0.0 all-to-all-done.recv_ref
  42.4 0.0 copy-done.6
  42.4 0.0 copy-done.9
  42.4 0.0 copy-start.1
  42.5 1.1 copy-done.1
  43.5 1.9 %dip.1._after_ref = f32[768,128]{1,0:T(8,128)} custom-call(bf16[2,512,256]{2,1,0:T(8,128)(2,1)S(1)} %copy-done.6, f32[2,2,128,128]{3,2,1,0:T(8,128)S(1)} %copy-done.10, bf16[2,2,136,256]{3,2,1,0:T(8,128)(2,1)S(1)} %copy-done.9, f32[4,192,128]{2,1,0:T(8,128)S(1)} %all-to-all-done.recv_ref, f32[72,2048]{1,0:T(8,128)S(1)} %copy-done.1), custom_call_target="tpu_custom_call" | custom-call | bytes 2654208 | tf_op jit(solution)/shard_map/dip/pallas_call | solution.py:666
  45.4 5.8 %all-to-all-start.1 = ((f32[128,1,768]{2,1,0:T(1,128)}), f32[128,1,768]{2,1,0:T(1,128)S(1)}, u32[]{:S(2)}, u32[]{:S(2)}) async-start(f32[128,1,768]{2,1,0:T(1,128)} %bitcast.2), calls=%async_computation.1 | async-start | bytes 786432 | tf_op jit(solution)/shard_map/all_to_all | solution.py:693
  51.2 0.0 copy-start.2
  51.2 0.0 copy-start.14
  51.2 3.1 %collective-permute-start.9 = (f32[18,2048]{1,0:T(8,128)S(1)}, f32[18,2048]{1,0:T(8,128)S(1)}, u32[]{:S(2)}, u32[]{:S(2)}) collective-permute-start(f32[18,2048]{1,0:T(8,128)S(1)} %copy-done.5), channel_id=1, source_target_pairs={{64,0},{65,63},{66,62},{67,61},{68,60},{69,59},{70,58},{71,57},{72... | collective-permute-start | bytes 442376 | tf_op jit(solution)/shard_map/ppermute | solution.py:766
  54.3 14.3 %step_one.1 = (f32[3,16,64,256]{3,2,1,0:T(8,128)}, f32[3,16,64,256]{3,2,1,0:T(8,128)}, f32[48,256]{1,0:T(8,128)S(1)}, f32[48,256]{1,0:T(8,128)S(1)}, f32[64,128]{1,0:T(8,128)S(1)}, /*index=5*/f32[64,128]{1,0:T(8,128)S(1)}) custom-call(f32[4]{0:T(128)S(1)} %copy-done.16, f32[4]{0:T(128)S(1)} %copy-done.17, f32[3,16,64,256]{3,2,1,0:T(8,128)} %u_ref.5, ...), custom_call_target="tpu_custom_call" | custom-call | bytes 14000000 | tf_op jit(solution)/shard_map/step_one/pallas_call | solution.py:774
  68.6 0.6 copy-done.19
  69.2 0.6 copy-done.21
  69.8 0.0 collective-permute-done.9.edge_ref
  69.8 0.0 collective-permute-done.8.main_ref
  69.9 0.0 copy-done.2
  69.9 0.0 copy-done.14
  69.9 1.7 %mirror.1.coef_ref = f32[8,3,8,2048]{3,2,1,0:T(8,128)S(1)} custom-call(s32[2]{0:T(128)S(1)} %add_convert_fusion.where_ref, bf16[128,128]{1,0:T(8,128)(2,1)S(1)} %copy-done.14, f32[72,2048]{1,0:T(8,128)S(1)} %copy-done.2, f32[72,2048]{1,0:T(8,128)S(1)} %collective-permute-done.8.main_ref, f32[18,2048]{1,0:T(8,128)S(1)} %collective-permute-done.9.edge_ref), custom_call_target="tpu_custom_call" | custom-call | bytes 2965512 | tf_op jit(solution)/shard_map/mirror/pallas_call | solution.py:666
  71.6 0.0 all-to-all-done.1
  71.6 0.0 copy-start.15
  71.6 0.9 copy-done.15
  72.5 2.9 %strike.1.refs_10_ = f32[1024,128]{1,0:T(8,128)} custom-call(bf16[2,256,256]{2,1,0:T(8,128)(2,1)S(1)} %copy-done.3, f32[2,128,128]{2,1,0:T(8,128)S(1)} %copy-done.15, bf16[2,256,256]{2,1,0:T(8,128)(2,1)S(1)} %copy-done.13, bf16[128,128]{1,0:T(8,128)(2,1)S(1)} %copy-done.14, bf16[2,256,256]{2,1,0:T(8,128)(2,1)S(1)} %copy-done.12, ...), custom_call_target="tpu_custom_call" | custom-call | bytes 4784128 | tf_op jit(solution)/shard_map/strike/pallas_call | solution.py:666
  75.4 9.8 %all-to-all-start.2 = ((f32[128,8,128]{2,1,0:T(8,128)}), f32[128,8,128]{2,1,0:T(8,128)S(1)}, u32[]{:S(2)}, u32[]{:S(2)}) async-start(f32[128,8,128]{2,1,0:T(8,128)} %bitcast.4), calls=%async_computation.2 | async-start | bytes 1048576 | tf_op jit(solution)/shard_map/all_to_all | solution.py:693
  85.1 3.5 %collective-permute-start.4 = (f32[48,256]{1,0:T(8,128)S(1)}, f32[48,256]{1,0:T(8,128)S(1)}, u32[]{:S(2)}, u32[]{:S(2)}) collective-permute-start(f32[48,256]{1,0:T(8,128)S(1)} %get-tuple-element.34), channel_id=1, source_target_pairs={{0,4},{4,8},{8,12},{12,16},{16,20},{20,24},{24,28},{28,32},{32,36}... | collective-permute-start | bytes 147464 | tf_op jit(solution)/shard_map/ppermute | solution.py:683
  88.7 8.0 %collective-permute-start.5 = (f32[48,256]{1,0:T(8,128)S(1)}, f32[48,256]{1,0:T(8,128)S(1)}, u32[]{:S(2)}, u32[]{:S(2)}) collective-permute-start(f32[48,256]{1,0:T(8,128)S(1)} %get-tuple-element.35), channel_id=1, source_target_pairs={{4,0},{8,4},{12,8},{16,12},{20,16},{24,20},{28,24},{32,28},{36,32}... | collective-permute-start | bytes 147464 | tf_op jit(solution)/shard_map/ppermute | solution.py:684
  96.7 0.0 copy-done.22
  96.7 1.5 %collective-permute-start.6 = (f32[64,128]{1,0:T(8,128)S(1)}, f32[64,128]{1,0:T(8,128)S(1)}, u32[]{:S(2)}, u32[]{:S(2)}) collective-permute-start(f32[64,128]{1,0:T(8,128)S(1)} %copy-done.22), channel_id=1, source_target_pairs={{0,1},{1,2},{2,3},{4,5},{5,6},{6,7},{8,9},{9,10},{10,11},{12,13},{... | collective-permute-start | bytes 98312 | tf_op jit(solution)/shard_map/ppermute | solution.py:687
  98.2 1.3 %collective-permute-start.7 = (f32[64,128]{1,0:T(8,128)S(1)}, f32[64,128]{1,0:T(8,128)S(1)}, u32[]{:S(2)}, u32[]{:S(2)}) collective-permute-start(f32[64,128]{1,0:T(8,128)S(1)} %copy-done.20), channel_id=1, source_target_pairs={{1,0},{2,1},{3,2},{5,4},{6,5},{7,6},{9,8},{10,9},{11,10},{13,12},{... | collective-permute-start | bytes 98312 | tf_op jit(solution)/shard_map/ppermute | solution.py:688
  99.5 0.0 collective-permute-done.6.refs_8_.left_ref
  99.5 3.0 %collective-permute-done.7.refs_9_.right_ref = f32[64,128]{1,0:T(8,128)S(1)} collective-permute-done((f32[64,128]{1,0:T(8,128)S(1)}, f32[64,128]{1,0:T(8,128)S(1)}, u32[]{:S(2)}, u32[]{:S(2)}) %collective-permute-start.7) | collective-permute-done | bytes 32800 | tf_op jit(solution)/shard_map/ppermute | solution.py:688
  102.5 0.0 collective-permute-done.4.refs_6_.top_ref
  102.5 0.0 collective-permute-done.5.refs_7_.bottom_ref
  102.5 0.0 copy-start.8
  102.6 0.0 copy-start.11
  102.6 5.9 %step_two.2 = (f32[3,16,64,256]{3,2,1,0:T(8,128)}, f32[3,16,64,256]{3,2,1,0:T(8,128)}) custom-call(f32[4]{0:T(128)S(1)} %copy-done.16, f32[4]{0:T(128)S(1)} %copy-done.17, f32[3,16,64,256]{3,2,1,0:T(8,128)} %get-tuple-element.32._after_ref.refs_2_.u_ref, f32[3,16,64,256]{3,2,1,0:T(8,128)} %get-tuple-element.33.refs_3_.v_ref, s32[16,64,256]{2,1,0:T(8,128)} %region_ref.5, ...), custom_call_target="tpu_custom_call" | custom-call | bytes 6400000 | tf_op jit(solution)/shard_map/step_two/pallas_call | solution.py:811
  108.4 0.0 all-to-all-done.2
  108.5 0.0 copy-start
  108.5 1.9 %copy-done = f32[3,16,64,256]{3,2,1,0:T(8,128)S(1)} copy-done((f32[3,16,64,256]{3,2,1,0:T(8,128)S(1)}, f32[3,16,64,256]{3,2,1,0:T(8,128)}, u32[]{:S(2)}) %copy-start) | copy-done | bytes 3145752
  110.4 2.1 %undip.1.refs_12_ = f32[4,224,128]{2,1,0:T(8,128)} custom-call(bf16[2,256,512]{2,1,0:T(8,128)(2,1)S(1)} %copy-done.8, f32[2,2,128,128]{3,2,1,0:T(8,128)S(1)} %copy-done.11, bf16[2,256,512]{2,1,0:T(8,128)(2,1)S(1)} %copy-done.7, f32[1024,128]{1,0:T(8,128)S(1)} %bitcast.6, f32[3,16,64,256]{3,2,1,0:T(8,128)S(1)} %copy-done), custom_call_target="tpu_custom_call" | custom-call | bytes 3342336 | tf_op jit(solution)/shard_map/undip/pallas_call | solution.py:666
  112.4 3.9 %all-to-all-start.3 = ((f32[4,224,128]{2,1,0:T(8,128)}), f32[4,224,128]{2,1,0:T(8,128)S(1)}, u32[]{:S(2)}, u32[]{:S(2)}) async-start(f32[4,224,128]{2,1,0:T(8,128)} %undip.1.refs_12_), calls=%async_computation.3 | async-start | bytes 917504 | tf_op jit(solution)/shard_map/all_to_all | solution.py:693
  116.3 5.2 %step_two.3 = (f32[3,16,64,256]{3,2,1,0:T(8,128)}, f32[3,16,64,256]{3,2,1,0:T(8,128)}) custom-call(f32[4]{0:T(128)S(1)} %copy-done.16, f32[4]{0:T(128)S(1)} %copy-done.17, f32[3,16,64,256]{3,2,1,0:T(8,128)} %get-tuple-element.32._after_ref.refs_2_.u_ref, ...), custom_call_target="tpu_custom_call", output_to_operand_aliasing={{0}: (10, {}), {1}: (11, {})} | custom-call | bytes 4800000 | tf_op jit(solution)/shard_map/step_two/pallas_call | solution.py:811
  121.5 2.9 %all-to-all-done.3.recv_ref = f32[4,224,128]{2,1,0:T(8,128)S(1)} async-done(((f32[4,224,128]{2,1,0:T(8,128)}), f32[4,224,128]{2,1,0:T(8,128)S(1)}, u32[]{:S(2)}, u32[]{:S(2)}) %all-to-all-start.3) | async-done | bytes 458784 | tf_op jit(solution)/shard_map/all_to_all | solution.py:693
  124.5 2.6 %last.1 = (f32[3,16,64,256]{3,2,1,0:T(8,128)}, f32[3,16,64,256]{3,2,1,0:T(8,128)}) custom-call(f32[4]{0:T(128)S(1)} %copy-done.16, f32[4]{0:T(128)S(1)} %copy-done.17, f32[3,16,64,256]{3,2,1,0:T(8,128)} %get-tuple-element.32._after_ref.refs_2_.u_ref, ...), custom_call_target="tpu_custom_call", output_to_operand_aliasing={{0}: (11, {}), {1}: (12, {})} | custom-call | bytes 4000000 | tf_op jit(solution)/shard_map/last/pallas_call | solution.py:840
  (23 shorter events, 0.0 us)
Async XLA Ops:
  0.6 0.7 copy-start.18
  4.8 20.2 %collective-permute-start.2 = (f32[64,128]{1,0:T(8,128)S(1)}, f32[64,128]{1,0:T(8,128)S(1)}, u32[]{:S(2)}, u32[]{:S(2)}) collective-permute-start(f32[64,128]{1,0:T(8,128)S(1)} %get-tuple-element.26), channel_id=1, source_target_pairs={{0,1},{1,2},{2,3},{4,5},{5,6},{6,7},{8,9},{9,10},{10,11},{12,13},{... | collective-permute-start | bytes 98312 | tf_op jit(solution)/shard_map/ppermute | solution.py:687
  6.5 18.4 %collective-permute-start.3 = (f32[64,128]{1,0:T(8,128)S(1)}, f32[64,128]{1,0:T(8,128)S(1)}, u32[]{:S(2)}, u32[]{:S(2)}) collective-permute-start(f32[64,128]{1,0:T(8,128)S(1)} %get-tuple-element.27), channel_id=1, source_target_pairs={{1,0},{2,1},{3,2},{5,4},{6,5},{7,6},{9,8},{10,9},{11,10},{13,12},{... | collective-permute-start | bytes 98312 | tf_op jit(solution)/shard_map/ppermute | solution.py:688
  7.8 17.2 %collective-permute-start = (f32[48,256]{1,0:T(8,128)S(1)}, f32[48,256]{1,0:T(8,128)S(1)}, u32[]{:S(2)}, u32[]{:S(2)}) collective-permute-start(f32[48,256]{1,0:T(8,128)S(1)} %get-tuple-element.24), channel_id=1, source_target_pairs={{0,4},{4,8},{8,12},{12,16},{16,20},{20,24},{24,28},{28,32},{32,36}... | collective-permute-start | bytes 147464 | tf_op jit(solution)/shard_map/ppermute | solution.py:683
  11.7 13.3 %collective-permute-start.1 = (f32[48,256]{1,0:T(8,128)S(1)}, f32[48,256]{1,0:T(8,128)S(1)}, u32[]{:S(2)}, u32[]{:S(2)}) collective-permute-start(f32[48,256]{1,0:T(8,128)S(1)} %get-tuple-element.25), channel_id=1, source_target_pairs={{4,0},{8,4},{12,8},{16,12},{20,16},{24,20},{28,24},{32,28},{36,32}... | collective-permute-start | bytes 147464 | tf_op jit(solution)/shard_map/ppermute | solution.py:684
  19.5 5.5 %copy-start.16 = (f32[4]{0:T(128)S(1)}, f32[4]{0:T(128)}, u32[]{:S(2)}) copy-start(f32[4]{0:T(128)} %shear_ref.5) | copy-start | bytes 52
  19.5 5.5 %copy-start.17 = (f32[4]{0:T(128)S(1)}, f32[4]{0:T(128)}, u32[]{:S(2)}) copy-start(f32[4]{0:T(128)} %yields_ref.5) | copy-start | bytes 52
  25.0 0.9 copy-start.4
  28.0 14.4 %all-to-all-start = ((f32[4,192,128]{2,1,0:T(8,128)}), f32[4,192,128]{2,1,0:T(8,128)S(1)}, u32[]{:S(2)}, u32[]{:S(2)}) async-start(f32[4,192,128]{2,1,0:T(8,128)} %slip.1), calls=%async_computation | async-start | bytes 786432 | tf_op jit(solution)/shard_map/all_to_all | solution.py:693
  33.0 9.4 %copy-start.6 = (bf16[2,512,256]{2,1,0:T(8,128)(2,1)S(1)}, bf16[2,512,256]{2,1,0:T(8,128)(2,1)}, u32[]{:S(2)}) copy-start(bf16[2,512,256]{2,1,0:T(8,128)(2,1)} %constant.37.clone.radix_ref) | copy-start | bytes 1572868
  33.0 9.4 %copy-start.9 = (bf16[2,2,136,256]{3,2,1,0:T(8,128)(2,1)S(1)}, bf16[2,2,136,256]{3,2,1,0:T(8,128)(2,1)}, u32[]{:S(2)}) copy-start(bf16[2,2,136,256]{3,2,1,0:T(8,128)(2,1)} %constant.39.clone.out_table_ref) | copy-start | bytes 835588
  33.0 9.4 %copy-start.10 = (f32[2,2,128,128]{3,2,1,0:T(8,128)S(1)}, f32[2,2,128,128]{3,2,1,0:T(8,128)}, u32[]{:S(2)}) copy-start(f32[2,2,128,128]{3,2,1,0:T(8,128)} %constant.38.clone.turn_ref) | copy-start | bytes 786436
  38.6 31.3 %collective-permute-start.8 = (f32[72,2048]{1,0:T(8,128)}, f32[72,2048]{1,0:T(8,128)S(1)}, u32[]{:S(2)}, u32[]{:S(2)}) collective-permute-start(f32[72,2048]{1,0:T(8,128)} %get-tuple-element.38), channel_id=1, source_target_pairs={{0,127},{1,126},{2,125},{3,124},{4,123},{5,122},{6,121},{7,120},{8... | collective-permute-start | bytes 1769480 | tf_op jit(solution)/shard_map/ppermute | solution.py:765
  42.4 1.1 copy-start.1
  43.5 7.6 %copy-start.5 = (f32[18,2048]{1,0:T(8,128)S(1)}, f32[18,2048]{1,0:T(8,128)}, u32[]{:S(2)}) copy-start(f32[18,2048]{1,0:T(8,128)} %get-tuple-element.39) | copy-start | bytes 442372
  45.4 26.2 %all-to-all-start.1 = ((f32[128,1,768]{2,1,0:T(1,128)}), f32[128,1,768]{2,1,0:T(1,128)S(1)}, u32[]{:S(2)}, u32[]{:S(2)}) async-start(f32[128,1,768]{2,1,0:T(1,128)} %bitcast.2), calls=%async_computation.1 | async-start | bytes 786432 | tf_op jit(solution)/shard_map/all_to_all | solution.py:693
  51.2 18.7 %copy-start.2 = (f32[72,2048]{1,0:T(8,128)S(1)}, f32[72,2048]{1,0:T(8,128)}, u32[]{:S(2)}) copy-start(f32[72,2048]{1,0:T(8,128)} %get-tuple-element.31._after_ref.own_ref) | copy-start | bytes 1769476
  51.2 18.7 %copy-start.14 = (bf16[128,128]{1,0:T(8,128)(2,1)S(1)}, bf16[128,128]{1,0:T(8,128)(2,1)}, u32[]{:S(2)}) copy-start(bf16[128,128]{1,0:T(8,128)(2,1)} %constant.40.clone.reverse_ref) | copy-start | bytes 98308
  51.2 18.7 %collective-permute-start.9 = (f32[18,2048]{1,0:T(8,128)S(1)}, f32[18,2048]{1,0:T(8,128)S(1)}, u32[]{:S(2)}, u32[]{:S(2)}) collective-permute-start(f32[18,2048]{1,0:T(8,128)S(1)} %copy-done.5), channel_id=1, source_target_pairs={{64,0},{65,63},{66,62},{67,61},{68,60},{69,59},{70,58},{71,57},{72... | collective-permute-start | bytes 442376 | tf_op jit(solution)/shard_map/ppermute | solution.py:766
  68.6 0.6 copy-start.19
  69.2 0.6 copy-start.21
  69.8 1.7 %copy-start.3 = (bf16[2,256,256]{2,1,0:T(8,128)(2,1)S(1)}, bf16[2,256,256]{2,1,0:T(8,128)(2,1)}, u32[]{:S(2)}) copy-start(bf16[2,256,256]{2,1,0:T(8,128)(2,1)} %constant.41.clone.in_ref.out_table_ref) | copy-start | bytes 786436
  69.8 1.7 %copy-start.12 = (bf16[2,256,256]{2,1,0:T(8,128)(2,1)S(1)}, bf16[2,256,256]{2,1,0:T(8,128)(2,1)}, u32[]{:S(2)}) copy-start(bf16[2,256,256]{2,1,0:T(8,128)(2,1)} %constant.44.clone.unmix_ref) | copy-start | bytes 786436
  69.8 1.7 %copy-start.13 = (bf16[2,256,256]{2,1,0:T(8,128)(2,1)S(1)}, bf16[2,256,256]{2,1,0:T(8,128)(2,1)}, u32[]{:S(2)}) copy-start(bf16[2,256,256]{2,1,0:T(8,128)(2,1)} %constant.43.clone.mix_ref) | copy-start | bytes 786436
  71.6 0.9 copy-start.15
  72.5 24.2 %copy-start.22 = (f32[64,128]{1,0:T(8,128)S(1)}, f32[64,128]{1,0:T(8,128)}, u32[]{:S(2)}) copy-start(f32[64,128]{1,0:T(8,128)} %copy-done.21) | copy-start | bytes 98308
  72.5 25.7 %copy-start.20 = (f32[64,128]{1,0:T(8,128)S(1)}, f32[64,128]{1,0:T(8,128)}, u32[]{:S(2)}) copy-start(f32[64,128]{1,0:T(8,128)} %copy-done.19) | copy-start | bytes 98308
  75.4 33.1 %all-to-all-start.2 = ((f32[128,8,128]{2,1,0:T(8,128)}), f32[128,8,128]{2,1,0:T(8,128)S(1)}, u32[]{:S(2)}, u32[]{:S(2)}) async-start(f32[128,8,128]{2,1,0:T(8,128)} %bitcast.4), calls=%async_computation.2 | async-start | bytes 1048576 | tf_op jit(solution)/shard_map/all_to_all | solution.py:693
  85.1 17.4 %collective-permute-start.4 = (f32[48,256]{1,0:T(8,128)S(1)}, f32[48,256]{1,0:T(8,128)S(1)}, u32[]{:S(2)}, u32[]{:S(2)}) collective-permute-start(f32[48,256]{1,0:T(8,128)S(1)} %get-tuple-element.34), channel_id=1, source_target_pairs={{0,4},{4,8},{8,12},{12,16},{16,20},{20,24},{24,28},{28,32},{32,36}... | collective-permute-start | bytes 147464 | tf_op jit(solution)/shard_map/ppermute | solution.py:683
  88.7 13.9 %collective-permute-start.5 = (f32[48,256]{1,0:T(8,128)S(1)}, f32[48,256]{1,0:T(8,128)S(1)}, u32[]{:S(2)}, u32[]{:S(2)}) collective-permute-start(f32[48,256]{1,0:T(8,128)S(1)} %get-tuple-element.35), channel_id=1, source_target_pairs={{4,0},{8,4},{12,8},{16,12},{20,16},{24,20},{28,24},{32,28},{36,32}... | collective-permute-start | bytes 147464 | tf_op jit(solution)/shard_map/ppermute | solution.py:684
  96.7 2.8 %collective-permute-start.6 = (f32[64,128]{1,0:T(8,128)S(1)}, f32[64,128]{1,0:T(8,128)S(1)}, u32[]{:S(2)}, u32[]{:S(2)}) collective-permute-start(f32[64,128]{1,0:T(8,128)S(1)} %copy-done.22), channel_id=1, source_target_pairs={{0,1},{1,2},{2,3},{4,5},{5,6},{6,7},{8,9},{9,10},{10,11},{12,13},{... | collective-permute-start | bytes 98312 | tf_op jit(solution)/shard_map/ppermute | solution.py:687
  98.2 4.3 %collective-permute-start.7 = (f32[64,128]{1,0:T(8,128)S(1)}, f32[64,128]{1,0:T(8,128)S(1)}, u32[]{:S(2)}, u32[]{:S(2)}) collective-permute-start(f32[64,128]{1,0:T(8,128)S(1)} %copy-done.20), channel_id=1, source_target_pairs={{1,0},{2,1},{3,2},{5,4},{6,5},{7,6},{9,8},{10,9},{11,10},{13,12},{... | collective-permute-start | bytes 98312 | tf_op jit(solution)/shard_map/ppermute | solution.py:688
  102.5 5.9 %copy-start.7 = (bf16[2,256,512]{2,1,0:T(8,128)(2,1)S(1)}, bf16[2,256,512]{2,1,0:T(8,128)(2,1)}, u32[]{:S(2)}) copy-start(bf16[2,256,512]{2,1,0:T(8,128)(2,1)} %constant.47.clone.unradix_ref) | copy-start | bytes 1572868
  102.5 5.9 %copy-start.8 = (bf16[2,256,512]{2,1,0:T(8,128)(2,1)S(1)}, bf16[2,256,512]{2,1,0:T(8,128)(2,1)}, u32[]{:S(2)}) copy-start(bf16[2,256,512]{2,1,0:T(8,128)(2,1)} %constant.45.clone.in_ref) | copy-start | bytes 1572868
  102.6 5.9 %copy-start.11 = (f32[2,2,128,128]{3,2,1,0:T(8,128)S(1)}, f32[2,2,128,128]{3,2,1,0:T(8,128)}, u32[]{:S(2)}) copy-start(f32[2,2,128,128]{3,2,1,0:T(8,128)} %constant.46.clone.turn_ref) | copy-start | bytes 786436
  108.5 1.9 %copy-start = (f32[3,16,64,256]{3,2,1,0:T(8,128)S(1)}, f32[3,16,64,256]{3,2,1,0:T(8,128)}, u32[]{:S(2)}) copy-start(f32[3,16,64,256]{3,2,1,0:T(8,128)} %get-tuple-element.40._after_ref.refs_10_) | copy-start | bytes 9437188
  112.4 12.0 %all-to-all-start.3 = ((f32[4,224,128]{2,1,0:T(8,128)}), f32[4,224,128]{2,1,0:T(8,128)S(1)}, u32[]{:S(2)}, u32[]{:S(2)}) async-start(f32[4,224,128]{2,1,0:T(8,128)} %undip.1.refs_12_), calls=%async_computation.3 | async-start | bytes 917504 | tf_op jit(solution)/shard_map/all_to_all | solution.py:693

commit v4 on v3

--- a/solution.py
+++ b/solution.py
@@ -139,21 +139,32 @@
     return total
 
 
-def strip_force(centers, sums, region, plastic, shear_ref, yields_ref):
+def label_table(shear_ref, yields_ref):
     one = jnp.ones((8, 128), F32)
-    wide = lambda x: jnp.concatenate([x, x], 1)
-    modulus = wide(one * shear_ref[0])
-    level = one * yields_ref[0]
-    level = wide(1.0 / (level * level))
+    ratios = []
+    for label in range(4):
+        ratio = (one * shear_ref[label]) / (one * yields_ref[label])
+        ratios.append(ratio * ratio)
+    return [shear_ref[label] for label in range(4)], ratios
+
+
+def force_scale(laplace, region, plastic, table):
+    shears, ratios = table
+    repeats = (region.shape[0] // 8, region.shape[1] // 128)
+    modulus = jnp.full(region.shape, shears[0], F32)
+    ratio = jnp.tile(ratios[0], repeats)
     for label in range(1, 4):
-        modulus = jnp.where(region == label, shear_ref[label], modulus)
-        other = one * yields_ref[label]
-        level = jnp.where(region == label, wide(1.0 / (other * other)), level)
-    force = [modulus * (total - 6.0 * center) for total, center in zip(sums, centers)]
-    squares = force[0] * force[0] + force[1] * force[1] + force[2] * force[2]
-    capped = lax.rsqrt(1.0 + squares * level)
-    scaling = jnp.where(plastic > 0.5, capped, 1.0)
-    return [f * scaling for f in force]
+        modulus = jnp.where(region == label, shears[label], modulus)
+        ratio = jnp.where(region == label, jnp.tile(ratios[label], repeats), ratio)
+    squares = laplace[0] * laplace[0] + laplace[1] * laplace[1] + laplace[2] * laplace[2]
+    capped = lax.rsqrt(1.0 + squares * ratio)
+    return modulus * jnp.where(plastic > 0.5, capped, 1.0)
+
+
+def strip_force(centers, sums, region, plastic, table):
+    laplace = [total - 6.0 * center for total, center in zip(sums, centers)]
+    scale = force_scale(laplace, region, plastic, table)
+    return [scale * part for part in laplace]
 
 
 def strip_of(i):
@@ -189,18 +200,11 @@
     return c * 16 + z
 
 
-def put_columns(left_ref, right_ref, strip, i, place):
-    c0, c1 = strip[:, :128], strip[:, 128:]
-    lane = lanes(c0.shape)
-    rows = strip_of(i)
-    left_ref[rows, :] = jnp.where(lane == place, pltpu.roll(c0, place, 1), left_ref[rows, :])
-    right_ref[rows, :] = jnp.where(
-        lane == place, pltpu.roll(c1, lax.rem(place + 1, 128), 1), right_ref[rows, :]
-    )
-
-
-def edges_kernel(u_ref, flags_ref, first_ref, last_ref, left_ref, right_ref, plastic_ref):
+def edges_kernel(
+    u_ref, v_ref, region_ref, flags_ref, first_ref, last_ref, left_ref, right_ref, plastic_ref
+):
     step = pl.program_id(0)
+    depth = u_ref.shape[1]
 
     @pl.when(step == 0)
     def _():
@@ -209,23 +213,149 @@
         wide = (rows_of((64, 8)) // 8 == lanes((64, 8))).astype(F32)
         high = (rows_of((32, 256)) == lanes((32, 256)) // 8).astype(F32)
         marks = (flags_ref[...] == 1).astype(F32)
-        plastic_ref[...] = dot(dot(wide, marks), high)
-
-    for k in range(u_ref.shape[1]):
-        z = step * u_ref.shape[1] + k
+        plastic = dot(dot(wide, marks), high)
+        plastic_ref[...] = plastic
+        first_ref[160:168, :] = jnp.broadcast_to(plastic[0:1], (8, 256))
+        last_ref[160:168, :] = jnp.broadcast_to(plastic[63:64], (8, 256))
+        lane = lanes((64, 128))
+        left_ref[1] = jnp.where(lane == 64, pltpu.roll(plastic[:, :128], 64, 1), 0.0)
+        right_ref[1] = jnp.where(lane == 64, pltpu.roll(plastic[:, 128:], 65, 1), 0.0)
+
+    for k in range(depth):
+        z = step * depth + k
         for c in range(3):
             place = slot(c, z)
             first_ref[pl.ds(place, 1), :] = u_ref[c, k, 0:1, :]
             last_ref[pl.ds(place, 1), :] = u_ref[c, k, 63:64, :]
-            for i in range(8):
-                put_columns(left_ref, right_ref, u_ref[c, k, strip_of(i), :], i, place)
+            first_ref[pl.ds(48 + place, 1), :] = u_ref[c, k, 1:2, :]
+            last_ref[pl.ds(48 + place, 1), :] = u_ref[c, k, 62:63, :]
+            first_ref[pl.ds(96 + place, 1), :] = v_ref[c, k, 0:1, :]
+            last_ref[pl.ds(96 + place, 1), :] = v_ref[c, k, 63:64, :]
+        first_ref[pl.ds(144 + z, 1), :] = region_ref[k, 0:1, :].astype(F32)
+        last_ref[pl.ds(144 + z, 1), :] = region_ref[k, 63:64, :].astype(F32)
+    lane = lanes((8, 128))
+    for i in range(8):
+        rows = strip_of(i)
+        total = [left_ref[0, rows, :], left_ref[1, rows, :], right_ref[0, rows, :], right_ref[1, rows, :]]
+
+        def put(index, tile, source, target):
+            moved = pltpu.roll(tile, lax.rem(target + (128 - source), 128), 1)
+            total[index] = jnp.where(lane == target, moved, total[index])
+
+        for k in range(depth):
+            z = step * depth + k
+            for c in range(3):
+                place = slot(c, z)
+                u0, u1 = u_ref[c, k, rows, 0:128], u_ref[c, k, rows, 128:256]
+                put(0, u0, 0, place)
+                put(0, u0, 1, place + 48)
+                put(2, u1, 127, place)
+                put(2, u1, 126, place + 48)
+                put(1, v_ref[c, k, rows, 0:128], 0, place)
+                put(3, v_ref[c, k, rows, 128:256], 127, place)
+            put(1, region_ref[k, rows, 0:128].astype(F32), 0, z + 48)
+            put(3, region_ref[k, rows, 128:256].astype(F32), 127, z + 48)
+        left_ref[0, rows, :] = total[0]
+        left_ref[1, rows, :] = total[1]
+        right_ref[0, rows, :] = total[2]
+        right_ref[1, rows, :] = total[3]
+
+
+def beside_kernel(
+    where_ref, shear_ref, yields_ref, first_ref, last_ref, left_ref, right_ref,
+    top_ref, bottom_ref, west_ref, east_ref, lines_ref,
+    new_top_ref, new_bottom_ref, new_west_ref, new_east_ref,
+):
+    narrow = where_ref[3]
+    table = label_table(shear_ref, yields_ref)
+    low = jnp.where(narrow > 0, lines_ref[jnp.maximum(narrow - 1, 0), 192:240, :], 0.0)
+    high = jnp.where(narrow < 3, lines_ref[jnp.minimum(narrow + 1, 3), 192:240, :], 0.0)
+
+    row = rows_of((16, 256))
+    lane = lanes((16, 128))
+    sides = (
+        (top_ref, first_ref, new_top_ref, 0, where_ref[2] > 0),
+        (bottom_ref, last_ref, new_bottom_ref, 1, where_ref[2] < 31),
+    )
+    for halo_ref, own_ref, out_ref, side, inside in sides:
+        laplace = []
+        for c in range(3):
+            part = slice(c * 16, c * 16 + 16)
+            center = halo_ref[part, :]
+            total = halo_ref[48 + c * 16 : 64 + c * 16, :] + own_ref[part, :]
+            total = total + jnp.where(row == 0, 0.0, pltpu.roll(center, 1, 0))
+            total = total + jnp.where(row == 15, 0.0, pltpu.roll(center, 15, 0))
+            c0, c1 = center[:, :128], center[:, 128:]
+            before = pltpu.roll(low[part], 128 - side, 1) if side else low[part]
+            after = pltpu.roll(high[part], 127 - side, 1)
+            w0, w1 = pltpu.roll(c0, 1, 1), pltpu.roll(c1, 1, 1)
+            e0, e1 = pltpu.roll(c0, 127, 1), pltpu.roll(c1, 127, 1)
+            west = [jnp.where(lane == 0, before, w0), jnp.where(lane == 0, w0, w1)]
+            east = [jnp.where(lane == 127, e1, e0), jnp.where(lane == 127, after, e1)]
+            total = total + jnp.concatenate(west, 1) + jnp.concatenate(east, 1)
+            laplace.append(total - 6.0 * center)
+        plastic = jnp.broadcast_to(halo_ref[160:161, :], (16, 256))
+        scale = force_scale(laplace, halo_ref[144:160, :].astype(jnp.int32), plastic, table)
+        damping = jnp.where(row == 0, DAMPING, 0.0)
+        for c in range(3):
+            part = slice(c * 16, c * 16 + 16)
+            v = halo_ref[96 + c * 16 : 112 + c * 16, :]
+            v = v + DT * (scale * laplace[c] - damping * v)
+            out_ref[part, :] = jnp.where(inside, halo_ref[part, :] + DT * v, 0.0)
+
+    row = rows_of((64, 128))
+    lane = lanes((64, 128))
+    layer = lax.rem(lane, 16)
+    used = lane < 48
+    sides = (
+        (west_ref, left_ref, new_west_ref, low, narrow > 0),
+        (east_ref, right_ref, new_east_ref, high, narrow < 3),
+    )
+    for halo_ref, own_ref, out_ref, corner, inside in sides:
+        tile, other = halo_ref[0], halo_ref[1]
+        center = jnp.where(used, tile, 0.0)
+        corners = jnp.concatenate([corner, jnp.zeros((80, 128), F32)], 0).T
+        total = pltpu.roll(tile, 80, 1) + own_ref[0]
+        total = total + jnp.where(row == 0, corners[0:1], pltpu.roll(center, 1, 0))
+        total = total + jnp.where(row == 63, corners[1:2], pltpu.roll(center, 63, 0))
+        total = total + jnp.where(layer == 0, 0.0, pltpu.roll(center, 1, 1))
+        total = total + jnp.where(layer == 15, 0.0, pltpu.roll(center, 127, 1))
+        laplace = jnp.where(used, total - 6.0 * center, 0.0)
+        squares = laplace * laplace
+        squares = (
+            (squares + pltpu.roll(squares, 16, 1))
+            + (pltpu.roll(squares, 32, 1) + pltpu.roll(squares, 96, 1))
+            + pltpu.roll(squares, 112, 1)
+        )
+        region = jnp.where(
+            lane < 16,
+            pltpu.roll(other, 80, 1),
+            jnp.where(lane < 32, pltpu.roll(other, 96, 1), pltpu.roll(other, 112, 1)),
+        ).astype(jnp.int32)
+        modulus = jnp.full(region.shape, table[0][0], F32)
+        ratio = jnp.tile(table[1][0], (8, 1))
+        for label in range(1, 4):
+            modulus = jnp.where(region == label, table[0][label], modulus)
+            ratio = jnp.where(region == label, jnp.tile(table[1][label], (8, 1)), ratio)
+        capped = lax.rsqrt(1.0 + squares * ratio)
+        scale = modulus * jnp.where(other[:, 64:65] > 0.5, capped, 1.0)
+        v = other + DT * (scale * laplace - jnp.where(layer == 0, DAMPING, 0.0) * other)
+        out_ref[...] = jnp.where(used & inside, center + DT * v, 0.0)
 
 
 def slip_kernel(
     shear_ref, yields_ref, u_ref, v_ref, region_ref, plastic_ref,
-    top_ref, bottom_ref, left_ref, right_ref, _after_ref, send_ref,
+    top_ref, bottom_ref, left_ref, right_ref, where_ref, _after_ref, send_ref,
 ):
-    halo_refs = (top_ref, bottom_ref, left_ref, right_ref)
+    halo_refs = (top_ref, bottom_ref, left_ref.at[0], right_ref.at[0])
+    table = label_table(shear_ref, yields_ref)
+    lane = lanes((48, 128))
+    t0, t1 = top_ref[0:48, 0:128], top_ref[0:48, 128:256]
+    b0, b1 = bottom_ref[0:48, 0:128], bottom_ref[0:48, 128:256]
+    to_lower = jnp.where(lane == 0, t0, pltpu.roll(b0, 1, 1))
+    to_upper = jnp.where(lane == 0, pltpu.roll(t1, 1, 1), pltpu.roll(b1, 2, 1))
+    for n in range(4):
+        send_ref[n, 192:240, :] = jnp.where(where_ref[3] < n, to_upper, to_lower)
     for i in range(8):
         rows = strip_of(i)
         centers, sums = stencil_strip(
@@ -238,7 +368,7 @@
             0,
         )
         force = strip_force(
-            centers, sums, region_ref[0, rows, :], plastic_ref[rows, :], shear_ref, yields_ref
+            centers, sums, region_ref[0, rows, :], plastic_ref[rows, :], table
         )
         n, part = i // 2, (i % 2) * 8
         for c in range(3):
@@ -254,16 +384,12 @@
 def step_one_kernel(
     shear_ref, yields_ref, u_ref, v_ref, region_ref, plastic_ref,
     top_ref, bottom_ref, left_ref, right_ref, _after_ref,
-    new_u_ref, new_v_ref, first_ref, last_ref, left_out_ref, right_out_ref,
+    new_u_ref, new_v_ref,
 ):
     step = pl.program_id(0)
 
-    @pl.when(step == 0)
-    def _():
-        left_out_ref[...] = jnp.zeros_like(left_out_ref)
-        right_out_ref[...] = jnp.zeros_like(right_out_ref)
-
-    halo_refs = (top_ref, bottom_ref, left_ref, right_ref)
+    halo_refs = (top_ref, bottom_ref, left_ref.at[0], right_ref.at[0])
+    table = label_table(shear_ref, yields_ref)
     for k in range(PLANES):
         z = step * PLANES + k
         damping = jnp.where(z == 0, DAMPING, 0.0).astype(F32)
@@ -283,7 +409,7 @@
                 i, lambda c, r: u_ref[c, z, r, :], None, load_above, load_below, halo_refs, z
             )
             force = strip_force(
-                centers, sums, region_ref[k, rows, :], plastic_ref[rows, :], shear_ref, yields_ref
+                centers, sums, region_ref[k, rows, :], plastic_ref[rows, :], table
             )
             for c in range(3):
                 v = v_ref[c, k, rows, :]
@@ -291,17 +417,12 @@
                 u = centers[c] + DT * v
                 new_v_ref[c, k, rows, :] = v
                 new_u_ref[c, k, rows, :] = u
-                place = slot(c, z)
-                if i == 0:
-                    first_ref[pl.ds(place, 1), :] = u[0:1]
-                if i == 7:
-                    last_ref[pl.ds(place, 1), :] = u[7:8]
-                put_columns(left_out_ref, right_out_ref, u, i, place)
 
 
 def step_two_kernel(start, *refs):
     (shear_ref, yields_ref, u_ref, v_ref, region_ref, plastic_ref) = refs[:6]
     halo_refs = refs[6:10]
+    table = label_table(shear_ref, yields_ref)
     new_u_ref, new_v_ref = refs[-2:]
     for k in range(PLANES):
         z = pl.program_id(0) * PLANES + (start + k)
@@ -322,7 +443,7 @@
                 z,
             )
             force = strip_force(
-                centers, sums, region_ref[k, rows, :], plastic_ref[rows, :], shear_ref, yields_ref
+                centers, sums, region_ref[k, rows, :], plastic_ref[rows, :], table
             )
             for c in range(3):
                 v = v_ref[c, k, rows, :] + DT * force[c]
@@ -336,6 +457,7 @@
     recv_ref, _old_u_ref, _old_v_ref, new_u_ref, new_v_ref, surface,
 ):
     square = DT * DT
+    table = label_table(shear_ref, yields_ref)
     halo_refs = (top_ref, bottom_ref, left_ref, right_ref)
 
     def traction(f, c, i):
@@ -376,7 +498,7 @@
                 i, load, beside if z == 0 else None, above, below, halo_refs, z
             )
             force = strip_force(
-                centers, sums, region_ref[z, rows, :], plastic_ref[rows, :], shear_ref, yields_ref
+                centers, sums, region_ref[z, rows, :], plastic_ref[rows, :], table
             )
             for c in range(3):
                 v = v_ref[c, z, rows, :]
@@ -674,7 +796,7 @@
         cost_estimate=pl.CostEstimate(flops=0, bytes_accessed=size, transcendentals=0),
         compiler_params=pltpu.CompilerParams(vmem_limit_bytes=limit),
         name=name,
-    )(*args, *after)
+    )(*args, *(in_hbm(x) for x in after))
 
 
 def halo(first, last, left, right):
@@ -695,8 +817,16 @@
 
 def body(u, v, region, flags, shear, yields, history, kernel):
     device = lax.axis_index(ALL)
-    where = jnp.stack([device < 64, device == 0]).astype(jnp.int32)
-    edge_shapes = [shape_of(48, 256)] * 2 + [shape_of(64, 128)] * 2
+    where = jnp.stack(
+        [
+            (device < 64).astype(jnp.int32),
+            (device == 0).astype(jnp.int32),
+            lax.axis_index("wide"),
+            lax.axis_index("narrow"),
+        ]
+    )
+    edge_shapes = [shape_of(168, 256)] * 2 + [shape_of(2, 64, 128)] * 2
+    halo_shapes = [shape_of(48, 256)] * 2 + [shape_of(64, 128)] * 2
     near = lambda depth: pl.BlockSpec((3, depth, 64, 256), lambda *_: (0, 0, 0, 0))
     slab = lambda depth: pl.BlockSpec((depth, 64, 256), lambda *_: (0, 0, 0))
     planes = lambda depth, start=0: pl.BlockSpec(
@@ -709,18 +839,20 @@
     any_spec = pl.BlockSpec(memory_space=pl.ANY)
     t = TABLES
     u, v, region, history, kernel = (in_hbm(x) for x in (u, v, region, history, kernel))
+    shear, yields, where = in_hbm(shear), in_hbm(yields), in_hbm(where)
 
     first, last, left, right, plastic = pl.pallas_call(
         edges_kernel,
         grid=(4,),
-        in_specs=[planes(4), full((8, 32))],
+        in_specs=[planes(4), planes(4), slabs(4), full((8, 32))],
         out_specs=[full(s.shape) for s in edge_shapes] + [full((64, 256))],
         out_shape=edge_shapes + [shape_of(64, 256)],
-        cost_estimate=pl.CostEstimate(flops=0, bytes_accessed=3300000, transcendentals=0),
+        cost_estimate=pl.CostEstimate(flops=0, bytes_accessed=8000000, transcendentals=0),
         compiler_params=pltpu.CompilerParams(vmem_limit_bytes=16 << 20),
             name="edges",
-    )(u, flags)
+    )(u, v, region, flags)
     halo_one = halo(first, last, left, right)
+    plastic = in_hbm(plastic)
 
     width = 256
     steps = 1024 // width
@@ -747,19 +879,21 @@
             cost_estimate=pl.CostEstimate(flops=0, bytes_accessed=5500000, transcendentals=0),
             compiler_params=pltpu.CompilerParams(vmem_limit_bytes=16 << 20),
             name="history",
-        )(where, kernel, history, *given)
+        )(where, kernel, history, *(in_hbm(x) for x in given))
 
     partial = sums(0, None)
     send = pl.pallas_call(
         slip_kernel,
         grid=(1,),
-        in_specs=[SMEM, SMEM, near(2), near(1), slab(1), full((64, 256))] + halo_specs + [any_spec],
-        out_specs=full((4, 192, 128)),
-        out_shape=shape_of(4, 192, 128),
+        in_specs=[SMEM, SMEM, near(2), near(1), slab(1), full((64, 256))]
+        + halo_specs
+        + [SMEM, any_spec],
+        out_specs=full((4, 240, 128)),
+        out_shape=shape_of(4, 240, 128),
         cost_estimate=pl.CostEstimate(flops=0, bytes_accessed=1500000, transcendentals=0),
         compiler_params=pltpu.CompilerParams(vmem_limit_bytes=16 << 20),
             name="slip",
-    )(shear, yields, u, v, region, plastic, *halo_one, partial[2])
+    )(shear, yields, u, v, region, plastic, *halo_one, where, in_hbm(partial[2]))
     lines = exchange(send, "narrow")
     own, main, edge = sums(1, partial)
     main = lax.ppermute(main, ALL, [(i, 127 - i) for i in range(128)])
@@ -771,25 +905,31 @@
     )
     waves = exchange(send.reshape(128, 1, 768), ALL).reshape(768, 128)
 
-    new_u, new_v, first, last, left, right = pl.pallas_call(
+    new_u, new_v = pl.pallas_call(
         step_one_kernel,
         grid=(16 // PLANES,),
         in_specs=[SMEM, SMEM, near(16), planes(PLANES), slabs(PLANES), full((64, 256))]
         + halo_specs
         + [any_spec],
-        out_specs=[planes(PLANES)] * 2 + [full(s.shape) for s in edge_shapes],
-        out_shape=[hbm_shape(3, 16, 64, 256)] * 2 + edge_shapes,
+        out_specs=[planes(PLANES)] * 2,
+        out_shape=[hbm_shape(3, 16, 64, 256)] * 2,
         cost_estimate=pl.CostEstimate(flops=0, bytes_accessed=14000000, transcendentals=0),
         compiler_params=pltpu.CompilerParams(vmem_limit_bytes=24 << 20),
             name="step_one",
-    )(shear, yields, u, v, region, plastic, *halo_one, send)
+    )(shear, yields, u, v, region, plastic, *halo_one, in_hbm(send))
     new_u, new_v = in_hbm(new_u), in_hbm(new_v)
-    halo_two = halo(first, last, left, right)
+    halo_two = call(
+        beside_kernel,
+        halo_shapes,
+        (where, shear, yields, *(in_hbm(x) for x in (first, last, left, right, *halo_one, lines))),
+        smem=3,
+        name="beside",
+    )
 
     coefficients = call(
         mirror_kernel,
         shape_of(8, 3, 8, 2048),
-        (where, t["reverse"], own, main, edge),
+        (where, t["reverse"], *(in_hbm(x) for x in (own, main, edge))),
         smem=1,
         scratch=[pltpu.VMEM((144, 2048), F32)] * 2,
         name="mirror",
@@ -824,7 +964,7 @@
             ),
             compiler_params=pltpu.CompilerParams(vmem_limit_bytes=24 << 20),
             name="step_two",
-        )(shear, yields, new_u, new_v, region, plastic, *halo_two, *given, after)
+        )(shear, yields, new_u, new_v, region, plastic, *halo_two, *given, in_hbm(after))
 
     out = later(2, 10, [], send)
     send = call(

time: 128 us -> 114 us (0.89)
  the two profiles are of different devices: /device:TPU:4 before, /device:TPU:1 now
where the time goes in v4:
time: 114 us; the launch traced here: 113 us
  Pallas kernels  53.4 us (47%)
  starting transfers between devices  42.9 us (38%)
  waiting for transfers between devices  12.8 us (11%)
  local copies, waits for them, and re-layouts  2.09 us (2%)
    all_to_all x4, starting transfers between devices, exchange(): return lax.all_to_all(x, axis, split_axis=0, concat_axis=0, tiled=True)  20.2 us
    pallas_call x5, Pallas kernels, call(): pl.pallas_call(body, in_specs=[SMEM] * smem + [full(x.shape) for x in arg...  11.2 us
    pallas_call x2, Pallas kernels, later(): pl.pallas_call(functools.partial(step_two_kernel, start), grid=((stop - s...  11 us
    pallas_call x2, Pallas kernels, sums(): pl.pallas_call(history_kernel, grid=(steps,), in_specs=[SMEM, pl.BlockSpe...  11 us
    ppermute x1, starting transfers between devices, body(): main = lax.ppermute(main, ALL, [(i, 127 - i) for i in range(128)])  9.73 us
    pallas_call x1, Pallas kernels, body(): pl.pallas_call(step_one_kernel, grid=(16 // PLANES,), in_specs=[SMEM, SME...  9.46 us
    all_to_all x4, waiting for transfers between devices, exchange(): return lax.all_to_all(x, axis, split_axis=0, concat_axis=0, tiled=True)  7.4 us
    pallas_call x1, Pallas kernels, body(): pl.pallas_call(edges_kernel, grid=(4,), in_specs=[planes(4), planes(4), s...  5.85 us
  transfers between devices with their start and end apart: 10, of which 3 were waited for; matrix products, arithmetic and copies ran while one was open for 1% of the time, Pallas kernels for 33%

profile of v4, /device:TPU:1, one launch (start us, length us, event | category | flops | bytes accessed | tf_op | source)
XLA Modules:
  0.0 112.8 jit_solution(5507854325394859280)
XLA Ops:
  0.6 0.0 copy-start.21
  0.6 0.7 copy-done.21
  1.3 5.8 %edges.1 = (f32[168,256]{1,0:T(8,128)S(1)}, f32[168,256]{1,0:T(8,128)S(1)}, f32[2,64,128]{2,1,0:T(8,128)S(1)}, f32[2,64,128]{2,1,0:T(8,128)S(1)}, f32[64,256]{1,0:T(8,128)S(1)}) custom-call(f32[3,16,64,256]{3,2,1,0:T(8,128)} %u_ref.5, f32[3,16,64,256]{3,2,1,0:T(8,128)} %v_ref.5, s32[16,64,256]{2,1,0:T(8,128)} %region_ref.7, s32[8,32]{1,0:T(8,128)S(1)} %copy-done.21), custom_call_target="tpu_custom_call" | custom-call | bytes 8000000 | tf_op jit(solution)/shard_map/edges/pallas_call | solution.py:844
  7.2 0.0 copy-start.1
  7.2 0.6 copy-done.1
  7.8 4.4 %collective-permute-start = (f32[168,256]{1,0:T(8,128)S(1)}, f32[168,256]{1,0:T(8,128)S(1)}, u32[]{:S(2)}, u32[]{:S(2)}) collective-permute-start(f32[168,256]{1,0:T(8,128)S(1)} %get-tuple-element.24.last_ref), channel_id=1, source_target_pairs={{0,4},{4,8},{8,12},{12,16},{16,20},{20,24},{24,28},{28,32},{32,36}... | collective-permute-start | bytes 516104 | tf_op jit(solution)/shard_map/ppermute | solution.py:805
  12.2 1.3 %collective-permute-start.1 = (f32[168,256]{1,0:T(8,128)S(1)}, f32[168,256]{1,0:T(8,128)S(1)}, u32[]{:S(2)}, u32[]{:S(2)}) collective-permute-start(f32[168,256]{1,0:T(8,128)S(1)} %get-tuple-element.25.first_ref), channel_id=1, source_target_pairs={{4,0},{8,4},{12,8},{16,12},{20,16},{24,20},{28,24},{32,28},{36,32}... | collective-permute-start | bytes 516104 | tf_op jit(solution)/shard_map/ppermute | solution.py:806
  13.5 4.0 %collective-permute-start.2 = (f32[2,64,128]{2,1,0:T(8,128)S(1)}, f32[2,64,128]{2,1,0:T(8,128)S(1)}, u32[]{:S(2)}, u32[]{:S(2)}) collective-permute-start(f32[2,64,128]{2,1,0:T(8,128)S(1)} %get-tuple-element.26.right_ref), channel_id=1, source_target_pairs={{0,1},{1,2},{2,3},{4,5},{5,6},{6,7},{8,9},{9,10},{10,11},{12,13},{... | collective-permute-start | bytes 196616 | tf_op jit(solution)/shard_map/ppermute | solution.py:809
  17.4 1.9 %collective-permute-start.3 = (f32[2,64,128]{2,1,0:T(8,128)S(1)}, f32[2,64,128]{2,1,0:T(8,128)S(1)}, u32[]{:S(2)}, u32[]{:S(2)}) collective-permute-start(f32[2,64,128]{2,1,0:T(8,128)S(1)} %get-tuple-element.27.left_ref), channel_id=1, source_target_pairs={{1,0},{2,1},{3,2},{5,4},{6,5},{7,6},{9,8},{10,9},{11,10},{13,12},{... | collective-permute-start | bytes 196616 | tf_op jit(solution)/shard_map/ppermute | solution.py:810
  19.4 0.6 pad_add_fusion.where_ref
  20.0 5.4 %history.2 = (f32[72,2048]{1,0:T(8,128)}, f32[72,2048]{1,0:T(8,128)}, f32[18,2048]{1,0:T(8,128)}) custom-call(s32[4]{0:T(128)} %pad_add_fusion.where_ref, bf16[33,3,8,2048]{3,2,1,0:T(8,128)(2,1)} %kernel_ref.3, bf16[32,2,3,8,2048]{4,3,2,1,0:T(8,128)(2,1)} %history_ref.3), custom_call_target="tpu_custom_call" | custom-call | bytes 5500000 | tf_op jit(solution)/shard_map/history/pallas_call | solution.py:863
  25.4 0.0 copy-done.15
  25.4 0.0 copy-done.16
  25.4 0.0 copy-done.19
  25.5 0.0 copy-done.20
  25.5 0.0 collective-permute-done.2.left_ref.west_ref
  25.5 0.0 copy-start.5
  25.5 0.0 collective-permute-done.3.right_ref.east_ref
  25.5 0.0 copy-start.6
  25.5 0.0 collective-permute-done.top_ref
  25.5 0.0 copy-start.2
  25.5 0.0 collective-permute-done.1.bottom_ref
  25.5 0.0 copy-start.3
  25.5 2.2 %slip.1 = f32[4,240,128]{2,1,0:T(8,128)} custom-call(f32[4]{0:T(128)} %shear_ref.7, f32[4]{0:T(128)} %yields_ref.7, f32[3,16,64,256]{3,2,1,0:T(8,128)} %u_ref.5, f32[3,16,64,256]{3,2,1,0:T(8,128)} %v_ref.5, s32[16,64,256]{2,1,0:T(8,128)} %region_ref.7, f32[64,256]{1,0:T(8,128)} %copy-done.1, f32[168,256]{1,0:T(8,128)S(1)} %collective-permute-done.top_ref, ...), custom_call_target="tpu_custom_call" | custom-call | bytes 1500000 | tf_op jit(solution)/shard_map/slip/pallas_call | solution.py:885
  27.8 3.5 %all-to-all-start = ((f32[4,240,128]{2,1,0:T(8,128)}), f32[4,240,128]{2,1,0:T(8,128)S(1)}, u32[]{:S(2)}, u32[]{:S(2)}) async-start(f32[4,240,128]{2,1,0:T(8,128)} %slip.1), calls=%async_computation | async-start | bytes 983040 | tf_op jit(solution)/shard_map/all_to_all | solution.py:815
  31.2 0.0 copy-start.7
  31.3 0.0 copy-start.10
  31.3 0.0 copy-start.11
  31.3 5.5 %history.3 = (f32[72,2048]{1,0:T(8,128)}, f32[72,2048]{1,0:T(8,128)}, f32[18,2048]{1,0:T(8,128)}) custom-call(s32[4]{0:T(128)} %pad_add_fusion.where_ref, bf16[33,3,8,2048]{3,2,1,0:T(8,128)(2,1)} %kernel_ref.3, bf16[32,2,3,8,2048]{4,3,2,1,0:T(8,128)(2,1)} %history_ref.3, ...), custom_call_target="tpu_custom_call", output_to_operand_aliasing={{0}: (3, {}), {1}: (4, {}), {2}: (5, {})} | custom-call | bytes 5500000 | tf_op jit(solution)/shard_map/history/pallas_call | solution.py:863
  36.8 9.7 %collective-permute-start.4 = (f32[72,2048]{1,0:T(8,128)}, f32[72,2048]{1,0:T(8,128)}, u32[]{:S(2)}, u32[]{:S(2)}) collective-permute-start(f32[72,2048]{1,0:T(8,128)} %get-tuple-element.38), channel_id=1, source_target_pairs={{0,127},{1,126},{2,125},{3,124},{4,123},{5,122},{6,121},{7,120},{8... | collective-permute-start | bytes 1769480 | tf_op jit(solution)/shard_map/ppermute | solution.py:899
  46.6 0.0 all-to-all-done.recv_ref.lines_ref
  46.6 0.0 copy-done.7
  46.6 0.0 copy-done.10
  46.6 0.0 copy-done.11
  46.6 1.9 %dip.1._after_ref = f32[768,128]{1,0:T(8,128)} custom-call(bf16[2,512,256]{2,1,0:T(8,128)(2,1)S(1)} %copy-done.7, f32[2,2,128,128]{3,2,1,0:T(8,128)S(1)} %copy-done.11, bf16[2,2,136,256]{3,2,1,0:T(8,128)(2,1)S(1)} %copy-done.10, f32[4,240,128]{2,1,0:T(8,128)S(1)} %all-to-all-done.recv_ref.lines_ref, f32[72,2048]{1,0:T(8,128)} %get-tuple-element.31._after_ref.own_ref), custom_call_target="tpu_custom_call" | custom-call | bytes 2752512 | tf_op jit(solution)/shard_map/dip/pallas_call | solution.py:788
  48.5 5.6 %all-to-all-start.1 = ((f32[128,1,768]{2,1,0:T(1,128)}), f32[128,1,768]{2,1,0:T(1,128)S(1)}, u32[]{:S(2)}, u32[]{:S(2)}) async-start(f32[128,1,768]{2,1,0:T(1,128)} %bitcast.4), calls=%async_computation.1 | async-start | bytes 786432 | tf_op jit(solution)/shard_map/all_to_all | solution.py:815
  54.0 0.0 copy-done.22
  54.0 0.0 copy-start.17
  54.0 0.0 copy-start.18
  54.1 1.4 %collective-permute-start.5 = (f32[18,2048]{1,0:T(8,128)S(1)}, f32[18,2048]{1,0:T(8,128)S(1)}, u32[]{:S(2)}, u32[]{:S(2)}) collective-permute-start(f32[18,2048]{1,0:T(8,128)S(1)} %copy-done.22), channel_id=1, source_target_pairs={{64,0},{65,63},{66,62},{67,61},{68,60},{69,59},{70,58},{71,57},{72... | collective-permute-start | bytes 442376 | tf_op jit(solution)/shard_map/ppermute | solution.py:900
  55.5 0.0 copy-done.5
  55.5 9.5 %step_one.1 = (f32[3,16,64,256]{3,2,1,0:T(8,128)}, f32[3,16,64,256]{3,2,1,0:T(8,128)}) custom-call(f32[4]{0:T(128)} %shear_ref.7, f32[4]{0:T(128)} %yields_ref.7, f32[3,16,64,256]{3,2,1,0:T(8,128)} %u_ref.5, f32[3,16,64,256]{3,2,1,0:T(8,128)} %v_ref.5, s32[16,64,256]{2,1,0:T(8,128)} %region_ref.7, f32[64,256]{1,0:T(8,128)} %copy-done.1, ...), custom_call_target="tpu_custom_call" | custom-call | bytes 14000000 | tf_op jit(solution)/shard_map/step_one/pallas_call | solution.py:908
  65.0 0.0 copy-start.4
  65.0 0.0 copy-start.13
  65.0 0.0 copy-start.14
  65.0 5.4 %collective-permute-done.5.edge_ref = f32[18,2048]{1,0:T(8,128)S(1)} collective-permute-done((f32[18,2048]{1,0:T(8,128)S(1)}, f32[18,2048]{1,0:T(8,128)S(1)}, u32[]{:S(2)}, u32[]{:S(2)}) %collective-permute-start.5) | collective-permute-done | bytes 147488 | tf_op jit(solution)/shard_map/ppermute | solution.py:900
  70.4 0.0 collective-permute-done.4.main_ref
  70.4 0.7 copy-done.23
  71.1 2.4 %mirror.1.coef_ref = f32[8,3,8,2048]{3,2,1,0:T(8,128)S(1)} custom-call(s32[4]{0:T(128)} %pad_add_fusion.where_ref, bf16[128,128]{1,0:T(8,128)(2,1)S(1)} %copy-done.17, f32[72,2048]{1,0:T(8,128)} %get-tuple-element.31._after_ref.own_ref, f32[72,2048]{1,0:T(8,128)} %collective-permute-done.4.main_ref, f32[18,2048]{1,0:T(8,128)} %copy-done.23), custom_call_target="tpu_custom_call" | custom-call | bytes 2965520 | tf_op jit(solution)/shard_map/mirror/pallas_call | solution.py:788
  73.6 0.0 all-to-all-done.1
  73.6 2.9 %strike.1.refs_10_ = f32[1024,128]{1,0:T(8,128)} custom-call(bf16[2,256,256]{2,1,0:T(8,128)(2,1)S(1)} %copy-done.4, f32[2,128,128]{2,1,0:T(8,128)S(1)} %copy-done.18, bf16[2,256,256]{2,1,0:T(8,128)(2,1)S(1)} %copy-done.14, bf16[128,128]{1,0:T(8,128)(2,1)S(1)} %copy-done.17, bf16[2,256,256]{2,1,0:T(8,128)(2,1)S(1)} %copy-done.13, ...), custom_call_target="tpu_custom_call" | custom-call | bytes 4784128 | tf_op jit(solution)/shard_map/strike/pallas_call | solution.py:788
  76.5 6.5 %all-to-all-start.2 = ((f32[128,8,128]{2,1,0:T(8,128)}), f32[128,8,128]{2,1,0:T(8,128)S(1)}, u32[]{:S(2)}, u32[]{:S(2)}) async-start(f32[128,8,128]{2,1,0:T(8,128)} %bitcast.6), calls=%async_computation.2 | async-start | bytes 1048576 | tf_op jit(solution)/shard_map/all_to_all | solution.py:815
  82.9 2.0 %beside.1 = (f32[48,256]{1,0:T(8,128)S(1)}, f32[48,256]{1,0:T(8,128)S(1)}, f32[64,128]{1,0:T(8,128)S(1)}, f32[64,128]{1,0:T(8,128)S(1)}) custom-call(s32[4]{0:T(128)} %pad_add_fusion.where_ref, f32[4]{0:T(128)} %shear_ref.7, f32[4]{0:T(128)} %yields_ref.7, f32[168,256]{1,0:T(8,128)} %copy-done.15, f32[168,256]{1,0:T(8,128)} %copy-done.16, ...), custom_call_target="tpu_custom_call" | custom-call | bytes 1605680 | tf_op jit(solution)/shard_map/beside/pallas_call | solution.py:788
  84.9 0.0 copy-start.8
  84.9 0.0 copy-start.9
  85.0 0.0 copy-start.12
  85.0 5.9 %step_two.2 = (f32[3,16,64,256]{3,2,1,0:T(8,128)}, f32[3,16,64,256]{3,2,1,0:T(8,128)}) custom-call(f32[4]{0:T(128)} %shear_ref.7, f32[4]{0:T(128)} %yields_ref.7, f32[3,16,64,256]{3,2,1,0:T(8,128)} %get-tuple-element.32._after_ref.refs_2_.u_ref, f32[3,16,64,256]{3,2,1,0:T(8,128)} %get-tuple-element.33.refs_3_.v_ref, s32[16,64,256]{2,1,0:T(8,128)} %region_ref.7, ...), custom_call_target="tpu_custom_call" | custom-call | bytes 6400000 | tf_op jit(solution)/shard_map/step_two/pallas_call | solution.py:951
  90.8 5.4 %all-to-all-done.2 = f32[128,8,128]{2,1,0:T(8,128)S(1)} async-done(((f32[128,8,128]{2,1,0:T(8,128)}), f32[128,8,128]{2,1,0:T(8,128)S(1)}, u32[]{:S(2)}, u32[]{:S(2)}) %all-to-all-start.2) | async-done | bytes 524320 | tf_op jit(solution)/shard_map/all_to_all | solution.py:815
  96.3 0.0 copy-done.9
  96.3 2.1 %undip.1.refs_12_ = f32[4,224,128]{2,1,0:T(8,128)} custom-call(bf16[2,256,512]{2,1,0:T(8,128)(2,1)S(1)} %copy-done.9, f32[2,2,128,128]{3,2,1,0:T(8,128)S(1)} %copy-done.12, bf16[2,256,512]{2,1,0:T(8,128)(2,1)S(1)} %copy-done.8, f32[1024,128]{1,0:T(8,128)S(1)} %bitcast.8, f32[3,16,64,256]{3,2,1,0:T(8,128)} %get-tuple-element.40._after_ref.refs_10_), custom_call_target="tpu_custom_call" | custom-call | bytes 3342336 | tf_op jit(solution)/shard_map/undip/pallas_call | solution.py:788
  98.3 4.7 %all-to-all-start.3 = ((f32[4,224,128]{2,1,0:T(8,128)}), f32[4,224,128]{2,1,0:T(8,128)S(1)}, u32[]{:S(2)}, u32[]{:S(2)}) async-start(f32[4,224,128]{2,1,0:T(8,128)} %undip.1.refs_12_), calls=%async_computation.3 | async-start | bytes 917504 | tf_op jit(solution)/shard_map/all_to_all | solution.py:815
  103.1 5.2 %step_two.3 = (f32[3,16,64,256]{3,2,1,0:T(8,128)}, f32[3,16,64,256]{3,2,1,0:T(8,128)}) custom-call(f32[4]{0:T(128)} %shear_ref.7, f32[4]{0:T(128)} %yields_ref.7, f32[3,16,64,256]{3,2,1,0:T(8,128)} %get-tuple-element.32._after_ref.refs_2_.u_ref, f32[3,16,64,256]{3,2,1,0:T(8,128)} %get-tuple-element.33.refs_3_.v_ref, ...), custom_call_target="tpu_custom_call", output_to_operand_aliasing={{0}: (10, {}), {1}: (11, {})} | custom-call | bytes 4800000 | tf_op jit(solution)/shard_map/step_two/pallas_call | solution.py:951
  108.2 2.0 %all-to-all-done.3.recv_ref = f32[4,224,128]{2,1,0:T(8,128)S(1)} async-done(((f32[4,224,128]{2,1,0:T(8,128)}), f32[4,224,128]{2,1,0:T(8,128)S(1)}, u32[]{:S(2)}, u32[]{:S(2)}) %all-to-all-start.3) | async-done | bytes 458784 | tf_op jit(solution)/shard_map/all_to_all | solution.py:815
  110.2 2.6 %last.1 = (f32[3,16,64,256]{3,2,1,0:T(8,128)}, f32[3,16,64,256]{3,2,1,0:T(8,128)}) custom-call(f32[4]{0:T(128)} %shear_ref.7, f32[4]{0:T(128)} %yields_ref.7, f32[3,16,64,256]{3,2,1,0:T(8,128)} %get-tuple-element.32._after_ref.refs_2_.u_ref, f32[3,16,64,256]{3,2,1,0:T(8,128)} %get-tuple-element.33.refs_3_.v_ref, ...), custom_call_target="tpu_custom_call", output_to_operand_aliasing={{0}: (11, {}), {1}: (12, {})} | custom-call | bytes 4000000 | tf_op jit(solution)/shard_map/last/pallas_call | solution.py:980
  (18 shorter events, 0.0 us)
Async XLA Ops:
  0.6 0.7 copy-start.21
  7.2 0.6 copy-start.1
  7.8 17.6 %copy-start.15 = (f32[168,256]{1,0:T(8,128)}, f32[168,256]{1,0:T(8,128)S(1)}, u32[]{:S(2)}) copy-start(f32[168,256]{1,0:T(8,128)S(1)} %get-tuple-element.25.first_ref) | copy-start | bytes 516100
  7.8 17.6 %copy-start.16 = (f32[168,256]{1,0:T(8,128)}, f32[168,256]{1,0:T(8,128)S(1)}, u32[]{:S(2)}) copy-start(f32[168,256]{1,0:T(8,128)S(1)} %get-tuple-element.24.last_ref) | copy-start | bytes 516100
  7.8 17.6 %copy-start.19 = (f32[2,64,128]{2,1,0:T(8,128)}, f32[2,64,128]{2,1,0:T(8,128)S(1)}, u32[]{:S(2)}) copy-start(f32[2,64,128]{2,1,0:T(8,128)S(1)} %get-tuple-element.27.left_ref) | copy-start | bytes 196612
  7.8 17.7 %copy-start.20 = (f32[2,64,128]{2,1,0:T(8,128)}, f32[2,64,128]{2,1,0:T(8,128)S(1)}, u32[]{:S(2)}) copy-start(f32[2,64,128]{2,1,0:T(8,128)S(1)} %get-tuple-element.26.right_ref) | copy-start | bytes 196612
  7.8 17.7 %collective-permute-start = (f32[168,256]{1,0:T(8,128)S(1)}, f32[168,256]{1,0:T(8,128)S(1)}, u32[]{:S(2)}, u32[]{:S(2)}) collective-permute-start(f32[168,256]{1,0:T(8,128)S(1)} %get-tuple-element.24.last_ref), channel_id=1, source_target_pairs={{0,4},{4,8},{8,12},{12,16},{16,20},{20,24},{24,28},{28,32},{32,36}... | collective-permute-start | bytes 516104 | tf_op jit(solution)/shard_map/ppermute | solution.py:805
  12.2 13.3 %collective-permute-start.1 = (f32[168,256]{1,0:T(8,128)S(1)}, f32[168,256]{1,0:T(8,128)S(1)}, u32[]{:S(2)}, u32[]{:S(2)}) collective-permute-start(f32[168,256]{1,0:T(8,128)S(1)} %get-tuple-element.25.first_ref), channel_id=1, source_target_pairs={{4,0},{8,4},{12,8},{16,12},{20,16},{24,20},{28,24},{32,28},{36,32}... | collective-permute-start | bytes 516104 | tf_op jit(solution)/shard_map/ppermute | solution.py:806
  13.5 12.0 %collective-permute-start.2 = (f32[2,64,128]{2,1,0:T(8,128)S(1)}, f32[2,64,128]{2,1,0:T(8,128)S(1)}, u32[]{:S(2)}, u32[]{:S(2)}) collective-permute-start(f32[2,64,128]{2,1,0:T(8,128)S(1)} %get-tuple-element.26.right_ref), channel_id=1, source_target_pairs={{0,1},{1,2},{2,3},{4,5},{5,6},{6,7},{8,9},{9,10},{10,11},{12,13},{... | collective-permute-start | bytes 196616 | tf_op jit(solution)/shard_map/ppermute | solution.py:809
  17.4 8.0 %collective-permute-start.3 = (f32[2,64,128]{2,1,0:T(8,128)S(1)}, f32[2,64,128]{2,1,0:T(8,128)S(1)}, u32[]{:S(2)}, u32[]{:S(2)}) collective-permute-start(f32[2,64,128]{2,1,0:T(8,128)S(1)} %get-tuple-element.27.left_ref), channel_id=1, source_target_pairs={{1,0},{2,1},{3,2},{5,4},{6,5},{7,6},{9,8},{10,9},{11,10},{13,12},{... | collective-permute-start | bytes 196616 | tf_op jit(solution)/shard_map/ppermute | solution.py:810
  25.5 30.0 %copy-start.5 = (f32[2,64,128]{2,1,0:T(8,128)}, f32[2,64,128]{2,1,0:T(8,128)S(1)}, u32[]{:S(2)}) copy-start(f32[2,64,128]{2,1,0:T(8,128)S(1)} %collective-permute-done.2.left_ref.west_ref) | copy-start | bytes 196612
  25.5 30.0 %copy-start.6 = (f32[2,64,128]{2,1,0:T(8,128)}, f32[2,64,128]{2,1,0:T(8,128)S(1)}, u32[]{:S(2)}) copy-start(f32[2,64,128]{2,1,0:T(8,128)S(1)} %collective-permute-done.3.right_ref.east_ref) | copy-start | bytes 196612
  25.5 30.0 %copy-start.2 = (f32[168,256]{1,0:T(8,128)}, f32[168,256]{1,0:T(8,128)S(1)}, u32[]{:S(2)}) copy-start(f32[168,256]{1,0:T(8,128)S(1)} %collective-permute-done.top_ref) | copy-start | bytes 516100
  25.5 30.0 %copy-start.3 = (f32[168,256]{1,0:T(8,128)}, f32[168,256]{1,0:T(8,128)S(1)}, u32[]{:S(2)}) copy-start(f32[168,256]{1,0:T(8,128)S(1)} %collective-permute-done.1.bottom_ref) | copy-start | bytes 516100
  27.8 18.8 %all-to-all-start = ((f32[4,240,128]{2,1,0:T(8,128)}), f32[4,240,128]{2,1,0:T(8,128)S(1)}, u32[]{:S(2)}, u32[]{:S(2)}) async-start(f32[4,240,128]{2,1,0:T(8,128)} %slip.1), calls=%async_computation | async-start | bytes 983040 | tf_op jit(solution)/shard_map/all_to_all | solution.py:815
  31.2 15.3 %copy-start.7 = (bf16[2,512,256]{2,1,0:T(8,128)(2,1)S(1)}, bf16[2,512,256]{2,1,0:T(8,128)(2,1)}, u32[]{:S(2)}) copy-start(bf16[2,512,256]{2,1,0:T(8,128)(2,1)} %constant.37.clone.radix_ref) | copy-start | bytes 1572868
  31.3 15.3 %copy-start.10 = (bf16[2,2,136,256]{3,2,1,0:T(8,128)(2,1)S(1)}, bf16[2,2,136,256]{3,2,1,0:T(8,128)(2,1)}, u32[]{:S(2)}) copy-start(bf16[2,2,136,256]{3,2,1,0:T(8,128)(2,1)} %constant.39.clone.out_table_ref) | copy-start | bytes 835588
  31.3 15.3 %copy-start.11 = (f32[2,2,128,128]{3,2,1,0:T(8,128)S(1)}, f32[2,2,128,128]{3,2,1,0:T(8,128)}, u32[]{:S(2)}) copy-start(f32[2,2,128,128]{3,2,1,0:T(8,128)} %constant.38.clone.turn_ref) | copy-start | bytes 786436
  36.8 17.2 %copy-start.22 = (f32[18,2048]{1,0:T(8,128)S(1)}, f32[18,2048]{1,0:T(8,128)}, u32[]{:S(2)}) copy-start(f32[18,2048]{1,0:T(8,128)} %get-tuple-element.39) | copy-start | bytes 442372
  36.8 33.6 %collective-permute-start.4 = (f32[72,2048]{1,0:T(8,128)}, f32[72,2048]{1,0:T(8,128)}, u32[]{:S(2)}, u32[]{:S(2)}) collective-permute-start(f32[72,2048]{1,0:T(8,128)} %get-tuple-element.38), channel_id=1, source_target_pairs={{0,127},{1,126},{2,125},{3,124},{4,123},{5,122},{6,121},{7,120},{8... | collective-permute-start | bytes 1769480 | tf_op jit(solution)/shard_map/ppermute | solution.py:899
  46.6 18.4 %copy-start = (f32[4,240,128]{2,1,0:T(8,128)}, f32[4,240,128]{2,1,0:T(8,128)S(1)}, u32[]{:S(2)}) copy-start(f32[4,240,128]{2,1,0:T(8,128)S(1)} %all-to-all-done.recv_ref.lines_ref) | copy-start | bytes 1474564
  48.5 25.1 %all-to-all-start.1 = ((f32[128,1,768]{2,1,0:T(1,128)}), f32[128,1,768]{2,1,0:T(1,128)S(1)}, u32[]{:S(2)}, u32[]{:S(2)}) async-start(f32[128,1,768]{2,1,0:T(1,128)} %bitcast.4), calls=%async_computation.1 | async-start | bytes 786432 | tf_op jit(solution)/shard_map/all_to_all | solution.py:815
  54.0 17.1 %copy-start.17 = (bf16[128,128]{1,0:T(8,128)(2,1)S(1)}, bf16[128,128]{1,0:T(8,128)(2,1)}, u32[]{:S(2)}) copy-start(bf16[128,128]{1,0:T(8,128)(2,1)} %constant.40.clone.reverse_ref) | copy-start | bytes 98308
  54.0 19.5 %copy-start.18 = (f32[2,128,128]{2,1,0:T(8,128)S(1)}, f32[2,128,128]{2,1,0:T(8,128)}, u32[]{:S(2)}) copy-start(f32[2,128,128]{2,1,0:T(8,128)} %constant.42.clone.turn_ref) | copy-start | bytes 393220
  54.1 16.4 %collective-permute-start.5 = (f32[18,2048]{1,0:T(8,128)S(1)}, f32[18,2048]{1,0:T(8,128)S(1)}, u32[]{:S(2)}, u32[]{:S(2)}) collective-permute-start(f32[18,2048]{1,0:T(8,128)S(1)} %copy-done.22), channel_id=1, source_target_pairs={{64,0},{65,63},{66,62},{67,61},{68,60},{69,59},{70,58},{71,57},{72... | collective-permute-start | bytes 442376 | tf_op jit(solution)/shard_map/ppermute | solution.py:900
  65.0 8.6 %copy-start.4 = (bf16[2,256,256]{2,1,0:T(8,128)(2,1)S(1)}, bf16[2,256,256]{2,1,0:T(8,128)(2,1)}, u32[]{:S(2)}) copy-start(bf16[2,256,256]{2,1,0:T(8,128)(2,1)} %constant.41.clone.in_ref.out_table_ref) | copy-start | bytes 786436
  65.0 8.6 %copy-start.13 = (bf16[2,256,256]{2,1,0:T(8,128)(2,1)S(1)}, bf16[2,256,256]{2,1,0:T(8,128)(2,1)}, u32[]{:S(2)}) copy-start(bf16[2,256,256]{2,1,0:T(8,128)(2,1)} %constant.44.clone.unmix_ref) | copy-start | bytes 786436
  65.0 8.6 %copy-start.14 = (bf16[2,256,256]{2,1,0:T(8,128)(2,1)S(1)}, bf16[2,256,256]{2,1,0:T(8,128)(2,1)}, u32[]{:S(2)}) copy-start(bf16[2,256,256]{2,1,0:T(8,128)(2,1)} %constant.43.clone.mix_ref) | copy-start | bytes 786436
  70.4 0.7 copy-start.23
  76.5 19.8 %all-to-all-start.2 = ((f32[128,8,128]{2,1,0:T(8,128)}), f32[128,8,128]{2,1,0:T(8,128)S(1)}, u32[]{:S(2)}, u32[]{:S(2)}) async-start(f32[128,8,128]{2,1,0:T(8,128)} %bitcast.6), calls=%async_computation.2 | async-start | bytes 1048576 | tf_op jit(solution)/shard_map/all_to_all | solution.py:815
  84.9 11.3 %copy-start.8 = (bf16[2,256,512]{2,1,0:T(8,128)(2,1)S(1)}, bf16[2,256,512]{2,1,0:T(8,128)(2,1)}, u32[]{:S(2)}) copy-start(bf16[2,256,512]{2,1,0:T(8,128)(2,1)} %constant.47.clone.unradix_ref) | copy-start | bytes 1572868
  84.9 11.3 %copy-start.9 = (bf16[2,256,512]{2,1,0:T(8,128)(2,1)S(1)}, bf16[2,256,512]{2,1,0:T(8,128)(2,1)}, u32[]{:S(2)}) copy-start(bf16[2,256,512]{2,1,0:T(8,128)(2,1)} %constant.45.clone.in_ref) | copy-start | bytes 1572868
  85.0 11.3 %copy-start.12 = (f32[2,2,128,128]{3,2,1,0:T(8,128)S(1)}, f32[2,2,128,128]{3,2,1,0:T(8,128)}, u32[]{:S(2)}) copy-start(f32[2,2,128,128]{3,2,1,0:T(8,128)} %constant.46.clone.turn_ref) | copy-start | bytes 786436
  98.3 11.9 %all-to-all-start.3 = ((f32[4,224,128]{2,1,0:T(8,128)}), f32[4,224,128]{2,1,0:T(8,128)S(1)}, u32[]{:S(2)}, u32[]{:S(2)}) async-start(f32[4,224,128]{2,1,0:T(8,128)} %undip.1.refs_12_), calls=%async_computation.3 | async-start | bytes 917504 | tf_op jit(solution)/shard_map/all_to_all | solution.py:815

commit v5 on v4

--- a/solution.py
+++ b/solution.py
@@ -14,6 +14,7 @@
 DAMPING = 0.5
 ALL = ("wide", "narrow")
 PLANES = 2
+UNROLL = 6
 F32 = jnp.float32
 BF16 = jnp.bfloat16
 
@@ -40,8 +41,8 @@
     unradix = np.einsum("isrnl,xz,fg->nglzisxfr", unradix, eye16, eye2).reshape(256, 512)
     y0 = np.arange(128)
     theta = 2 * np.pi * r8[:, :, None] * y0 / 1024
-    turn = np.stack([np.cos(theta), -np.sin(theta)])[:, :, None, None]
-    dip_turn = np.broadcast_to(turn, (2, 2, 16, 2, 4, 128)).reshape(2, 2, 128, 128) * factor
+    turn = np.stack([np.cos(theta), -np.sin(theta)])[:, :, None]
+    dip_turn = np.broadcast_to(turn, (2, 2, 2, 4, 128)).reshape(2, 2, 8, 128) * factor
     alt = (-1.0) ** y0
     place = np.stack([np.arange(64), 63 - np.arange(64)])
     theta = 2 * np.pi * place[:, :, None] * y0 / 128
@@ -69,21 +70,19 @@
     theta = 2 * np.pi * np.outer(a, a) / 16
     cos, sin = np.kron(np.cos(theta), eye8), np.kron(np.sin(theta), eye8)
     strike_mix = np.block([[cos, sin], [-sin, cos]])
-    strike_unmix = np.block([[cos, -sin], [sin, cos]]) * factor
     reverse = np.zeros((128, 128))
     reverse[(128 - y0) % 128, y0] = 1.0
     return {
         "radix": split_table(radix),
         "unradix": split_table(unradix),
         "dip_turn": dip_turn.astype(np.float32),
-        "undip_turn": (dip_turn / factor * 2.0).astype(np.float32),
+        "undip_turn": (dip_turn * 2.0).astype(np.float32),
         "dip_out": split_table(dip_out),
         "dip_in": split_table(dip_in),
         "strike_in": split_table(strike_in),
         "strike_out": split_table(strike_out),
         "strike_turn": strike_turn.astype(np.float32),
         "strike_mix": split_table(strike_mix),
-        "strike_unmix": split_table(strike_unmix),
         "reverse": reverse.astype(ml_dtypes.bfloat16),
     }
 
@@ -528,11 +527,18 @@
                 out.append((p1 + ones[c] * past, p2 + two * past))
         return tuple(out), tuple(twos)
 
+    def block(j, carry):
+        for k in range(UNROLL):
+            carry = step(j * UNROLL + k, carry)
+        return carry
+
     zero = jnp.zeros((8, width), F32)
-    total, _ = lax.fori_loop(
-        0, 31, step,
-        (tuple((zero, zero) for _ in range(6)), tuple(kernel_ref[1, c].astype(F32) for c in range(3))),
-    )
+    carry = (
+        tuple((zero, zero) for _ in range(6)),
+        tuple(kernel_ref[1, c].astype(F32) for c in range(3)),
+    )
+    carry = lax.fori_loop(0, 30 // UNROLL, block, carry)
+    total, _ = step(30, carry)
     values = [None] * 18
     for c in range(3):
         one = kernel_ref[32, c].astype(F32)
@@ -625,7 +631,7 @@
     z = left_dot(radix_ref, jnp.concatenate(wide, 1))
     lane = lanes((1, 128))
     for s in range(2):
-        tr, ti = turn_ref[0, s], turn_ref[1, s]
+        tr, ti = jnp.tile(turn_ref[0, s], (16, 1)), jnp.tile(turn_ref[1, s], (16, 1))
         for c in range(3):
             part = slice(c * 128, c * 128 + 128)
             zr = z[s * 128 : s * 128 + 128, part]
@@ -643,7 +649,7 @@
 
 
 def strike_kernel(
-    in_ref, turn_ref, mix_ref, reverse_ref, unmix_ref, out_table_ref,
+    in_ref, turn_ref, mix_ref, reverse_ref, out_table_ref,
     coef_ref, recv_ref, _after_ref, send_ref, spec, back, total,
 ):
     tr, ti = turn_ref[0], turn_ref[1]
@@ -686,14 +692,15 @@
                 t = a0 * s + m0 * r + coef_ref[4 + ri, c, :, wave]
                 q = a0 * r + m0 * s + coef_ref[6 + ri, c, :, wave]
                 more = (DT * DT) * (a0 * swap(t) + m0 * swap(q)) + a1 * swap(s) + m1 * swap(r)
-                total[rows, part] = t + jnp.where(upper, more, 0.0)
-    y = left_dot(unmix_ref, total[...])
+                g = t + jnp.where(upper, more, 0.0)
+                total[rows, part] = g if ri == 0 else -g
+    y = left_dot(mix_ref, total[...])
     owner = rows_of((128, 128))
     wide_lane = lanes((128, 128))
     extra = [jnp.zeros((128, 128), F32)] * 2
     for c in range(3):
         part = slice(c * 128, c * 128 + 128)
-        yr, yi = y[:128, part], y[128:, part]
+        yr, yi = y[:128, part], -y[128:, part]
         turned = jnp.concatenate([yr * tr + yi * ti, yi * tr - yr * ti], 1)
         high, low = halves(turned)
         res = dot(out_table_ref[0], high, (1, 1)) + (
@@ -730,7 +737,7 @@
             if s == 0:
                 fix = alt * im[:, 0:1] - 0.5 * re[:, 0:1]
                 hr = hr + jnp.where(lax.rem(row, 4) == 0, fix, 0.0)
-            tr, ti = turn_ref[0, s], turn_ref[1, s]
+            tr, ti = jnp.tile(turn_ref[0, s], (16, 1)), jnp.tile(turn_ref[1, s], (16, 1))
             stacks[s].append(hr * tr + hi * ti)
             stacks[2 + s].append(hi * tr - hr * ti)
     stacked = jnp.concatenate([jnp.concatenate(part, 1) for part in stacks], 0)
@@ -846,11 +853,11 @@
         grid=(4,),
         in_specs=[planes(4), planes(4), slabs(4), full((8, 32))],
         out_specs=[full(s.shape) for s in edge_shapes] + [full((64, 256))],
-        out_shape=edge_shapes + [shape_of(64, 256)],
+        out_shape=edge_shapes + [hbm_shape(64, 256)],
         cost_estimate=pl.CostEstimate(flops=0, bytes_accessed=8000000, transcendentals=0),
         compiler_params=pltpu.CompilerParams(vmem_limit_bytes=16 << 20),
             name="edges",
-    )(u, v, region, flags)
+    )(u, v, region, in_hbm(flags))
     halo_one = halo(first, last, left, right)
     plastic = in_hbm(plastic)
 
@@ -939,7 +946,7 @@
         shape_of(1024, 128),
         (
             t["strike_in"], t["strike_turn"], t["strike_mix"], t["reverse"],
-            t["strike_unmix"], t["strike_out"], coefficients, waves,
+            t["strike_out"], coefficients, waves,
         ),
         scratch=[pltpu.VMEM((256, 384), F32)] * 3,
         after=[new_u],

time: 114 us -> 112 us (0.982)
  local copies, waits for them, and re-layouts: 2.09 us -> 0.78 us
    pallas_call x2, Pallas kernels: 11 us -> 9.66 us  [sums(): pl.pallas_call(history_kernel, grid=(steps,), in_specs=[SMEM, pl.BlockSpe...]
    unnamed x48 -> x40, local copies, waits for them, and re-layouts: 2.09 us -> 0.78 us
where the time goes in v5:
time: 112 us; the launch traced here: 111 us
  Pallas kernels  52.6 us (47%)
  starting transfers between devices  43.2 us (39%)
  waiting for transfers between devices  12.9 us (12%)
    all_to_all x4, starting transfers between devices, exchange(): return lax.all_to_all(x, axis, split_axis=0, concat_axis=0, tiled=True)  20.5 us
    pallas_call x5, Pallas kernels, call(): pl.pallas_call(body, in_specs=[SMEM] * smem + [full(x.shape) for x in arg...  11.2 us
    pallas_call x2, Pallas kernels, later(): pl.pallas_call(functools.partial(step_two_kernel, start), grid=((stop - s...  11 us
    pallas_call x2, Pallas kernels, sums(): pl.pallas_call(history_kernel, grid=(steps,), in_specs=[SMEM, pl.BlockSpe...  9.66 us
    ppermute x1, starting transfers between devices, body(): main = lax.ppermute(main, ALL, [(i, 127 - i) for i in range(128)])  9.65 us
    pallas_call x1, Pallas kernels, body(): pl.pallas_call(step_one_kernel, grid=(16 // PLANES,), in_specs=[SMEM, SME...  9.46 us
    all_to_all x4, waiting for transfers between devices, exchange(): return lax.all_to_all(x, axis, split_axis=0, concat_axis=0, tiled=True)  7.41 us
    pallas_call x1, Pallas kernels, body(): pl.pallas_call(edges_kernel, grid=(4,), in_specs=[planes(4), planes(4), s...  6.41 us
  transfers between devices with their start and end apart: 10, of which 3 were waited for; matrix products, arithmetic and copies ran while one was open for 1% of the time, Pallas kernels for 33%

profile of v5, /device:TPU:1, one launch (start us, length us, event | category | flops | bytes accessed | tf_op | source)
XLA Modules:
  0.0 111.0 jit_solution(4688779462449482908)
XLA Ops:
  0.6 6.4 %edges.1 = (f32[168,256]{1,0:T(8,128)S(1)}, f32[168,256]{1,0:T(8,128)S(1)}, f32[2,64,128]{2,1,0:T(8,128)S(1)}, f32[2,64,128]{2,1,0:T(8,128)S(1)}, f32[64,256]{1,0:T(8,128)}) custom-call(f32[3,16,64,256]{3,2,1,0:T(8,128)} %u_ref.5, f32[3,16,64,256]{3,2,1,0:T(8,128)} %v_ref.5, s32[16,64,256]{2,1,0:T(8,128)} %region_ref.7, s32[8,32]{1,0:T(8,128)} %flags_ref.1), custom_call_target="tpu_custom_call" | custom-call | bytes 8000000 | tf_op jit(solution)/shard_map/edges/pallas_call | solution.py:851
  7.1 0.0 copy-start.16
  7.1 4.4 %collective-permute-start = (f32[168,256]{1,0:T(8,128)S(1)}, f32[168,256]{1,0:T(8,128)S(1)}, u32[]{:S(2)}, u32[]{:S(2)}) collective-permute-start(f32[168,256]{1,0:T(8,128)S(1)} %get-tuple-element.24.last_ref), channel_id=1, source_target_pairs={{0,4},{4,8},{8,12},{12,16},{16,20},{20,24},{24,28},{28,32},{32,36}... | collective-permute-start | bytes 516104 | tf_op jit(solution)/shard_map/ppermute | solution.py:812
  11.4 1.3 %collective-permute-start.1 = (f32[168,256]{1,0:T(8,128)S(1)}, f32[168,256]{1,0:T(8,128)S(1)}, u32[]{:S(2)}, u32[]{:S(2)}) collective-permute-start(f32[168,256]{1,0:T(8,128)S(1)} %get-tuple-element.25.first_ref), channel_id=1, source_target_pairs={{4,0},{8,4},{12,8},{16,12},{20,16},{24,20},{28,24},{32,28},{36,32}... | collective-permute-start | bytes 516104 | tf_op jit(solution)/shard_map/ppermute | solution.py:813
  12.7 4.0 %collective-permute-start.2 = (f32[2,64,128]{2,1,0:T(8,128)S(1)}, f32[2,64,128]{2,1,0:T(8,128)S(1)}, u32[]{:S(2)}, u32[]{:S(2)}) collective-permute-start(f32[2,64,128]{2,1,0:T(8,128)S(1)} %get-tuple-element.26.right_ref), channel_id=1, source_target_pairs={{0,1},{1,2},{2,3},{4,5},{5,6},{6,7},{8,9},{9,10},{10,11},{12,13},{... | collective-permute-start | bytes 196616 | tf_op jit(solution)/shard_map/ppermute | solution.py:816
  16.7 1.9 %collective-permute-start.3 = (f32[2,64,128]{2,1,0:T(8,128)S(1)}, f32[2,64,128]{2,1,0:T(8,128)S(1)}, u32[]{:S(2)}, u32[]{:S(2)}) collective-permute-start(f32[2,64,128]{2,1,0:T(8,128)S(1)} %get-tuple-element.27.left_ref), channel_id=1, source_target_pairs={{1,0},{2,1},{3,2},{5,4},{6,5},{7,6},{9,8},{10,9},{11,10},{13,12},{... | collective-permute-start | bytes 196616 | tf_op jit(solution)/shard_map/ppermute | solution.py:817
  18.6 0.6 pad_add_fusion.where_ref
  19.3 4.8 %history.2 = (f32[72,2048]{1,0:T(8,128)}, f32[72,2048]{1,0:T(8,128)}, f32[18,2048]{1,0:T(8,128)}) custom-call(s32[4]{0:T(128)} %pad_add_fusion.where_ref, bf16[33,3,8,2048]{3,2,1,0:T(8,128)(2,1)} %kernel_ref.3, bf16[32,2,3,8,2048]{4,3,2,1,0:T(8,128)(2,1)} %history_ref.3), custom_call_target="tpu_custom_call" | custom-call | bytes 5500000 | tf_op jit(solution)/shard_map/history/pallas_call | solution.py:870
  24.1 0.0 copy-done.11
  24.1 0.0 copy-done.12
  24.1 0.0 copy-done.15
  24.1 0.0 copy-done.16
  24.1 0.0 collective-permute-done.2.left_ref.west_ref
  24.1 0.0 copy-start.4
  24.1 0.0 collective-permute-done.3.right_ref.east_ref
  24.1 0.0 copy-start.5
  24.1 0.0 collective-permute-done.top_ref
  24.1 0.0 copy-start.1
  24.1 0.0 collective-permute-done.1.bottom_ref
  24.2 0.0 copy-start.2
  24.2 2.3 %slip.1 = f32[4,240,128]{2,1,0:T(8,128)} custom-call(f32[4]{0:T(128)} %shear_ref.7, f32[4]{0:T(128)} %yields_ref.7, f32[3,16,64,256]{3,2,1,0:T(8,128)} %u_ref.5, f32[3,16,64,256]{3,2,1,0:T(8,128)} %v_ref.5, s32[16,64,256]{2,1,0:T(8,128)} %region_ref.7, f32[64,256]{1,0:T(8,128)} %get-tuple-element.23.plastic_ref.refs_5_, ...), custom_call_target="tpu_custom_call" | custom-call | bytes 1500000 | tf_op jit(solution)/shard_map/slip/pallas_call | solution.py:892
  26.4 3.5 %all-to-all-start = ((f32[4,240,128]{2,1,0:T(8,128)}), f32[4,240,128]{2,1,0:T(8,128)S(1)}, u32[]{:S(2)}, u32[]{:S(2)}) async-start(f32[4,240,128]{2,1,0:T(8,128)} %slip.1), calls=%async_computation | async-start | bytes 983040 | tf_op jit(solution)/shard_map/all_to_all | solution.py:822
  29.9 0.0 copy-start.8
  29.9 0.0 copy-start.9
  29.9 0.0 copy-start.18
  29.9 4.9 %history.3 = (f32[72,2048]{1,0:T(8,128)}, f32[72,2048]{1,0:T(8,128)}, f32[18,2048]{1,0:T(8,128)}) custom-call(s32[4]{0:T(128)} %pad_add_fusion.where_ref, bf16[33,3,8,2048]{3,2,1,0:T(8,128)(2,1)} %kernel_ref.3, bf16[32,2,3,8,2048]{4,3,2,1,0:T(8,128)(2,1)} %history_ref.3, ...), custom_call_target="tpu_custom_call", output_to_operand_aliasing={{0}: (3, {}), {1}: (4, {}), {2}: (5, {})} | custom-call | bytes 5500000 | tf_op jit(solution)/shard_map/history/pallas_call | solution.py:870
  34.8 9.7 %collective-permute-start.4 = (f32[72,2048]{1,0:T(8,128)}, f32[72,2048]{1,0:T(8,128)}, u32[]{:S(2)}, u32[]{:S(2)}) collective-permute-start(f32[72,2048]{1,0:T(8,128)} %get-tuple-element.38), channel_id=1, source_target_pairs={{0,127},{1,126},{2,125},{3,124},{4,123},{5,122},{6,121},{7,120},{8... | collective-permute-start | bytes 1769480 | tf_op jit(solution)/shard_map/ppermute | solution.py:906
  44.4 0.0 all-to-all-done.recv_ref.lines_ref
  44.5 0.0 copy-done.8
  44.5 0.0 copy-done.9
  44.5 0.0 copy-done.18
  44.5 1.9 %dip.1._after_ref = f32[768,128]{1,0:T(8,128)} custom-call(bf16[2,512,256]{2,1,0:T(8,128)(2,1)S(1)} %copy-done.8, f32[2,2,8,128]{3,2,1,0:T(8,128)S(1)} %copy-done.18, bf16[2,2,136,256]{3,2,1,0:T(8,128)(2,1)S(1)} %copy-done.9, f32[4,240,128]{2,1,0:T(8,128)S(1)} %all-to-all-done.recv_ref.lines_ref, f32[72,2048]{1,0:T(8,128)} %get-tuple-element.31._after_ref.own_ref), custom_call_target="tpu_custom_call" | custom-call | bytes 2506752 | tf_op jit(solution)/shard_map/dip/pallas_call | solution.py:795
  46.3 5.6 %all-to-all-start.1 = ((f32[128,1,768]{2,1,0:T(1,128)}), f32[128,1,768]{2,1,0:T(1,128)S(1)}, u32[]{:S(2)}, u32[]{:S(2)}) async-start(f32[128,1,768]{2,1,0:T(1,128)} %bitcast.4), calls=%async_computation.1 | async-start | bytes 786432 | tf_op jit(solution)/shard_map/all_to_all | solution.py:822
  51.9 0.0 copy-start.13
  51.9 0.0 copy-start.14
  51.9 1.4 %collective-permute-start.5 = (f32[18,2048]{1,0:T(8,128)}, f32[18,2048]{1,0:T(8,128)S(1)}, u32[]{:S(2)}, u32[]{:S(2)}) collective-permute-start(f32[18,2048]{1,0:T(8,128)} %get-tuple-element.39), channel_id=1, source_target_pairs={{64,0},{65,63},{66,62},{67,61},{68,60},{69,59},{70,58},{71,57},{72... | collective-permute-start | bytes 442376 | tf_op jit(solution)/shard_map/ppermute | solution.py:907
  53.4 0.0 copy-done.4
  53.4 0.0 copy-done.5
  53.4 0.0 copy-done.1
  53.4 9.5 %step_one.1 = (f32[3,16,64,256]{3,2,1,0:T(8,128)}, f32[3,16,64,256]{3,2,1,0:T(8,128)}) custom-call(f32[4]{0:T(128)} %shear_ref.7, f32[4]{0:T(128)} %yields_ref.7, f32[3,16,64,256]{3,2,1,0:T(8,128)} %u_ref.5, f32[3,16,64,256]{3,2,1,0:T(8,128)} %v_ref.5, s32[16,64,256]{2,1,0:T(8,128)} %region_ref.7, f32[64,256]{1,0:T(8,128)} %get-tuple-element.23.plastic_ref.refs_5_, ...), custom_call_target="tpu_custom_call" | custom-call | bytes 14000000 | tf_op jit(solution)/shard_map/step_one/pallas_call | solution.py:915
  62.9 0.0 copy-start.3
  62.9 0.0 copy-start.10
  62.9 5.4 %collective-permute-done.5.edge_ref = f32[18,2048]{1,0:T(8,128)S(1)} collective-permute-done((f32[18,2048]{1,0:T(8,128)}, f32[18,2048]{1,0:T(8,128)S(1)}, u32[]{:S(2)}, u32[]{:S(2)}) %collective-permute-start.5) | collective-permute-done | bytes 147488 | tf_op jit(solution)/shard_map/ppermute | solution.py:907
  68.3 0.0 collective-permute-done.4.main_ref
  68.3 0.7 copy-done.19
  69.0 2.4 %mirror.1.coef_ref = f32[8,3,8,2048]{3,2,1,0:T(8,128)S(1)} custom-call(s32[4]{0:T(128)} %pad_add_fusion.where_ref, bf16[128,128]{1,0:T(8,128)(2,1)S(1)} %copy-done.13, f32[72,2048]{1,0:T(8,128)} %get-tuple-element.31._after_ref.own_ref, f32[72,2048]{1,0:T(8,128)} %collective-permute-done.4.main_ref, f32[18,2048]{1,0:T(8,128)} %copy-done.19), custom_call_target="tpu_custom_call" | custom-call | bytes 2965520 | tf_op jit(solution)/shard_map/mirror/pallas_call | solution.py:795
  71.4 0.0 all-to-all-done.1
  71.4 0.0 copy-done.14
  71.4 0.0 copy-done.3
  71.5 0.0 copy-done.10
  71.5 2.9 %strike.1.refs_10_ = f32[1024,128]{1,0:T(8,128)} custom-call(bf16[2,256,256]{2,1,0:T(8,128)(2,1)S(1)} %copy-done.3, f32[2,128,128]{2,1,0:T(8,128)S(1)} %copy-done.14, bf16[2,256,256]{2,1,0:T(8,128)(2,1)S(1)} %copy-done.10, bf16[128,128]{1,0:T(8,128)(2,1)S(1)} %copy-done.13, bf16[2,256,256]{2,1,0:T(8,128)(2,1)S(1)} %copy-done.3, ...), custom_call_target="tpu_custom_call" | custom-call | bytes 4259840 | tf_op jit(solution)/shard_map/strike/pallas_call | solution.py:795
  74.3 6.8 %all-to-all-start.2 = ((f32[128,8,128]{2,1,0:T(8,128)}), f32[128,8,128]{2,1,0:T(8,128)S(1)}, u32[]{:S(2)}, u32[]{:S(2)}) async-start(f32[128,8,128]{2,1,0:T(8,128)} %bitcast.6), calls=%async_computation.2 | async-start | bytes 1048576 | tf_op jit(solution)/shard_map/all_to_all | solution.py:822
  81.2 2.0 %beside.1 = (f32[48,256]{1,0:T(8,128)S(1)}, f32[48,256]{1,0:T(8,128)S(1)}, f32[64,128]{1,0:T(8,128)S(1)}, f32[64,128]{1,0:T(8,128)S(1)}) custom-call(s32[4]{0:T(128)} %pad_add_fusion.where_ref, f32[4]{0:T(128)} %shear_ref.7, f32[4]{0:T(128)} %yields_ref.7, f32[168,256]{1,0:T(8,128)} %copy-done.11, f32[168,256]{1,0:T(8,128)} %copy-done.12, ...), custom_call_target="tpu_custom_call" | custom-call | bytes 1605680 | tf_op jit(solution)/shard_map/beside/pallas_call | solution.py:795
  83.1 0.0 copy-start.6
  83.1 0.0 copy-start.7
  83.2 0.0 copy-start.17
  83.2 5.9 %step_two.2 = (f32[3,16,64,256]{3,2,1,0:T(8,128)}, f32[3,16,64,256]{3,2,1,0:T(8,128)}) custom-call(f32[4]{0:T(128)} %shear_ref.7, f32[4]{0:T(128)} %yields_ref.7, f32[3,16,64,256]{3,2,1,0:T(8,128)} %get-tuple-element.32._after_ref.refs_2_.u_ref, f32[3,16,64,256]{3,2,1,0:T(8,128)} %get-tuple-element.33.refs_3_.v_ref, s32[16,64,256]{2,1,0:T(8,128)} %region_ref.7, ...), custom_call_target="tpu_custom_call" | custom-call | bytes 6400000 | tf_op jit(solution)/shard_map/step_two/pallas_call | solution.py:958
  89.0 5.4 %all-to-all-done.2 = f32[128,8,128]{2,1,0:T(8,128)S(1)} async-done(((f32[128,8,128]{2,1,0:T(8,128)}), f32[128,8,128]{2,1,0:T(8,128)S(1)}, u32[]{:S(2)}, u32[]{:S(2)}) %all-to-all-start.2) | async-done | bytes 524320 | tf_op jit(solution)/shard_map/all_to_all | solution.py:822
  94.5 0.0 copy-done.17
  94.5 2.1 %undip.1.refs_12_ = f32[4,224,128]{2,1,0:T(8,128)} custom-call(bf16[2,256,512]{2,1,0:T(8,128)(2,1)S(1)} %copy-done.7, f32[2,2,8,128]{3,2,1,0:T(8,128)S(1)} %copy-done.17, bf16[2,256,512]{2,1,0:T(8,128)(2,1)S(1)} %copy-done.6, f32[1024,128]{1,0:T(8,128)S(1)} %bitcast.8, f32[3,16,64,256]{3,2,1,0:T(8,128)} %get-tuple-element.40._after_ref.refs_10_), custom_call_target="tpu_custom_call" | custom-call | bytes 3096576 | tf_op jit(solution)/shard_map/undip/pallas_call | solution.py:795
  96.5 4.7 %all-to-all-start.3 = ((f32[4,224,128]{2,1,0:T(8,128)}), f32[4,224,128]{2,1,0:T(8,128)S(1)}, u32[]{:S(2)}, u32[]{:S(2)}) async-start(f32[4,224,128]{2,1,0:T(8,128)} %undip.1.refs_12_), calls=%async_computation.3 | async-start | bytes 917504 | tf_op jit(solution)/shard_map/all_to_all | solution.py:822
  101.3 5.2 %step_two.3 = (f32[3,16,64,256]{3,2,1,0:T(8,128)}, f32[3,16,64,256]{3,2,1,0:T(8,128)}) custom-call(f32[4]{0:T(128)} %shear_ref.7, f32[4]{0:T(128)} %yields_ref.7, f32[3,16,64,256]{3,2,1,0:T(8,128)} %get-tuple-element.32._after_ref.refs_2_.u_ref, f32[3,16,64,256]{3,2,1,0:T(8,128)} %get-tuple-element.33.refs_3_.v_ref, ...), custom_call_target="tpu_custom_call", output_to_operand_aliasing={{0}: (10, {}), {1}: (11, {})} | custom-call | bytes 4800000 | tf_op jit(solution)/shard_map/step_two/pallas_call | solution.py:958
  106.4 2.0 %all-to-all-done.3.recv_ref = f32[4,224,128]{2,1,0:T(8,128)S(1)} async-done(((f32[4,224,128]{2,1,0:T(8,128)}), f32[4,224,128]{2,1,0:T(8,128)S(1)}, u32[]{:S(2)}, u32[]{:S(2)}) %all-to-all-start.3) | async-done | bytes 458784 | tf_op jit(solution)/shard_map/all_to_all | solution.py:822
  108.4 2.6 %last.1 = (f32[3,16,64,256]{3,2,1,0:T(8,128)}, f32[3,16,64,256]{3,2,1,0:T(8,128)}) custom-call(f32[4]{0:T(128)} %shear_ref.7, f32[4]{0:T(128)} %yields_ref.7, f32[3,16,64,256]{3,2,1,0:T(8,128)} %get-tuple-element.32._after_ref.refs_2_.u_ref, f32[3,16,64,256]{3,2,1,0:T(8,128)} %get-tuple-element.33.refs_3_.v_ref, ...), custom_call_target="tpu_custom_call", output_to_operand_aliasing={{0}: (11, {}), {1}: (12, {})} | custom-call | bytes 4000000 | tf_op jit(solution)/shard_map/last/pallas_call | solution.py:987
  (10 shorter events, 0.0 us)
Async XLA Ops:
  7.0 17.0 %copy-start.11 = (f32[168,256]{1,0:T(8,128)}, f32[168,256]{1,0:T(8,128)S(1)}, u32[]{:S(2)}) copy-start(f32[168,256]{1,0:T(8,128)S(1)} %get-tuple-element.25.first_ref) | copy-start | bytes 516100
  7.0 17.0 %copy-start.12 = (f32[168,256]{1,0:T(8,128)}, f32[168,256]{1,0:T(8,128)S(1)}, u32[]{:S(2)}) copy-start(f32[168,256]{1,0:T(8,128)S(1)} %get-tuple-element.24.last_ref) | copy-start | bytes 516100
  7.0 17.0 %copy-start.15 = (f32[2,64,128]{2,1,0:T(8,128)}, f32[2,64,128]{2,1,0:T(8,128)S(1)}, u32[]{:S(2)}) copy-start(f32[2,64,128]{2,1,0:T(8,128)S(1)} %get-tuple-element.27.left_ref) | copy-start | bytes 196612
  7.1 17.0 %copy-start.16 = (f32[2,64,128]{2,1,0:T(8,128)}, f32[2,64,128]{2,1,0:T(8,128)S(1)}, u32[]{:S(2)}) copy-start(f32[2,64,128]{2,1,0:T(8,128)S(1)} %get-tuple-element.26.right_ref) | copy-start | bytes 196612
  7.1 17.1 %collective-permute-start = (f32[168,256]{1,0:T(8,128)S(1)}, f32[168,256]{1,0:T(8,128)S(1)}, u32[]{:S(2)}, u32[]{:S(2)}) collective-permute-start(f32[168,256]{1,0:T(8,128)S(1)} %get-tuple-element.24.last_ref), channel_id=1, source_target_pairs={{0,4},{4,8},{8,12},{12,16},{16,20},{20,24},{24,28},{28,32},{32,36}... | collective-permute-start | bytes 516104 | tf_op jit(solution)/shard_map/ppermute | solution.py:812
  11.4 12.7 %collective-permute-start.1 = (f32[168,256]{1,0:T(8,128)S(1)}, f32[168,256]{1,0:T(8,128)S(1)}, u32[]{:S(2)}, u32[]{:S(2)}) collective-permute-start(f32[168,256]{1,0:T(8,128)S(1)} %get-tuple-element.25.first_ref), channel_id=1, source_target_pairs={{4,0},{8,4},{12,8},{16,12},{20,16},{24,20},{28,24},{32,28},{36,32}... | collective-permute-start | bytes 516104 | tf_op jit(solution)/shard_map/ppermute | solution.py:813
  12.7 11.3 %collective-permute-start.2 = (f32[2,64,128]{2,1,0:T(8,128)S(1)}, f32[2,64,128]{2,1,0:T(8,128)S(1)}, u32[]{:S(2)}, u32[]{:S(2)}) collective-permute-start(f32[2,64,128]{2,1,0:T(8,128)S(1)} %get-tuple-element.26.right_ref), channel_id=1, source_target_pairs={{0,1},{1,2},{2,3},{4,5},{5,6},{6,7},{8,9},{9,10},{10,11},{12,13},{... | collective-permute-start | bytes 196616 | tf_op jit(solution)/shard_map/ppermute | solution.py:816
  16.7 7.4 %collective-permute-start.3 = (f32[2,64,128]{2,1,0:T(8,128)S(1)}, f32[2,64,128]{2,1,0:T(8,128)S(1)}, u32[]{:S(2)}, u32[]{:S(2)}) collective-permute-start(f32[2,64,128]{2,1,0:T(8,128)S(1)} %get-tuple-element.27.left_ref), channel_id=1, source_target_pairs={{1,0},{2,1},{3,2},{5,4},{6,5},{7,6},{9,8},{10,9},{11,10},{13,12},{... | collective-permute-start | bytes 196616 | tf_op jit(solution)/shard_map/ppermute | solution.py:817
  24.1 29.3 %copy-start.4 = (f32[2,64,128]{2,1,0:T(8,128)}, f32[2,64,128]{2,1,0:T(8,128)S(1)}, u32[]{:S(2)}) copy-start(f32[2,64,128]{2,1,0:T(8,128)S(1)} %collective-permute-done.2.left_ref.west_ref) | copy-start | bytes 196612
  24.1 29.3 %copy-start.5 = (f32[2,64,128]{2,1,0:T(8,128)}, f32[2,64,128]{2,1,0:T(8,128)S(1)}, u32[]{:S(2)}) copy-start(f32[2,64,128]{2,1,0:T(8,128)S(1)} %collective-permute-done.3.right_ref.east_ref) | copy-start | bytes 196612
  24.1 29.2 %copy-start.1 = (f32[168,256]{1,0:T(8,128)}, f32[168,256]{1,0:T(8,128)S(1)}, u32[]{:S(2)}) copy-start(f32[168,256]{1,0:T(8,128)S(1)} %collective-permute-done.top_ref) | copy-start | bytes 516100
  24.2 29.2 %copy-start.2 = (f32[168,256]{1,0:T(8,128)}, f32[168,256]{1,0:T(8,128)S(1)}, u32[]{:S(2)}) copy-start(f32[168,256]{1,0:T(8,128)S(1)} %collective-permute-done.1.bottom_ref) | copy-start | bytes 516100
  26.4 18.0 %all-to-all-start = ((f32[4,240,128]{2,1,0:T(8,128)}), f32[4,240,128]{2,1,0:T(8,128)S(1)}, u32[]{:S(2)}, u32[]{:S(2)}) async-start(f32[4,240,128]{2,1,0:T(8,128)} %slip.1), calls=%async_computation | async-start | bytes 983040 | tf_op jit(solution)/shard_map/all_to_all | solution.py:822
  29.9 14.6 %copy-start.8 = (bf16[2,512,256]{2,1,0:T(8,128)(2,1)S(1)}, bf16[2,512,256]{2,1,0:T(8,128)(2,1)}, u32[]{:S(2)}) copy-start(bf16[2,512,256]{2,1,0:T(8,128)(2,1)} %constant.35.clone.radix_ref) | copy-start | bytes 1572868
  29.9 14.6 %copy-start.9 = (bf16[2,2,136,256]{3,2,1,0:T(8,128)(2,1)S(1)}, bf16[2,2,136,256]{3,2,1,0:T(8,128)(2,1)}, u32[]{:S(2)}) copy-start(bf16[2,2,136,256]{3,2,1,0:T(8,128)(2,1)} %constant.37.clone.out_table_ref) | copy-start | bytes 835588
  29.9 14.5 %copy-start.18 = (f32[2,2,8,128]{3,2,1,0:T(8,128)S(1)}, f32[2,2,8,128]{3,2,1,0:T(8,128)}, u32[]{:S(2)}) copy-start(f32[2,2,8,128]{3,2,1,0:T(8,128)} %constant.36.clone.turn_ref) | copy-start | bytes 49156
  34.8 33.5 %collective-permute-start.4 = (f32[72,2048]{1,0:T(8,128)}, f32[72,2048]{1,0:T(8,128)}, u32[]{:S(2)}, u32[]{:S(2)}) collective-permute-start(f32[72,2048]{1,0:T(8,128)} %get-tuple-element.38), channel_id=1, source_target_pairs={{0,127},{1,126},{2,125},{3,124},{4,123},{5,122},{6,121},{7,120},{8... | collective-permute-start | bytes 1769480 | tf_op jit(solution)/shard_map/ppermute | solution.py:906
  44.5 18.4 %copy-start = (f32[4,240,128]{2,1,0:T(8,128)}, f32[4,240,128]{2,1,0:T(8,128)S(1)}, u32[]{:S(2)}) copy-start(f32[4,240,128]{2,1,0:T(8,128)S(1)} %all-to-all-done.recv_ref.lines_ref) | copy-start | bytes 1474564
  46.3 25.1 %all-to-all-start.1 = ((f32[128,1,768]{2,1,0:T(1,128)}), f32[128,1,768]{2,1,0:T(1,128)S(1)}, u32[]{:S(2)}, u32[]{:S(2)}) async-start(f32[128,1,768]{2,1,0:T(1,128)} %bitcast.4), calls=%async_computation.1 | async-start | bytes 786432 | tf_op jit(solution)/shard_map/all_to_all | solution.py:822
  51.9 17.1 %copy-start.13 = (bf16[128,128]{1,0:T(8,128)(2,1)S(1)}, bf16[128,128]{1,0:T(8,128)(2,1)}, u32[]{:S(2)}) copy-start(bf16[128,128]{1,0:T(8,128)(2,1)} %constant.38.clone.reverse_ref) | copy-start | bytes 98308
  51.9 19.5 %copy-start.14 = (f32[2,128,128]{2,1,0:T(8,128)S(1)}, f32[2,128,128]{2,1,0:T(8,128)}, u32[]{:S(2)}) copy-start(f32[2,128,128]{2,1,0:T(8,128)} %constant.40.clone.turn_ref) | copy-start | bytes 393220
  51.9 16.4 %collective-permute-start.5 = (f32[18,2048]{1,0:T(8,128)}, f32[18,2048]{1,0:T(8,128)S(1)}, u32[]{:S(2)}, u32[]{:S(2)}) collective-permute-start(f32[18,2048]{1,0:T(8,128)} %get-tuple-element.39), channel_id=1, source_target_pairs={{64,0},{65,63},{66,62},{67,61},{68,60},{69,59},{70,58},{71,57},{72... | collective-permute-start | bytes 442376 | tf_op jit(solution)/shard_map/ppermute | solution.py:907
  62.9 8.6 %copy-start.3 = (bf16[2,256,256]{2,1,0:T(8,128)(2,1)S(1)}, bf16[2,256,256]{2,1,0:T(8,128)(2,1)}, u32[]{:S(2)}) copy-start(bf16[2,256,256]{2,1,0:T(8,128)(2,1)} %constant.39.clone.in_ref.out_table_ref) | copy-start | bytes 786436
  62.9 8.6 %copy-start.10 = (bf16[2,256,256]{2,1,0:T(8,128)(2,1)S(1)}, bf16[2,256,256]{2,1,0:T(8,128)(2,1)}, u32[]{:S(2)}) copy-start(bf16[2,256,256]{2,1,0:T(8,128)(2,1)} %constant.41.clone.mix_ref) | copy-start | bytes 786436
  68.3 0.7 copy-start.19
  74.3 20.1 %all-to-all-start.2 = ((f32[128,8,128]{2,1,0:T(8,128)}), f32[128,8,128]{2,1,0:T(8,128)S(1)}, u32[]{:S(2)}, u32[]{:S(2)}) async-start(f32[128,8,128]{2,1,0:T(8,128)} %bitcast.6), calls=%async_computation.2 | async-start | bytes 1048576 | tf_op jit(solution)/shard_map/all_to_all | solution.py:822
  83.1 11.3 %copy-start.6 = (bf16[2,256,512]{2,1,0:T(8,128)(2,1)S(1)}, bf16[2,256,512]{2,1,0:T(8,128)(2,1)}, u32[]{:S(2)}) copy-start(bf16[2,256,512]{2,1,0:T(8,128)(2,1)} %constant.44.clone.unradix_ref) | copy-start | bytes 1572868
  83.1 11.3 %copy-start.7 = (bf16[2,256,512]{2,1,0:T(8,128)(2,1)S(1)}, bf16[2,256,512]{2,1,0:T(8,128)(2,1)}, u32[]{:S(2)}) copy-start(bf16[2,256,512]{2,1,0:T(8,128)(2,1)} %constant.42.clone.in_ref) | copy-start | bytes 1572868
  83.2 11.3 %copy-start.17 = (f32[2,2,8,128]{3,2,1,0:T(8,128)S(1)}, f32[2,2,8,128]{3,2,1,0:T(8,128)}, u32[]{:S(2)}) copy-start(f32[2,2,8,128]{3,2,1,0:T(8,128)} %constant.43.clone.turn_ref) | copy-start | bytes 49156
  96.5 11.9 %all-to-all-start.3 = ((f32[4,224,128]{2,1,0:T(8,128)}), f32[4,224,128]{2,1,0:T(8,128)S(1)}, u32[]{:S(2)}, u32[]{:S(2)}) async-start(f32[4,224,128]{2,1,0:T(8,128)} %undip.1.refs_12_), calls=%async_computation.3 | async-start | bytes 917504 | tf_op jit(solution)/shard_map/all_to_all | solution.py:822

commit v6 on v5

--- a/solution.py
+++ b/solution.py
@@ -10,11 +10,12 @@
 from jax.experimental.pallas import tpu as pltpu
 from jax.sharding import PartitionSpec as P
 
+
 DT = 0.1
 DAMPING = 0.5
 ALL = ("wide", "narrow")
-PLANES = 2
 UNROLL = 6
+CUTS = (4, 11)
 F32 = jnp.float32
 BF16 = jnp.bfloat16
 
@@ -29,7 +30,6 @@
 def make_tables():
     factor = 1.0 / math.sqrt(2048 * 1024)
     eye2 = np.eye(2)
-    eye4 = np.eye(4)
     eye8 = np.eye(8)
     eye16 = np.eye(16)
     r8 = np.arange(8).reshape(2, 4)
@@ -380,74 +380,110 @@
                     send_ref[n, start : start + 8, :] = values[:, half * 128 : half * 128 + 128]
 
 
-def step_one_kernel(
-    shear_ref, yields_ref, u_ref, v_ref, region_ref, plastic_ref,
-    top_ref, bottom_ref, left_ref, right_ref, _after_ref,
-    new_u_ref, new_v_ref,
-):
-    step = pl.program_id(0)
-
-    halo_refs = (top_ref, bottom_ref, left_ref.at[0], right_ref.at[0])
+def both_steps_kernel(low, high, *refs):
+    (shear_ref, yields_ref, u_hbm, v_hbm, region_hbm, plastic_ref) = refs[:6]
+    halo_one = (refs[6], refs[7], refs[8].at[0], refs[9].at[0])
+    halo_two = refs[10:14]
+    head = low == 2
+    count = 4 if head else 2
+    outs, scratch = refs[-10 - count : -10], refs[-10:]
+    us, vs, rs, new_us, new_vs, out_us, out_vs, in_sems, out_sems, head_sems = scratch
     table = label_table(shear_ref, yields_ref)
-    for k in range(PLANES):
-        z = step * PLANES + k
+    start = 0 if head else low - 1
+    stop = min(high, 15)
+    begin, end = max(start - 1, 0), min(stop + 1, 15)
+
+    def bring(z):
+        return (
+            pltpu.make_async_copy(u_hbm.at[:, z], us.at[:, z - begin], in_sems.at[z - begin, 0]),
+            pltpu.make_async_copy(v_hbm.at[:, z], vs.at[:, z - begin], in_sems.at[z - begin, 1]),
+            pltpu.make_async_copy(region_hbm.at[z], rs.at[z - begin], in_sems.at[z - begin, 2]),
+        )
+
+    def put(z):
+        return (
+            pltpu.make_async_copy(out_us.at[:, z - low], outs[0].at[:, z], out_sems.at[z - low, 0]),
+            pltpu.make_async_copy(out_vs.at[:, z - low], outs[1].at[:, z], out_sems.at[z - low, 1]),
+        )
+
+    for z in range(begin, end + 1):
+        for copy in bring(z):
+            copy.start()
+
+    def ready(z):
+        for copy in bring(z):
+            copy.wait()
+
+    for z in range(begin, start + 1):
+        ready(z)
+
+    @pl.loop(start, stop + 1)
+    def _(z):
+        @pl.when(z < end)
+        def _():
+            ready(z + 1)
+
         damping = jnp.where(z == 0, DAMPING, 0.0).astype(F32)
         lower = jnp.where(z > 0, 1.0, 0.0).astype(F32)
         upper = jnp.where(z < 15, 1.0, 0.0).astype(F32)
-        if k < PLANES - 1:
-            load_above = lambda c, r: u_ref[c, z + 1, r, :]
-        else:
-            load_above = lambda c, r: u_ref[c, jnp.minimum(z + 1, 15), r, :] * upper
-        if k > 0:
-            load_below = lambda c, r: u_ref[c, z - 1, r, :]
-        else:
-            load_below = lambda c, r: u_ref[c, jnp.maximum(z - 1, 0), r, :] * lower
-        for i in range(8):
-            rows = strip_of(i)
-            centers, sums = stencil_strip(
-                i, lambda c, r: u_ref[c, z, r, :], None, load_above, load_below, halo_refs, z
-            )
-            force = strip_force(
-                centers, sums, region_ref[k, rows, :], plastic_ref[rows, :], table
-            )
-            for c in range(3):
-                v = v_ref[c, k, rows, :]
-                v = v + DT * (force[c] - damping * v)
-                u = centers[c] + DT * v
-                new_v_ref[c, k, rows, :] = v
-                new_u_ref[c, k, rows, :] = u
-
-
-def step_two_kernel(start, *refs):
-    (shear_ref, yields_ref, u_ref, v_ref, region_ref, plastic_ref) = refs[:6]
-    halo_refs = refs[6:10]
-    table = label_table(shear_ref, yields_ref)
-    new_u_ref, new_v_ref = refs[-2:]
-    for k in range(PLANES):
-        z = pl.program_id(0) * PLANES + (start + k)
-        upper = jnp.where(z < 15, 1.0, 0.0).astype(F32)
-        if k < PLANES - 1:
-            load_above = lambda c, r: u_ref[c, z + 1, r, :]
-        else:
-            load_above = lambda c, r: u_ref[c, jnp.minimum(z + 1, 15), r, :] * upper
+        here = z - begin
         for i in range(8):
             rows = strip_of(i)
             centers, sums = stencil_strip(
                 i,
-                lambda c, r: u_ref[c, z, r, :],
+                lambda c, r: us[c, here, r, :],
                 None,
-                load_above,
-                lambda c, r: u_ref[c, z - 1, r, :],
-                halo_refs,
+                lambda c, r: us[c, jnp.minimum(here + 1, end - begin), r, :] * upper,
+                lambda c, r: us[c, jnp.maximum(here - 1, 0), r, :] * lower,
+                halo_one,
                 z,
             )
-            force = strip_force(
-                centers, sums, region_ref[k, rows, :], plastic_ref[rows, :], table
+            force = strip_force(centers, sums, rs[here, rows, :], plastic_ref[rows, :], table)
+            for c in range(3):
+                v = vs[c, here, rows, :]
+                v = v + DT * (force[c] - damping * v)
+                new_vs[c, z - start, rows, :] = v
+                new_us[c, z - start, rows, :] = centers[c] + DT * v
+
+    heads = []
+    if head:
+        heads = [
+            pltpu.make_async_copy(new_us.at[:, 0:4], outs[2], head_sems.at[0]),
+            pltpu.make_async_copy(new_vs.at[:, 0:2], outs[3], head_sems.at[1]),
+        ]
+        for copy in heads:
+            copy.start()
+
+    @pl.loop(low, high)
+    def _(z):
+        upper = jnp.where(z < 15, 1.0, 0.0).astype(F32)
+        here = z - start
+        for i in range(8):
+            rows = strip_of(i)
+            centers, sums = stencil_strip(
+                i,
+                lambda c, r: new_us[c, here, r, :],
+                None,
+                lambda c, r: new_us[c, jnp.minimum(here + 1, stop - start), r, :] * upper,
+                lambda c, r: new_us[c, here - 1, r, :],
+                halo_two,
+                z,
             )
+            force = strip_force(centers, sums, rs[z - begin, rows, :], plastic_ref[rows, :], table)
             for c in range(3):
-                v = v_ref[c, k, rows, :] + DT * force[c]
-                new_v_ref[c, k, rows, :] = v
-                new_u_ref[c, k, rows, :] = centers[c] + DT * v
+                v = new_vs[c, here, rows, :] + DT * force[c]
+                out_vs[c, z - low, rows, :] = v
+                out_us[c, z - low, rows, :] = centers[c] + DT * v
+        for copy in put(z):
+            copy.start()
+
+    @pl.loop(low, high)
+    def _(z):
+        for copy in put(z):
+            copy.wait()
+
+    for copy in heads:
+        copy.wait()
 
 
 def last_kernel(
@@ -788,7 +824,7 @@
     return jax.ShapeDtypeStruct(shape, F32)
 
 
-def call(body, out_shape, args, smem=0, scratch=(), after=(), name=None, limit=16 << 20):
+def call(body, out_shape, args, smem=0, scratch=(), after=(), limit=16 << 20):
     outs = out_shape if isinstance(out_shape, (tuple, list)) else [out_shape]
     size = sum(math.prod(x.shape) * 4 for x in list(args) + list(outs))
     out_specs = [full(x.shape) for x in outs]
@@ -802,7 +838,6 @@
         scratch_shapes=scratch,
         cost_estimate=pl.CostEstimate(flops=0, bytes_accessed=size, transcendentals=0),
         compiler_params=pltpu.CompilerParams(vmem_limit_bytes=limit),
-        name=name,
     )(*args, *(in_hbm(x) for x in after))
 
 
@@ -822,7 +857,7 @@
     return lax.all_to_all(x, axis, split_axis=0, concat_axis=0, tiled=True)
 
 
-def body(u, v, region, flags, shear, yields, history, kernel):
+def program(u, v, region, flags, shear, yields, history, kernel):
     device = lax.axis_index(ALL)
     where = jnp.stack(
         [
@@ -833,7 +868,7 @@
         ]
     )
     edge_shapes = [shape_of(168, 256)] * 2 + [shape_of(2, 64, 128)] * 2
-    halo_shapes = [shape_of(48, 256)] * 2 + [shape_of(64, 128)] * 2
+    halo_shapes = [hbm_shape(48, 256)] * 2 + [hbm_shape(64, 128)] * 2
     near = lambda depth: pl.BlockSpec((3, depth, 64, 256), lambda *_: (0, 0, 0, 0))
     slab = lambda depth: pl.BlockSpec((depth, 64, 256), lambda *_: (0, 0, 0))
     planes = lambda depth, start=0: pl.BlockSpec(
@@ -908,38 +943,57 @@
 
     send = call(
         dip_kernel, shape_of(768, 128), (t["radix"], t["dip_turn"], t["dip_out"], lines),
-        after=[own], name="dip",
+        after=[own],
     )
     waves = exchange(send.reshape(128, 1, 768), ALL).reshape(768, 128)
 
-    new_u, new_v = pl.pallas_call(
-        step_one_kernel,
-        grid=(16 // PLANES,),
-        in_specs=[SMEM, SMEM, near(16), planes(PLANES), slabs(PLANES), full((64, 256))]
-        + halo_specs
-        + [any_spec],
-        out_specs=[planes(PLANES)] * 2,
-        out_shape=[hbm_shape(3, 16, 64, 256)] * 2,
-        cost_estimate=pl.CostEstimate(flops=0, bytes_accessed=14000000, transcendentals=0),
-        compiler_params=pltpu.CompilerParams(vmem_limit_bytes=24 << 20),
-            name="step_one",
-    )(shear, yields, u, v, region, plastic, *halo_one, in_hbm(send))
-    new_u, new_v = in_hbm(new_u), in_hbm(new_v)
     halo_two = call(
         beside_kernel,
         halo_shapes,
         (where, shear, yields, *(in_hbm(x) for x in (first, last, left, right, *halo_one, lines))),
         smem=3,
-        name="beside",
-    )
-
+    )
+
+    def both_steps(low, high, given, after):
+        head = low == 2
+        start = 0 if head else low - 1
+        stop = min(high, 15)
+        held = min(stop + 1, 15) - max(start - 1, 0) + 1
+        made = stop - start + 1
+        tile = lambda n: pltpu.VMEM((3, n, 64, 256), F32)
+        extra = [hbm_shape(3, 4, 64, 256), hbm_shape(3, 2, 64, 256)] if head else []
+        return pl.pallas_call(
+            functools.partial(both_steps_kernel, low, high),
+            in_specs=[SMEM, SMEM] + [any_spec] * 3 + [full(None)] * 9
+            + [any_spec] * (len(given) + 1),
+            out_specs=[any_spec] * (2 + len(extra)),
+            out_shape=[hbm_shape(3, 16, 64, 256)] * 2 + extra,
+            input_output_aliases={14: 0, 15: 1} if given else {},
+            scratch_shapes=[
+                tile(held), tile(held), pltpu.VMEM((held, 64, 256), jnp.int32),
+                tile(made), tile(made), tile(high - low), tile(high - low),
+                pltpu.SemaphoreType.DMA((held, 3)),
+                pltpu.SemaphoreType.DMA((high - low, 2)),
+                pltpu.SemaphoreType.DMA((2,)),
+            ],
+            cost_estimate=pl.CostEstimate(
+                flops=0, bytes_accessed=(high - low) * 1000000, transcendentals=0
+            ),
+            compiler_params=pltpu.CompilerParams(vmem_limit_bytes=24 << 20),
+            name="both_steps",
+        )(
+            shear, yields, u, v, region, plastic,
+            *(in_hbm(x) for x in halo_one), *(in_hbm(x) for x in halo_two),
+            *(in_hbm(x) for x in given), in_hbm(after),
+        )
+
+    out_u, out_v, new_u, new_v = both_steps(2, CUTS[0], [], send)
     coefficients = call(
         mirror_kernel,
         shape_of(8, 3, 8, 2048),
         (where, t["reverse"], *(in_hbm(x) for x in (own, main, edge))),
         smem=1,
         scratch=[pltpu.VMEM((144, 2048), F32)] * 2,
-        name="mirror",
     )
     send = call(
         strike_kernel,
@@ -949,40 +1003,19 @@
             t["strike_out"], coefficients, waves,
         ),
         scratch=[pltpu.VMEM((256, 384), F32)] * 3,
-        after=[new_u],
-        name="strike",
+        after=[out_u],
     )
     columns = exchange(send.reshape(128, 8, 128), ALL).reshape(1024, 128)
 
-    def later(start, stop, given, after):
-        return pl.pallas_call(
-            functools.partial(step_two_kernel, start),
-            grid=((stop - start) // PLANES,),
-            in_specs=[
-                SMEM, SMEM, near(16), planes(PLANES, start), slabs(PLANES, start), full((64, 256)),
-            ]
-            + halo_specs
-            + [any_spec] * (len(given) + 1),
-            out_specs=[planes(PLANES, start)] * 2,
-            out_shape=[hbm_shape(3, 16, 64, 256)] * 2,
-            input_output_aliases={10: 0, 11: 1} if given else {},
-            cost_estimate=pl.CostEstimate(
-                flops=0, bytes_accessed=(stop - start) * 800000, transcendentals=0
-            ),
-            compiler_params=pltpu.CompilerParams(vmem_limit_bytes=24 << 20),
-            name="step_two",
-        )(shear, yields, new_u, new_v, region, plastic, *halo_two, *given, in_hbm(after))
-
-    out = later(2, 10, [], send)
+    out = both_steps(CUTS[0], CUTS[1], [out_u, out_v], send)
     send = call(
         undip_kernel,
         shape_of(4, 224, 128),
         (t["dip_in"], t["undip_turn"], t["unradix"], columns),
         after=[out[0]],
-        name="undip",
     )
     tractions = exchange(send, "narrow")
-    out = later(10, 16, out, send)
+    out = both_steps(CUTS[1], 16, out, send)
     return tuple(
         pl.pallas_call(
             last_kernel,
@@ -1014,4 +1047,4 @@
         P(None, None, None, ALL, None),
         P(None, None, ALL, None),
     )
-    return jax.shard_map(body, mesh=mesh, in_specs=in_specs, out_specs=(tile, tile), check_vma=False)
+    return jax.shard_map(program, mesh=mesh, in_specs=in_specs, out_specs=(tile, tile), check_vma=False)

time: 112 us -> 112 us (level)
    ppermute x2, waiting for transfers between devices: 5.43 us -> 7.25 us  [the longest x1 7.25 us: program(): lax.ppermute(edge, ALL, [(64, 0)] + [(i, 128 - i) for i in range(65, 128)])]
    all_to_all x4, waiting for transfers between devices: 7.41 us -> 5.85 us  [exchange(): return lax.all_to_all(x, axis, split_axis=0, concat_axis=0, tiled=True)]
where the time goes in v6:
time: 112 us; the launch traced here: 111 us
  Pallas kernels  52.2 us (47%)
  starting transfers between devices  42.9 us (38%)
  waiting for transfers between devices  13.1 us (12%)
  local copies, waits for them, and re-layouts  1.6 us (1%)
    all_to_all x4, starting transfers between devices, exchange(): return lax.all_to_all(x, axis, split_axis=0, concat_axis=0, tiled=True)  20.4 us
    pallas_call x3, Pallas kernels, both_steps(): pl.pallas_call(functools.partial(both_steps_kernel, low, high), in_specs=...  19.8 us
    pallas_call x5, Pallas kernels, call(): pl.pallas_call(body, in_specs=[SMEM] * smem + [full(x.shape) for x in arg...  11.8 us
    pallas_call x2, Pallas kernels, sums(): pl.pallas_call(history_kernel, grid=(steps,), in_specs=[SMEM, pl.BlockSpe...  9.73 us
    ppermute x1, starting transfers between devices, program(): main = lax.ppermute(main, ALL, [(i, 127 - i) for i in range(128)])  9.65 us
    ppermute x1, waiting for transfers between devices, program(): lax.ppermute(edge, ALL, [(64, 0)] + [(i, 128 - i) for i in range(65, 128)])  7.25 us
    pallas_call x1, Pallas kernels, program(): pl.pallas_call(edges_kernel, grid=(4,), in_specs=[planes(4), planes(4), s...  6.41 us
    all_to_all x4, waiting for transfers between devices, exchange(): return lax.all_to_all(x, axis, split_axis=0, concat_axis=0, tiled=True)  5.85 us
  transfers between devices with their start and end apart: 10, of which 3 were waited for; matrix products, arithmetic and copies ran while one was open for 1% of the time, Pallas kernels for 33%

profile of v6, /device:TPU:1, one launch (start us, length us, event | category | flops | bytes accessed | tf_op | source)
XLA Modules:
  0.0 111.4 jit_solution(3469409584409811713)
XLA Ops:
  0.6 6.4 %edges.1 = (f32[168,256]{1,0:T(8,128)S(1)}, f32[168,256]{1,0:T(8,128)S(1)}, f32[2,64,128]{2,1,0:T(8,128)S(1)}, f32[2,64,128]{2,1,0:T(8,128)S(1)}, f32[64,256]{1,0:T(8,128)}) custom-call(f32[3,16,64,256]{3,2,1,0:T(8,128)} %refs_2_.5, f32[3,16,64,256]{3,2,1,0:T(8,128)} %refs_3_.5, s32[16,64,256]{2,1,0:T(8,128)} %region_ref.5, s32[8,32]{1,0:T(8,128)} %flags_ref.1), custom_call_target="tpu_custom_call" | custom-call | bytes 8000000 | tf_op jit(solution)/shard_map/edges/pallas_call | solution.py:886
  7.1 0.0 copy-start.22
  7.1 4.4 %collective-permute-start = (f32[168,256]{1,0:T(8,128)S(1)}, f32[168,256]{1,0:T(8,128)S(1)}, u32[]{:S(2)}, u32[]{:S(2)}) collective-permute-start(f32[168,256]{1,0:T(8,128)S(1)} %get-tuple-element.26.last_ref), channel_id=1, source_target_pairs={{0,4},{4,8},{8,12},{12,16},{16,20},{20,24},{24,28},{28,32},{32,36}... | collective-permute-start | bytes 516104 | tf_op jit(solution)/shard_map/ppermute | solution.py:847
  11.4 1.3 %collective-permute-start.1 = (f32[168,256]{1,0:T(8,128)S(1)}, f32[168,256]{1,0:T(8,128)S(1)}, u32[]{:S(2)}, u32[]{:S(2)}) collective-permute-start(f32[168,256]{1,0:T(8,128)S(1)} %get-tuple-element.27.first_ref), channel_id=1, source_target_pairs={{4,0},{8,4},{12,8},{16,12},{20,16},{24,20},{28,24},{32,28},{36,32}... | collective-permute-start | bytes 516104 | tf_op jit(solution)/shard_map/ppermute | solution.py:848
  12.7 4.0 %collective-permute-start.2 = (f32[2,64,128]{2,1,0:T(8,128)S(1)}, f32[2,64,128]{2,1,0:T(8,128)S(1)}, u32[]{:S(2)}, u32[]{:S(2)}) collective-permute-start(f32[2,64,128]{2,1,0:T(8,128)S(1)} %get-tuple-element.28.right_ref), channel_id=1, source_target_pairs={{0,1},{1,2},{2,3},{4,5},{5,6},{6,7},{8,9},{9,10},{10,11},{12,13},{... | collective-permute-start | bytes 196616 | tf_op jit(solution)/shard_map/ppermute | solution.py:851
  16.7 1.9 %collective-permute-start.3 = (f32[2,64,128]{2,1,0:T(8,128)S(1)}, f32[2,64,128]{2,1,0:T(8,128)S(1)}, u32[]{:S(2)}, u32[]{:S(2)}) collective-permute-start(f32[2,64,128]{2,1,0:T(8,128)S(1)} %get-tuple-element.29.left_ref), channel_id=1, source_target_pairs={{1,0},{2,1},{3,2},{5,4},{6,5},{7,6},{9,8},{10,9},{11,10},{13,12},{... | collective-permute-start | bytes 196616 | tf_op jit(solution)/shard_map/ppermute | solution.py:852
  18.6 0.6 pad_add_fusion.where_ref
  19.2 4.8 %history.2 = (f32[72,2048]{1,0:T(8,128)}, f32[72,2048]{1,0:T(8,128)}, f32[18,2048]{1,0:T(8,128)}) custom-call(s32[4]{0:T(128)} %pad_add_fusion.where_ref, bf16[33,3,8,2048]{3,2,1,0:T(8,128)(2,1)} %kernel_ref.3, bf16[32,2,3,8,2048]{4,3,2,1,0:T(8,128)(2,1)} %history_ref.3), custom_call_target="tpu_custom_call" | custom-call | bytes 5500000 | tf_op jit(solution)/shard_map/history/pallas_call | solution.py:905
  24.1 0.0 copy-done.17
  24.1 0.0 copy-done.18
  24.1 0.0 copy-done.21
  24.1 0.0 copy-done.22
  24.1 0.0 collective-permute-done.2.left_ref.west_ref.refs_8_
  24.1 0.0 copy-start.3
  24.1 0.0 collective-permute-done.3.right_ref.east_ref.refs_9_
  24.1 0.0 copy-start.4
  24.2 0.0 collective-permute-done.top_ref.refs_6_
  24.2 0.0 copy-start.1
  24.2 0.0 collective-permute-done.1.bottom_ref.refs_7_
  24.2 0.0 copy-start.2
  24.2 2.2 %slip.1 = f32[4,240,128]{2,1,0:T(8,128)} custom-call(f32[4]{0:T(128)} %shear_ref.5, f32[4]{0:T(128)} %yields_ref.5, f32[3,16,64,256]{3,2,1,0:T(8,128)} %refs_2_.5, f32[3,16,64,256]{3,2,1,0:T(8,128)} %refs_3_.5, s32[16,64,256]{2,1,0:T(8,128)} %region_ref.5, f32[64,256]{1,0:T(8,128)} %get-tuple-element.25.plastic_ref.refs_5_, ...), custom_call_target="tpu_custom_call" | custom-call | bytes 1500000 | tf_op jit(solution)/shard_map/slip/pallas_call | solution.py:927
  26.5 0.0 copy-done.2
  26.5 3.5 %all-to-all-start = ((f32[4,240,128]{2,1,0:T(8,128)}), f32[4,240,128]{2,1,0:T(8,128)S(1)}, u32[]{:S(2)}, u32[]{:S(2)}) async-start(f32[4,240,128]{2,1,0:T(8,128)} %slip.1), calls=%async_computation | async-start | bytes 983040 | tf_op jit(solution)/shard_map/all_to_all | solution.py:857
  29.9 0.0 copy-start.13
  30.0 0.0 copy-start.15
  30.0 0.0 copy-start.24
  30.0 4.9 %history.3 = (f32[72,2048]{1,0:T(8,128)}, f32[72,2048]{1,0:T(8,128)}, f32[18,2048]{1,0:T(8,128)}) custom-call(s32[4]{0:T(128)} %pad_add_fusion.where_ref, bf16[33,3,8,2048]{3,2,1,0:T(8,128)(2,1)} %kernel_ref.3, bf16[32,2,3,8,2048]{4,3,2,1,0:T(8,128)(2,1)} %history_ref.3, ...), custom_call_target="tpu_custom_call", output_to_operand_aliasing={{0}: (3, {}), {1}: (4, {}), {2}: (5, {})} | custom-call | bytes 5500000 | tf_op jit(solution)/shard_map/history/pallas_call | solution.py:905
  34.9 9.7 %collective-permute-start.4 = (f32[72,2048]{1,0:T(8,128)}, f32[72,2048]{1,0:T(8,128)S(1)}, u32[]{:S(2)}, u32[]{:S(2)}) collective-permute-start(f32[72,2048]{1,0:T(8,128)} %get-tuple-element.40), channel_id=1, source_target_pairs={{0,127},{1,126},{2,125},{3,124},{4,123},{5,122},{6,121},{7,120},{8... | collective-permute-start | bytes 1769480 | tf_op jit(solution)/shard_map/ppermute | solution.py:941
  44.5 0.0 all-to-all-done.lines_ref.recv_ref
  44.5 1.8 %shard_map.195.refs_14_ = f32[768,128]{1,0:T(8,128)} custom-call(bf16[2,512,256]{2,1,0:T(8,128)(2,1)S(1)} %copy-done.13, f32[2,2,8,128]{3,2,1,0:T(8,128)S(1)} %copy-done.24, bf16[2,2,136,256]{3,2,1,0:T(8,128)(2,1)S(1)} %copy-done.15, f32[4,240,128]{2,1,0:T(8,128)S(1)} %all-to-all-done.lines_ref.recv_ref, f32[72,2048]{1,0:T(8,128)} %get-tuple-element.37._after_ref.own_ref), custom_call_target="tpu_custom_call" | custom-call | bytes 2506752 | tf_op jit(solution)/shard_map/pallas_call | solution.py:831
  46.4 5.5 %all-to-all-start.1 = ((f32[128,1,768]{2,1,0:T(1,128)}), f32[128,1,768]{2,1,0:T(1,128)S(1)}, u32[]{:S(2)}, u32[]{:S(2)}) async-start(f32[128,1,768]{2,1,0:T(1,128)} %bitcast.4), calls=%async_computation.1 | async-start | bytes 786432 | tf_op jit(solution)/shard_map/all_to_all | solution.py:857
  51.9 1.3 %collective-permute-start.5 = (f32[18,2048]{1,0:T(8,128)}, f32[18,2048]{1,0:T(8,128)S(1)}, u32[]{:S(2)}, u32[]{:S(2)}) collective-permute-start(f32[18,2048]{1,0:T(8,128)} %get-tuple-element.41), channel_id=1, source_target_pairs={{64,0},{65,63},{66,62},{67,61},{68,60},{69,59},{70,58},{71,57},{72... | collective-permute-start | bytes 442376 | tf_op jit(solution)/shard_map/ppermute | solution.py:942
  53.3 2.6 %shard_map.194 = (f32[48,256]{1,0:T(8,128)}, f32[48,256]{1,0:T(8,128)}, f32[64,128]{1,0:T(8,128)}, f32[64,128]{1,0:T(8,128)}) custom-call(s32[4]{0:T(128)} %pad_add_fusion.where_ref, f32[4]{0:T(128)} %shear_ref.5, f32[4]{0:T(128)} %yields_ref.5, f32[168,256]{1,0:T(8,128)} %copy-done.17, f32[168,256]{1,0:T(8,128)} %copy-done.18, f32[2,64,128]{2,1,0:T(8,128)} %copy-done.21, ...), custom_call_target="tpu_custom_call" | custom-call | bytes 1605680 | tf_op jit(solution)/shard_map/pallas_call | solution.py:831
  55.8 5.2 %both_steps.3 = (f32[3,16,64,256]{3,2,1,0:T(8,128)}, f32[3,16,64,256]{3,2,1,0:T(8,128)}, f32[3,4,64,256]{3,2,1,0:T(8,128)}, f32[3,2,64,256]{3,2,1,0:T(8,128)}) custom-call(f32[4]{0:T(128)} %shear_ref.5, f32[4]{0:T(128)} %yields_ref.5, f32[3,16,64,256]{3,2,1,0:T(8,128)} %refs_2_.5, f32[3,16,64,256]{3,2,1,0:T(8,128)} %refs_3_.5, s32[16,64,256]{2,1,0:T(8,128)} %region_ref.5, ...), custom_call_target="tpu_custom_call" | custom-call | bytes 2000000 | tf_op jit(solution)/shard_map/both_steps/pallas_call | solution.py:965
  61.1 0.0 copy-start.5
  61.1 0.0 copy-start.16
  61.1 7.3 %collective-permute-done.5.edge_ref = f32[18,2048]{1,0:T(8,128)S(1)} collective-permute-done((f32[18,2048]{1,0:T(8,128)}, f32[18,2048]{1,0:T(8,128)S(1)}, u32[]{:S(2)}, u32[]{:S(2)}) %collective-permute-start.5) | collective-permute-done | bytes 147488 | tf_op jit(solution)/shard_map/ppermute | solution.py:942
  68.4 0.0 collective-permute-done.4.main_ref
  68.4 0.7 copy-done.26
  69.0 0.8 copy-done.25
  69.8 0.0 copy-done.19
  69.8 2.4 %shard_map.196.coef_ref = f32[8,3,8,2048]{3,2,1,0:T(8,128)S(1)} custom-call(s32[4]{0:T(128)} %pad_add_fusion.where_ref, bf16[128,128]{1,0:T(8,128)(2,1)S(1)} %copy-done.19, f32[72,2048]{1,0:T(8,128)} %get-tuple-element.37._after_ref.own_ref, f32[72,2048]{1,0:T(8,128)} %copy-done.25, f32[18,2048]{1,0:T(8,128)} %copy-done.26), custom_call_target="tpu_custom_call" | custom-call | bytes 2965520 | tf_op jit(solution)/shard_map/pallas_call | solution.py:831
  72.3 0.0 all-to-all-done.1
  72.3 0.0 copy-done.20
  72.3 0.0 copy-done.5
  72.3 0.0 copy-done.16
  72.3 2.9 %shard_map.197.refs_16_ = f32[1024,128]{1,0:T(8,128)} custom-call(bf16[2,256,256]{2,1,0:T(8,128)(2,1)S(1)} %copy-done.5, f32[2,128,128]{2,1,0:T(8,128)S(1)} %copy-done.20, bf16[2,256,256]{2,1,0:T(8,128)(2,1)S(1)} %copy-done.16, bf16[128,128]{1,0:T(8,128)(2,1)S(1)} %copy-done.19, bf16[2,256,256]{2,1,0:T(8,128)(2,1)S(1)} %copy-done.5, ...), custom_call_target="tpu_custom_call" | custom-call | bytes 4259840 | tf_op jit(solution)/shard_map/pallas_call | solution.py:831
  75.2 6.6 %all-to-all-start.2 = ((f32[128,8,128]{2,1,0:T(8,128)}), f32[128,8,128]{2,1,0:T(8,128)S(1)}, u32[]{:S(2)}, u32[]{:S(2)}) async-start(f32[128,8,128]{2,1,0:T(8,128)} %bitcast.6), calls=%async_computation.2 | async-start | bytes 1048576 | tf_op jit(solution)/shard_map/all_to_all | solution.py:857
  81.8 0.0 copy-start.11
  81.8 0.0 copy-start.12
  81.8 0.0 copy-start.23
  81.9 8.0 %both_steps.4 = (f32[3,16,64,256]{3,2,1,0:T(8,128)}, f32[3,16,64,256]{3,2,1,0:T(8,128)}) custom-call(f32[4]{0:T(128)} %shear_ref.5, f32[4]{0:T(128)} %yields_ref.5, f32[3,16,64,256]{3,2,1,0:T(8,128)} %refs_2_.5, f32[3,16,64,256]{3,2,1,0:T(8,128)} %refs_3_.5, s32[16,64,256]{2,1,0:T(8,128)} %region_ref.5, ...), custom_call_target="tpu_custom_call", output_to_operand_aliasing={{0}: (14, {}), {1}: (15, {})} | custom-call | bytes 7000000 | tf_op jit(solution)/shard_map/both_steps/pallas_call | solution.py:965
  89.9 5.3 %all-to-all-done.2 = f32[128,8,128]{2,1,0:T(8,128)S(1)} async-done(((f32[128,8,128]{2,1,0:T(8,128)}), f32[128,8,128]{2,1,0:T(8,128)S(1)}, u32[]{:S(2)}, u32[]{:S(2)}) %all-to-all-start.2) | async-done | bytes 524320 | tf_op jit(solution)/shard_map/all_to_all | solution.py:857
  95.1 0.0 copy-done.12
  95.1 2.1 %shard_map.198.refs_16_ = f32[4,224,128]{2,1,0:T(8,128)} custom-call(bf16[2,256,512]{2,1,0:T(8,128)(2,1)S(1)} %copy-done.11, f32[2,2,8,128]{3,2,1,0:T(8,128)S(1)} %copy-done.23, bf16[2,256,512]{2,1,0:T(8,128)(2,1)S(1)} %copy-done.12, f32[1024,128]{1,0:T(8,128)S(1)} %bitcast.8, f32[3,16,64,256]{3,2,1,0:T(8,128)} %get-tuple-element.44._after_ref.refs_14_), custom_call_target="tpu_custom_call" | custom-call | bytes 3096576 | tf_op jit(solution)/shard_map/pallas_call | solution.py:831
  97.2 4.7 %all-to-all-start.3 = ((f32[4,224,128]{2,1,0:T(8,128)}), f32[4,224,128]{2,1,0:T(8,128)S(1)}, u32[]{:S(2)}, u32[]{:S(2)}) async-start(f32[4,224,128]{2,1,0:T(8,128)} %shard_map.198.refs_16_), calls=%async_computation.3 | async-start | bytes 917504 | tf_op jit(solution)/shard_map/all_to_all | solution.py:857
  101.9 0.0 copy-start.10
  102.0 0.0 copy-start.14
  102.0 6.5 %both_steps.5 = (f32[3,16,64,256]{3,2,1,0:T(8,128)}, f32[3,16,64,256]{3,2,1,0:T(8,128)}) custom-call(f32[4]{0:T(128)} %shear_ref.5, f32[4]{0:T(128)} %yields_ref.5, f32[3,16,64,256]{3,2,1,0:T(8,128)} %refs_2_.5, f32[3,16,64,256]{3,2,1,0:T(8,128)} %refs_3_.5, s32[16,64,256]{2,1,0:T(8,128)} %region_ref.5, ...), custom_call_target="tpu_custom_call", output_to_operand_aliasing={{0}: (14, {}), {1}: (15, {})} | custom-call | bytes 5000000 | tf_op jit(solution)/shard_map/both_steps/pallas_call | solution.py:965
  108.5 0.6 all-to-all-done.3.recv_ref
  109.1 0.0 copy-done.9
  109.1 0.0 copy-done.10
  109.1 0.0 copy-done.14
  109.1 2.3 %last.1 = (f32[3,16,64,256]{3,2,1,0:T(8,128)}, f32[3,16,64,256]{3,2,1,0:T(8,128)}) custom-call(f32[4]{0:T(128)} %shear_ref.5, f32[4]{0:T(128)} %yields_ref.5, f32[3,4,64,256]{3,2,1,0:T(8,128)S(1)} %copy-done.8, f32[3,2,64,256]{3,2,1,0:T(8,128)S(1)} %copy-done.14, s32[16,64,256]{2,1,0:T(8,128)} %region_ref.5, ...), custom_call_target="tpu_custom_call", output_to_operand_aliasing={{0}: (11, {}), {1}: (12, {})} | custom-call | bytes 4000000 | tf_op jit(solution)/shard_map/last/pallas_call | solution.py:1020
  (24 shorter events, 0.0 us)
Async XLA Ops:
  7.0 17.0 %copy-start.17 = (f32[168,256]{1,0:T(8,128)}, f32[168,256]{1,0:T(8,128)S(1)}, u32[]{:S(2)}) copy-start(f32[168,256]{1,0:T(8,128)S(1)} %get-tuple-element.27.first_ref) | copy-start | bytes 516100
  7.0 17.0 %copy-start.18 = (f32[168,256]{1,0:T(8,128)}, f32[168,256]{1,0:T(8,128)S(1)}, u32[]{:S(2)}) copy-start(f32[168,256]{1,0:T(8,128)S(1)} %get-tuple-element.26.last_ref) | copy-start | bytes 516100
  7.0 17.1 %copy-start.21 = (f32[2,64,128]{2,1,0:T(8,128)}, f32[2,64,128]{2,1,0:T(8,128)S(1)}, u32[]{:S(2)}) copy-start(f32[2,64,128]{2,1,0:T(8,128)S(1)} %get-tuple-element.29.left_ref) | copy-start | bytes 196612
  7.1 17.1 %copy-start.22 = (f32[2,64,128]{2,1,0:T(8,128)}, f32[2,64,128]{2,1,0:T(8,128)S(1)}, u32[]{:S(2)}) copy-start(f32[2,64,128]{2,1,0:T(8,128)S(1)} %get-tuple-element.28.right_ref) | copy-start | bytes 196612
  7.1 17.1 %collective-permute-start = (f32[168,256]{1,0:T(8,128)S(1)}, f32[168,256]{1,0:T(8,128)S(1)}, u32[]{:S(2)}, u32[]{:S(2)}) collective-permute-start(f32[168,256]{1,0:T(8,128)S(1)} %get-tuple-element.26.last_ref), channel_id=1, source_target_pairs={{0,4},{4,8},{8,12},{12,16},{16,20},{20,24},{24,28},{28,32},{32,36}... | collective-permute-start | bytes 516104 | tf_op jit(solution)/shard_map/ppermute | solution.py:847
  11.4 12.7 %collective-permute-start.1 = (f32[168,256]{1,0:T(8,128)S(1)}, f32[168,256]{1,0:T(8,128)S(1)}, u32[]{:S(2)}, u32[]{:S(2)}) collective-permute-start(f32[168,256]{1,0:T(8,128)S(1)} %get-tuple-element.27.first_ref), channel_id=1, source_target_pairs={{4,0},{8,4},{12,8},{16,12},{20,16},{24,20},{28,24},{32,28},{36,32}... | collective-permute-start | bytes 516104 | tf_op jit(solution)/shard_map/ppermute | solution.py:848
  12.7 11.4 %collective-permute-start.2 = (f32[2,64,128]{2,1,0:T(8,128)S(1)}, f32[2,64,128]{2,1,0:T(8,128)S(1)}, u32[]{:S(2)}, u32[]{:S(2)}) collective-permute-start(f32[2,64,128]{2,1,0:T(8,128)S(1)} %get-tuple-element.28.right_ref), channel_id=1, source_target_pairs={{0,1},{1,2},{2,3},{4,5},{5,6},{6,7},{8,9},{9,10},{10,11},{12,13},{... | collective-permute-start | bytes 196616 | tf_op jit(solution)/shard_map/ppermute | solution.py:851
  16.7 7.4 %collective-permute-start.3 = (f32[2,64,128]{2,1,0:T(8,128)S(1)}, f32[2,64,128]{2,1,0:T(8,128)S(1)}, u32[]{:S(2)}, u32[]{:S(2)}) collective-permute-start(f32[2,64,128]{2,1,0:T(8,128)S(1)} %get-tuple-element.29.left_ref), channel_id=1, source_target_pairs={{1,0},{2,1},{3,2},{5,4},{6,5},{7,6},{9,8},{10,9},{11,10},{13,12},{... | collective-permute-start | bytes 196616 | tf_op jit(solution)/shard_map/ppermute | solution.py:852
  24.1 2.3 %copy-start.3 = (f32[2,64,128]{2,1,0:T(8,128)}, f32[2,64,128]{2,1,0:T(8,128)S(1)}, u32[]{:S(2)}) copy-start(f32[2,64,128]{2,1,0:T(8,128)S(1)} %collective-permute-done.2.left_ref.west_ref.refs_8_) | copy-start | bytes 196612
  24.1 2.3 %copy-start.4 = (f32[2,64,128]{2,1,0:T(8,128)}, f32[2,64,128]{2,1,0:T(8,128)S(1)}, u32[]{:S(2)}) copy-start(f32[2,64,128]{2,1,0:T(8,128)S(1)} %collective-permute-done.3.right_ref.east_ref.refs_9_) | copy-start | bytes 196612
  24.2 2.3 %copy-start.1 = (f32[168,256]{1,0:T(8,128)}, f32[168,256]{1,0:T(8,128)S(1)}, u32[]{:S(2)}) copy-start(f32[168,256]{1,0:T(8,128)S(1)} %collective-permute-done.top_ref.refs_6_) | copy-start | bytes 516100
  24.2 2.3 %copy-start.2 = (f32[168,256]{1,0:T(8,128)}, f32[168,256]{1,0:T(8,128)S(1)}, u32[]{:S(2)}) copy-start(f32[168,256]{1,0:T(8,128)S(1)} %collective-permute-done.1.bottom_ref.refs_7_) | copy-start | bytes 516100
  26.5 18.1 %all-to-all-start = ((f32[4,240,128]{2,1,0:T(8,128)}), f32[4,240,128]{2,1,0:T(8,128)S(1)}, u32[]{:S(2)}, u32[]{:S(2)}) async-start(f32[4,240,128]{2,1,0:T(8,128)} %slip.1), calls=%async_computation | async-start | bytes 983040 | tf_op jit(solution)/shard_map/all_to_all | solution.py:857
  29.9 14.6 %copy-start.13 = (bf16[2,512,256]{2,1,0:T(8,128)(2,1)S(1)}, bf16[2,512,256]{2,1,0:T(8,128)(2,1)}, u32[]{:S(2)}) copy-start(bf16[2,512,256]{2,1,0:T(8,128)(2,1)} %constant.35.clone.radix_ref) | copy-start | bytes 1572868
  30.0 14.6 %copy-start.15 = (bf16[2,2,136,256]{3,2,1,0:T(8,128)(2,1)S(1)}, bf16[2,2,136,256]{3,2,1,0:T(8,128)(2,1)}, u32[]{:S(2)}) copy-start(bf16[2,2,136,256]{3,2,1,0:T(8,128)(2,1)} %constant.37.clone.out_table_ref) | copy-start | bytes 835588
  30.0 14.6 %copy-start.24 = (f32[2,2,8,128]{3,2,1,0:T(8,128)S(1)}, f32[2,2,8,128]{3,2,1,0:T(8,128)}, u32[]{:S(2)}) copy-start(f32[2,2,8,128]{3,2,1,0:T(8,128)} %constant.36.clone.turn_ref) | copy-start | bytes 49156
  34.9 33.5 %collective-permute-start.4 = (f32[72,2048]{1,0:T(8,128)}, f32[72,2048]{1,0:T(8,128)S(1)}, u32[]{:S(2)}, u32[]{:S(2)}) collective-permute-start(f32[72,2048]{1,0:T(8,128)} %get-tuple-element.40), channel_id=1, source_target_pairs={{0,127},{1,126},{2,125},{3,124},{4,123},{5,122},{6,121},{7,120},{8... | collective-permute-start | bytes 1769480 | tf_op jit(solution)/shard_map/ppermute | solution.py:941
  44.5 8.7 %copy-start = (f32[4,240,128]{2,1,0:T(8,128)}, f32[4,240,128]{2,1,0:T(8,128)S(1)}, u32[]{:S(2)}) copy-start(f32[4,240,128]{2,1,0:T(8,128)S(1)} %all-to-all-done.lines_ref.recv_ref) | copy-start | bytes 1474564
  46.4 25.9 %all-to-all-start.1 = ((f32[128,1,768]{2,1,0:T(1,128)}), f32[128,1,768]{2,1,0:T(1,128)S(1)}, u32[]{:S(2)}, u32[]{:S(2)}) async-start(f32[128,1,768]{2,1,0:T(1,128)} %bitcast.4), calls=%async_computation.1 | async-start | bytes 786432 | tf_op jit(solution)/shard_map/all_to_all | solution.py:857
  51.9 16.4 %collective-permute-start.5 = (f32[18,2048]{1,0:T(8,128)}, f32[18,2048]{1,0:T(8,128)S(1)}, u32[]{:S(2)}, u32[]{:S(2)}) collective-permute-start(f32[18,2048]{1,0:T(8,128)} %get-tuple-element.41), channel_id=1, source_target_pairs={{64,0},{65,63},{66,62},{67,61},{68,60},{69,59},{70,58},{71,57},{72... | collective-permute-start | bytes 442376 | tf_op jit(solution)/shard_map/ppermute | solution.py:942
  55.8 14.0 %copy-start.19 = (bf16[128,128]{1,0:T(8,128)(2,1)S(1)}, bf16[128,128]{1,0:T(8,128)(2,1)}, u32[]{:S(2)}) copy-start(bf16[128,128]{1,0:T(8,128)(2,1)} %constant.38.clone.reverse_ref) | copy-start | bytes 98308
  55.8 16.4 %copy-start.20 = (f32[2,128,128]{2,1,0:T(8,128)S(1)}, f32[2,128,128]{2,1,0:T(8,128)}, u32[]{:S(2)}) copy-start(f32[2,128,128]{2,1,0:T(8,128)} %constant.40.clone.turn_ref) | copy-start | bytes 393220
  61.1 11.2 %copy-start.5 = (bf16[2,256,256]{2,1,0:T(8,128)(2,1)S(1)}, bf16[2,256,256]{2,1,0:T(8,128)(2,1)}, u32[]{:S(2)}) copy-start(bf16[2,256,256]{2,1,0:T(8,128)(2,1)} %constant.39.clone.in_ref.out_table_ref) | copy-start | bytes 786436
  61.1 11.2 %copy-start.16 = (bf16[2,256,256]{2,1,0:T(8,128)(2,1)S(1)}, bf16[2,256,256]{2,1,0:T(8,128)(2,1)}, u32[]{:S(2)}) copy-start(bf16[2,256,256]{2,1,0:T(8,128)(2,1)} %constant.41.clone.mix_ref) | copy-start | bytes 786436
  68.4 0.7 copy-start.26
  69.0 0.8 copy-start.25
  75.2 19.9 %all-to-all-start.2 = ((f32[128,8,128]{2,1,0:T(8,128)}), f32[128,8,128]{2,1,0:T(8,128)S(1)}, u32[]{:S(2)}, u32[]{:S(2)}) async-start(f32[128,8,128]{2,1,0:T(8,128)} %bitcast.6), calls=%async_computation.2 | async-start | bytes 1048576 | tf_op jit(solution)/shard_map/all_to_all | solution.py:857
  81.8 13.3 %copy-start.11 = (bf16[2,256,512]{2,1,0:T(8,128)(2,1)S(1)}, bf16[2,256,512]{2,1,0:T(8,128)(2,1)}, u32[]{:S(2)}) copy-start(bf16[2,256,512]{2,1,0:T(8,128)(2,1)} %constant.42.clone.in_ref) | copy-start | bytes 1572868
  81.8 13.3 %copy-start.12 = (bf16[2,256,512]{2,1,0:T(8,128)(2,1)S(1)}, bf16[2,256,512]{2,1,0:T(8,128)(2,1)}, u32[]{:S(2)}) copy-start(bf16[2,256,512]{2,1,0:T(8,128)(2,1)} %constant.44.clone.unradix_ref) | copy-start | bytes 1572868
  81.8 13.3 %copy-start.23 = (f32[2,2,8,128]{3,2,1,0:T(8,128)S(1)}, f32[2,2,8,128]{3,2,1,0:T(8,128)}, u32[]{:S(2)}) copy-start(f32[2,2,8,128]{3,2,1,0:T(8,128)} %constant.43.clone.turn_ref) | copy-start | bytes 49156
  97.2 11.9 %all-to-all-start.3 = ((f32[4,224,128]{2,1,0:T(8,128)}), f32[4,224,128]{2,1,0:T(8,128)S(1)}, u32[]{:S(2)}, u32[]{:S(2)}) async-start(f32[4,224,128]{2,1,0:T(8,128)} %shard_map.198.refs_16_), calls=%async_computation.3 | async-start | bytes 917504 | tf_op jit(solution)/shard_map/all_to_all | solution.py:857
  101.9 7.2 %copy-start.6 = (f32[48,256]{1,0:T(8,128)S(1)}, f32[48,256]{1,0:T(8,128)}, u32[]{:S(2)}) copy-start(f32[48,256]{1,0:T(8,128)} %get-tuple-element.31.refs_10_.top_ref) | copy-start | bytes 147460
  101.9 7.2 %copy-start.7 = (f32[48,256]{1,0:T(8,128)S(1)}, f32[48,256]{1,0:T(8,128)}, u32[]{:S(2)}) copy-start(f32[48,256]{1,0:T(8,128)} %get-tuple-element.32.refs_11_.bottom_ref) | copy-start | bytes 147460
  101.9 7.2 %copy-start.8 = (f32[3,4,64,256]{3,2,1,0:T(8,128)S(1)}, f32[3,4,64,256]{3,2,1,0:T(8,128)}, u32[]{:S(2)}) copy-start(f32[3,4,64,256]{3,2,1,0:T(8,128)} %get-tuple-element.38.u_ref) | copy-start | bytes 2359300
  101.9 7.2 %copy-start.9 = (f32[64,128]{1,0:T(8,128)S(1)}, f32[64,128]{1,0:T(8,128)}, u32[]{:S(2)}) copy-start(f32[64,128]{1,0:T(8,128)} %get-tuple-element.33.refs_12_.left_ref) | copy-start | bytes 98308
  101.9 7.2 %copy-start.10 = (f32[64,128]{1,0:T(8,128)S(1)}, f32[64,128]{1,0:T(8,128)}, u32[]{:S(2)}) copy-start(f32[64,128]{1,0:T(8,128)} %get-tuple-element.34.refs_13_.right_ref) | copy-start | bytes 98308
  102.0 7.2 %copy-start.14 = (f32[3,2,64,256]{3,2,1,0:T(8,128)S(1)}, f32[3,2,64,256]{3,2,1,0:T(8,128)}, u32[]{:S(2)}) copy-start(f32[3,2,64,256]{3,2,1,0:T(8,128)} %get-tuple-element.39.v_ref) | copy-start | bytes 1179652
